TPU v7x, 512 devices: a whole 4x8x8 slice. The times are simulated.
512 devices in a mesh: ctx: 64 (over z_lo, x, y), head: 8 (over z_hi, core).
Axes of the slice: x: 4, y: 8, z: 8 (z_hi: 4, z_lo: 2; z = z_hi * 2 + z_lo), core: 2. Of those that a mesh axis runs over, the one named last changes fastest.
Arguments:
- queries: bfloat16 [10240, 8192], P(('ctx', 'head')), may hold values from -18 to 18
- keys: bfloat16 [10240, 1024], P(('ctx', 'head')), may hold values from -4.5 to 4.5
- values: bfloat16 [10240, 1024], P(('ctx', 'head')), may hold values from -12 to 12
- block_order: int32 [128], replicated, may hold values from 0 to 127, each once
Outputs:
- attended: bfloat16 [10240, 8192], P(('ctx', 'head'))
Inputs may be any that keep to these rules, and one draw needn't show every extreme that they name: Storage block b holds sequence block block_order[b], its tokens in order; block_order is a permutation.
All inputs are finite; a program needn't handle non-finite values.
Results may differ from a plain program's by a relative error of at most 0.0049.
Values may be sent and summed in bfloat16 or wider, within the bound.
No kernel may reach another device: no remote copies, remote signals or barrier semaphores. Data moves between devices by JAX's collectives and lax.ppermute only.
A program may use at most 64 MiB of HBM per device.

v0:
```python
import math

import jax
import jax.numpy as jnp
import numpy as np
from jax import lax
from jax.sharding import PartitionSpec as P

QUERY_HEADS = 64
VALUE_KEY_HEADS = 8
HEAD_DIMENSION = 128


def token_positions(block_order, row_ids, block_rows):
    block_ids = row_ids // block_rows
    block_table = jnp.arange(block_order.shape[0], dtype=jnp.int32)
    chosen = jnp.sum(
        jnp.where(block_ids[:, None] == block_table[None, :], block_order[None, :], 0), axis=1
    )
    return chosen * block_rows + row_ids % block_rows


def attend(states, query_block, query_pos, key_rows, value_rows, key_pos, key_heads, score_scale):
    max_old, total_old, weighted_old = states
    query_count = query_block.shape[0]
    head_size = key_rows.shape[1] // key_heads
    heads_per_group = query_block.shape[1] // (key_heads * head_size)
    head_total = key_heads * heads_per_group
    query_split = query_block.reshape(query_count, key_heads, heads_per_group, head_size)
    key_split = key_rows.reshape(-1, key_heads, head_size)
    value_split = value_rows.reshape(-1, key_heads, head_size)
    scores = (
        jnp.einsum("qkgd,nkd->kgqn", query_split, key_split, preferred_element_type=jnp.float32)
        * score_scale
    )
    visible = key_pos[None, :] <= query_pos[:, None]
    scores = jnp.where(visible[None, None], scores, -jnp.inf)
    max_prev = max_old.reshape(key_heads, heads_per_group, query_count)
    max_new = jnp.maximum(max_prev, jnp.max(scores, axis=3))
    weights = jnp.exp(scores - max_new[..., None])
    rescale = jnp.exp(max_prev - max_new)
    total_new = total_old.reshape(key_heads, heads_per_group, query_count) * rescale + jnp.sum(
        weights, axis=3
    )
    mixed_values = jnp.einsum(
        "kgqn,nkd->qkgd",
        weights.astype(jnp.bfloat16),
        value_split,
        preferred_element_type=jnp.float32,
    )
    weighted_new = (
        weighted_old.reshape(query_count, key_heads, heads_per_group, head_size)
        * jnp.transpose(rescale, (2, 0, 1))[..., None]
        + mixed_values
    )
    return (
        max_new.reshape(head_total, query_count),
        total_new.reshape(head_total, query_count),
        weighted_new.reshape(query_count, head_total * head_size),
    )


def on_device(queries, keys, values, block_order):
    head_count = lax.axis_size("head")
    ctx_index = lax.axis_index("ctx")
    tokens_per_shard = queries.shape[0]
    query_heads = QUERY_HEADS // head_count
    heads_per_group = QUERY_HEADS // VALUE_KEY_HEADS
    local_kv = max(1, query_heads // heads_per_group)
    score_scale = HEAD_DIMENSION ** (-0.5)
    placement_index = np.array(
        [
            slot_number * query_heads // heads_per_group + offset
            for slot_number in range(head_count)
            for offset in range(local_kv)
        ],
        dtype=np.int32,
    )
    key_placements = keys.reshape(tokens_per_shard, VALUE_KEY_HEADS, HEAD_DIMENSION)[
        :, placement_index, :
    ].reshape(tokens_per_shard, head_count * local_kv * HEAD_DIMENSION)
    value_placements = values.reshape(tokens_per_shard, VALUE_KEY_HEADS, HEAD_DIMENSION)[
        :, placement_index, :
    ].reshape(tokens_per_shard, head_count * local_kv * HEAD_DIMENSION)
    tok_ctx = tokens_per_shard * head_count
    block_rows = tok_ctx // 2
    query_pos = token_positions(
        block_order, ctx_index * tok_ctx + jnp.arange(tok_ctx, dtype=jnp.int32), block_rows
    )

    def make_fold(query_all, key_heads, position_of):

        def tile(states, key_rows, value_rows, key_pos):
            updated = []
            for number in range(2):
                query_block = query_all[number * block_rows : (number + 1) * block_rows]
                block_pos = query_pos[number * block_rows : (number + 1) * block_rows]
                reach = jnp.min(key_pos) <= jnp.max(block_pos)
                updated.append(
                    lax.cond(
                        reach,
                        lambda carry_state: attend(
                            carry_state,
                            query_block,
                            block_pos,
                            key_rows,
                            value_rows,
                            key_pos,
                            key_heads,
                            score_scale,
                        ),
                        lambda carry_state: carry_state,
                        states[number],
                    )
                )
            return tuple(updated)

        def fold_step(states, key_piece, first_row):
            key_rows, value_rows = key_piece
            count = key_rows.shape[0]
            key_pos = position_of(jnp.arange(count, dtype=jnp.int32))
            piece_rows = tok_ctx * math.gcd(count // tok_ctx, 4)
            splits = count // piece_rows

            def scan_step(carry_states, parts):
                return (tile(carry_states, parts[0], parts[1], parts[2]), None)

            states, unused = lax.scan(
                scan_step,
                states,
                (
                    key_rows.reshape(splits, piece_rows, -1),
                    value_rows.reshape(splits, piece_rows, -1),
                    key_pos.reshape(splits, piece_rows),
                ),
            )
            return states

        return fold_step

    local_q, local_k, local_v = (
        lax.all_to_all(queries, "head", split_axis=1, concat_axis=0, tiled=True),
        lax.all_to_all(key_placements, "head", split_axis=1, concat_axis=0, tiled=True),
        lax.all_to_all(value_placements, "head", split_axis=1, concat_axis=0, tiled=True),
    )

    def full_positions(row_ids):
        return token_positions(block_order, row_ids, block_rows)

    fold_each = make_fold(local_q, local_kv, full_positions)
    one_state = (
        jnp.full((query_heads, block_rows), -1e30, jnp.float32),
        jnp.zeros((query_heads, block_rows), jnp.float32),
        jnp.zeros((block_rows, query_heads * HEAD_DIMENSION), jnp.float32),
    )
    states = fold_each(
        (one_state, one_state),
        (
            lax.all_gather(local_k, "ctx", axis=0, tiled=True),
            lax.all_gather(local_v, "ctx", axis=0, tiled=True),
        ),
        jnp.int32(0),
    )
    total_all = jnp.concatenate([states[0][1], states[1][1]], axis=1)
    weighted_all = jnp.concatenate([states[0][2], states[1][2]], axis=0)
    weighted_all = weighted_all.reshape(tok_ctx, query_heads, HEAD_DIMENSION)
    attended = (
        (weighted_all / total_all.T[:, :, None])
        .reshape(tok_ctx, query_heads * HEAD_DIMENSION)
        .astype(jnp.bfloat16)
    )
    return lax.all_to_all(attended, "head", split_axis=0, concat_axis=1, tiled=True)


def solution(mesh):
    placed = (P(("ctx", "head"), None), P(("ctx", "head"), None), P(("ctx", "head"), None), P())
    return jax.shard_map(
        on_device, mesh=mesh, in_specs=placed, out_specs=P(("ctx", "head"), None), check_vma=False
    )
```

profile of v0, /device:TPU:24, one launch (start us, length us, event | category | flops | bytes accessed | tf_op | source)
XLA Modules:
  0.0 789.5 jit_solution(8596616769344484240)
XLA Ops:
  8.0 18.4 %all_to_all.67 = bf16[20,8,128]{2,0,1:T(8,128)(2,1)S(1)} all-to-all(bf16[20,8,128]{2,0,1:T(8,128)(2,1)S(1)} %bitcast.142), channel_id=1, replica_groups=mesh['ctx'=64,'head'=8] {'head'}, dimensions={1} | all-to-all | bytes 81920 | tf_op jit(solution)/shard_map/all_to_all | solution.py:143
  28.4 10.5 %all_to_all.68 = bf16[20,8,128]{2,0,1:T(8,128)(2,1)S(1)} all-to-all(bf16[20,8,128]{2,0,1:T(8,128)(2,1)S(1)} %bitcast.141), channel_id=1, replica_groups=mesh['ctx'=64,'head'=8] {'head'}, dimensions={1} | all-to-all | bytes 81920 | tf_op jit(solution)/shard_map/all_to_all | solution.py:144
  39.6 1.2 copy.51
  41.8 3.5 all-to-all-start.2
  45.3 6.3 select_reduce_fusion
  52.7 7.9 %all-to-all-done.2 = bf16[20,8,1024]{2,0,1:T(8,128)(2,1)S(1)} async-done(((bf16[20,8,1024]{2,0,1:T(8,128)(2,1)}), bf16[20,8,1024]{2,0,1:T(8,128)(2,1)S(1)}, u32[]{:S(2)}, u32[]{:S(2)}) %all-to-all-start.2) | async-done | bytes 327712 | tf_op jit(solution)/shard_map/all_to_all | solution.py:142
  60.7 260.5 %all-gather.3.cloned.1.call-done = bf16[10240,128]{1,0:T(8,128)(2,1)} async-done(((bf16[160,128]{1,0:T(8,128)(2,1)}), bf16[10240,128]{1,0:T(8,128)(2,1)}) %all-gather.3.cloned.1.call-update) | async-done | bytes 2621456 | tf_op jit(solution)/shard_map/all_gather | solution.py:159
  321.2 302.3 %all-gather.5.cloned.1.call-done = bf16[10240,128]{1,0:T(8,128)(2,1)} async-done(((bf16[160,128]{1,0:T(8,128)(2,1)}), bf16[10240,128]{1,0:T(8,128)(2,1)}) %all-gather.5.cloned.1.call-update) | async-done | bytes 2621456 | tf_op jit(solution)/shard_map/all_gather | solution.py:160
  623.6 135.3 %while.21 = (s32[]{:T(128)}, f32[8,80]{1,0:T(8,128)S(1)}, f32[8,80]{1,0:T(8,128)S(1)}, f32[80,1024]{1,0:T(8,128)S(1)}, f32[8,80]{1,0:T(8,128)S(1)}, /*index=5*/f...) while((s32[]{:T(128)}, f32[8,80]{1,0:T(8,128)S(1)}, ...), condition=%wide.region_14.15_spmd, body=%wide.region_4.14_spmd.sunk | while | flops 425599360 | bytes 17010988 | solution.py:128
  626.8 1.0 dynamic-slice_bitcast_fusion.3
  627.8 2.1 conditional.4
  629.9 2.1 conditional.5
  636.3 2.1 conditional.4
  638.4 2.1 conditional.5
  643.7 1.0 dynamic-slice_bitcast_fusion.3
  644.8 2.1 conditional.4
  646.8 2.1 conditional.5
  652.2 1.0 dynamic-slice_bitcast_fusion.3
  653.2 2.1 conditional.4
  655.3 2.1 conditional.5
  660.6 1.0 dynamic-slice_bitcast_fusion.3
  661.7 2.1 conditional.4
  663.7 2.1 conditional.5
  670.1 2.1 conditional.4
  672.2 2.1 conditional.5
  678.6 2.1 conditional.4
  680.6 2.1 conditional.5
  687.0 2.1 conditional.4
  689.1 2.1 conditional.5
  694.5 1.0 dynamic-slice_bitcast_fusion.3
  695.5 2.1 conditional.4
  697.6 2.1 conditional.5
  702.9 1.0 dynamic-slice_bitcast_fusion.3
  703.9 2.1 conditional.4
  706.0 2.1 conditional.5
  712.4 2.1 conditional.4
  714.5 2.1 conditional.5
  720.8 2.1 conditional.4
  722.9 2.1 conditional.5
  729.3 2.1 conditional.4
  731.4 2.1 conditional.5
  737.8 2.1 conditional.4
  739.8 2.1 conditional.5
  746.2 2.1 conditional.4
  748.3 2.1 conditional.5
  754.7 2.1 conditional.4
  756.7 2.1 conditional.5
  759.7 21.7 %all_to_all.69 = bf16[8,20,1024]{2,1,0:T(8,128)(2,1)S(1)} all-to-all(bf16[8,20,1024]{2,1,0:T(8,128)(2,1)S(1)} %divide_convert_fusion), channel_id=1, replica_groups=mesh['ctx'=64,'head'=8] {'head'}, dimensions={0} | all-to-all | bytes 655360 | tf_op jit(solution)/shard_map/all_to_all | solution.py:172
  (423 shorter events, 93.1 us)
Async XLA Ops:
  6.5 314.7 %all-gather.3.cloned.1.call-start = ((), (), s32[]{:S(2)}) async-start(), calls=%async_computation.4 | async-start | bytes 2662400 | tf_op jit(solution)/shard_map/all_gather | solution.py:159
  27.0 596.6 %all-gather.5.cloned.1.call-start = ((), (), s32[]{:S(2)}) async-start(), calls=%async_computation.5 | async-start | bytes 2662400 | tf_op jit(solution)/shard_map/all_gather | solution.py:160
  28.4 16.9 %copy-start = (s32[128]{0:T(128)S(1)}, s32[128]{0:T(128)}, u32[]{:S(2)}) copy-start(s32[128]{0:T(128)} %param.16) | copy-start | bytes 1540
  41.8 18.8 %all-to-all-start.2 = ((bf16[20,8,1024]{2,0,1:T(8,128)(2,1)}), bf16[20,8,1024]{2,0,1:T(8,128)(2,1)S(1)}, u32[]{:S(2)}, u32[]{:S(2)}) async-start(bf16[20,8,1024]{2,0,1:T(8,128)(2,1)} %copy.40), calls=%async_computation.2 | async-start | bytes 786432 | tf_op jit(solution)/shard_map/all_to_all | solution.py:142
Sparse Core Ops, SparseCore 0:
  27.1 294.0 all-gather.2
  323.3 300.2 all-gather.4
where the time goes:
time: 791 us; the launch traced here: 789 us
  waiting for transfers between devices  571 us (72%)
  blocking collectives  50.6 us (6%)
  loops' own time  44.3 us (6%)
  other arithmetic  40.1 us (5%)
  matrix products  33.5 us (4%)
  local copies, waits for them, and re-layouts  33.1 us (4%)
  between operations  13.6 us (2%)
    all_gather x1, waiting for transfers between devices, on_device(): lax.all_gather(local_v, 'ctx', axis=0, tiled=True)  302 us
    all_gather x1, waiting for transfers between devices, on_device(): lax.all_gather(local_k, 'ctx', axis=0, tiled=True)  261 us
    another operation x1, loops' own time, fold_step(): lax.scan(scan_step, states, (key_rows.reshape(splits, piece_rows, -1), va...  41.5 us
    all_to_all x1, blocking collectives, on_device(): lax.all_to_all(attended, 'head', split_axis=0, concat_axis=1, tiled=True)  21.7 us
    reduce_sum x32, other arithmetic, attend(): jnp.sum(weights, axis=3)  18.5 us
    all_to_all x1, blocking collectives, on_device(): lax.all_to_all(key_placements, 'head', split_axis=1, concat_axis=0, tiled...  18.4 us
    dot_general x32, matrix products, attend(): jnp.einsum('qkgd,nkd->kgqn', query_split, key_split, preferred_element_ty...  17.7 us
    squeeze x16, local copies, waits for them, and re-layouts, fold_step(): lax.scan(scan_step, states, (key_rows.reshape(splits, piece_rows, -1), va...  16.4 us
  transfers between devices with their start and end apart: 3, of which 3 were waited for; matrix products, arithmetic and copies ran while one was open for 1% of the time, Pallas kernels for 0%

commit v1 on v0

v1 whole, which is shorter than its diff:
```python
import jax
import jax.numpy as jnp
from jax import lax
from jax.experimental import pallas as pl
from jax.experimental.pallas import tpu as pltpu
from jax.sharding import Mesh, PartitionSpec as P

HEAD_DIMENSION = 128
GROUP_HEADS = 8
PIECE = 20
BLOCK_TOKENS = 80
NX, NY, NZL, NZH = 4, 8, 2, 4
NZ = NZL * NZH
AXES = ("zl", "x", "y", "zh", "core")
LOG2E = 1.4426950408889634
SCALE = HEAD_DIMENSION ** (-0.5) * LOG2E
HIDDEN = -1e30
KEYS = 2 * NY * NZ * PIECE
HALF = KEYS // 2
TOKENS = NZ * PIECE
WIDTH = GROUP_HEADS * HEAD_DIMENSION
ROWS = GROUP_HEADS * BLOCK_TOKENS
TILE = 320


def offsets(index):
    inner = index % 40
    return (inner // 20) * 40 + inner % 20


def attend_kernel(shift, meta, q_ref, own_ref, other_ref, out_ref, qa, ka, va):
    group = pl.program_id(0)
    x_index = meta[0]
    y_index = meta[1]
    core = meta[2]
    query_x = lax.rem(x_index + (NX - shift), NX)

    def block_of(zl, x, y, half):
        return meta[8 + ((zl * NX + x) * NY + y) * 2 + half]

    @pl.when(group == 0)
    def _():
        ka[0:HALF, 0:128] = own_ref[:, 0:128]
        ka[HALF:KEYS, 0:128] = other_ref[:, 0:128]
        va[0:HALF, 0:128] = own_ref[:, 128:256]
        va[HALF:KEYS, 0:128] = other_ref[:, 128:256]
        va[:, 128:256] = jnp.ones((KEYS, 128), jnp.bfloat16)
        token = lax.broadcasted_iota(jnp.int32, (BLOCK_TOKENS, 128), 0)
        lane = lax.broadcasted_iota(jnp.int32, (BLOCK_TOKENS, 128), 1)
        pick = jnp.where(token == lane, 1.0, 0.0).astype(jnp.bfloat16)
        for head in range(GROUP_HEADS):
            qa[head * BLOCK_TOKENS : (head + 1) * BLOCK_TOKENS, 128:256] = pick

    lane = lax.broadcasted_iota(jnp.int32, (BLOCK_TOKENS, 128), 1)
    row = lax.broadcasted_iota(jnp.int32, (BLOCK_TOKENS, 128), 0)
    query_pos = (
        jnp.where(
            lane < 40,
            block_of(group, query_x, y_index, 0),
            block_of(group, query_x, y_index, 1),
        )
        * BLOCK_TOKENS
        + offsets(lane)
        + core * PIECE
    )
    row_offset = offsets(row)
    for side in range(2):
        key_core = core if side == 0 else 1 - core
        gap = query_pos - (row_offset + key_core * PIECE)
        for y in range(NY):
            for zl in range(NZL):
                base = (
                    jnp.where(row < 40, block_of(zl, x_index, y, 0), block_of(zl, x_index, y, 1))
                    * BLOCK_TOKENS
                )
                start = side * HALF + (y * NZL + zl) * BLOCK_TOKENS
                ka[start : start + BLOCK_TOKENS, 128:256] = jnp.where(
                    base > gap, HIDDEN, 0.0
                ).astype(jnp.bfloat16)
    for head in range(GROUP_HEADS):
        qa[head * BLOCK_TOKENS : (head + 1) * BLOCK_TOKENS, 0:128] = q_ref[
            :, head * 128 : (head + 1) * 128
        ]

    stats = jnp.zeros((BLOCK_TOKENS, 128), jnp.float32)
    for tile in range(ROWS // TILE):
        scores = lax.dot_general(
            qa[tile * TILE : (tile + 1) * TILE, :],
            ka[...],
            (((1,), (1,)), ((), ())),
            preferred_element_type=jnp.float32,
        )
        top = jnp.max(scores, axis=1, keepdims=True) * SCALE
        weights = jnp.exp2(scores * SCALE - top).astype(jnp.bfloat16)
        mixed = jnp.dot(weights, va[...], preferred_element_type=jnp.float32)
        total = mixed[:, 128:256]
        result = mixed[:, 0:128] / total
        spread = top + jnp.log2(total)
        for part in range(TILE // BLOCK_TOKENS):
            head = tile * (TILE // BLOCK_TOKENS) + part
            rows = slice(part * BLOCK_TOKENS, (part + 1) * BLOCK_TOKENS)
            out_ref[:, head * 128 : (head + 1) * 128] = result[rows].astype(jnp.bfloat16)
            level = spread[rows]
            high = level.astype(jnp.bfloat16).astype(jnp.float32)
            rest = level - high
            middle = rest.astype(jnp.bfloat16).astype(jnp.float32)
            low = rest - middle
            stats = jnp.where(lane == head, high, stats)
            stats = jnp.where(lane == 8 + head, middle, stats)
            stats = jnp.where(lane == 16 + head, low, stats)
    out_ref[:, WIDTH : WIDTH + 128] = stats.astype(jnp.bfloat16)


def attend(shift, meta, q, own, other):
    def kernel(*refs):
        attend_kernel(shift, *refs)

    return pl.pallas_call(
        kernel,
        out_shape=jax.ShapeDtypeStruct((TOKENS, WIDTH + 128), jnp.bfloat16),
        grid_spec=pltpu.PrefetchScalarGridSpec(
            num_scalar_prefetch=1,
            grid=(TOKENS // BLOCK_TOKENS,),
            in_specs=[
                pl.BlockSpec((BLOCK_TOKENS, WIDTH), lambda g, m: (g, 0)),
                pl.BlockSpec((HALF, 256), lambda g, m: (0, 0)),
                pl.BlockSpec((HALF, 256), lambda g, m: (0, 0)),
            ],
            out_specs=pl.BlockSpec((BLOCK_TOKENS, WIDTH + 128), lambda g, m: (g, 0)),
            scratch_shapes=[
                pltpu.VMEM((ROWS, 256), jnp.bfloat16),
                pltpu.VMEM((KEYS, 256), jnp.bfloat16),
                pltpu.VMEM((KEYS, 256), jnp.bfloat16),
            ],
        ),
        compiler_params=pltpu.CompilerParams(
            dimension_semantics=("arbitrary",), vmem_limit_bytes=48 * 1024 * 1024
        ),
        name=f"attend{shift}",
    )(meta, q, own, other)


def merge_kernel(*refs):
    parts, out_ref = refs[:NX], refs[NX]
    stats = [part[:, WIDTH : WIDTH + 128].astype(jnp.float32) for part in parts]
    for head in range(GROUP_HEADS):
        levels = [
            (s[:, head : head + 1] + s[:, 8 + head : 9 + head]) + s[:, 16 + head : 17 + head]
            for s in stats
        ]
        top = levels[0]
        for level in levels[1:]:
            top = jnp.maximum(top, level)
        shares = [jnp.exp2(level - top) for level in levels]
        total = shares[0]
        for share in shares[1:]:
            total = total + share
        columns = slice(head * 128, (head + 1) * 128)
        mixed = sum(
            part[:, columns].astype(jnp.float32) * share for part, share in zip(parts, shares)
        )
        out_ref[:, columns] = (mixed / total).astype(jnp.bfloat16)


def merge(parts):
    return pl.pallas_call(
        merge_kernel,
        out_shape=jax.ShapeDtypeStruct((TOKENS, WIDTH), jnp.bfloat16),
        name="merge",
    )(*parts)


def ring(shift, size):
    return [(i, (i + shift) % size) for i in range(size)]


def on_device(queries, keys, values, block_order):
    z_axes = ("zl", "zh")
    meta = jnp.concatenate(
        [
            jnp.stack([lax.axis_index("x"), lax.axis_index("y"), lax.axis_index("core")]),
            jnp.zeros((5,), jnp.int32),
            block_order,
        ]
    )
    packed = jnp.concatenate(
        [
            queries.reshape(PIECE, NZ, WIDTH),
            keys.reshape(PIECE, NZ, HEAD_DIMENSION),
            values.reshape(PIECE, NZ, HEAD_DIMENSION),
        ],
        axis=2,
    ).transpose(1, 0, 2)
    packed = lax.all_to_all(packed, z_axes, split_axis=0, concat_axis=0, tiled=True)
    packed = packed.reshape(TOKENS, WIDTH + 256)
    q_own = packed[:, :WIDTH]
    kv = packed[:, WIDTH:]
    q_from = {0: q_own}
    for shift in (2, 1, 3):
        q_from[shift] = lax.ppermute(q_own, "x", ring(shift, NX))
    own = lax.all_to_all(
        jnp.broadcast_to(kv[None], (NY, TOKENS, 256)), "y", split_axis=0, concat_axis=0, tiled=True
    ).reshape(HALF, 256)
    other = lax.ppermute(own, "core", ring(1, 2))
    parts = []
    for shift in (2, 1, 3):
        part = attend(shift, meta, q_from[shift], own, other)
        parts.append(lax.ppermute(part, "x", ring(-shift, NX)))
    parts.append(attend(0, meta, q_own, own, other))
    attended = merge(parts).reshape(NZ, PIECE, WIDTH)
    attended = lax.all_to_all(attended, z_axes, split_axis=0, concat_axis=0, tiled=True)
    return attended.transpose(1, 0, 2).reshape(PIECE, NZ * WIDTH)


def solution(mesh):
    fine = Mesh(mesh.devices.reshape(NZL, NX, NY, NZH, 2), AXES)
    rows = P(AXES, None)
    return jax.shard_map(
        on_device, mesh=fine, in_specs=(rows, rows, rows, P()), out_specs=rows, check_vma=False
    )
```

time: 791 us -> 134 us (0.17)
  the two profiles are of different devices: /device:TPU:24 before, /device:TPU:6 now
where the time goes in v1:
time: 134 us; the launch traced here: 133 us
  blocking collectives  67.8 us (51%)
  Pallas kernels  32.7 us (24%)
  starting transfers between devices  21.7 us (16%)
  local copies, waits for them, and re-layouts  6.81 us (5%)
  waiting for transfers between devices  4 us (3%)
    pallas_call x4, Pallas kernels, attend(): pl.pallas_call(kernel, out_shape=jax.ShapeDtypeStruct((TOKENS, WIDTH + 12...  29.6 us
    all_to_all x1, blocking collectives, on_device(): lax.all_to_all(packed, z_axes, split_axis=0, concat_axis=0, tiled=True)  24.9 us
    all_to_all x1, blocking collectives, on_device(): lax.all_to_all(jnp.broadcast_to(kv[None], (NY, TOKENS, 256)), 'y', split_...  24.3 us
    all_to_all x1, blocking collectives, on_device(): lax.all_to_all(attended, z_axes, split_axis=0, concat_axis=0, tiled=True)  18.5 us
    ppermute x3, starting transfers between devices, on_device(): parts.append(lax.ppermute(part, 'x', ring(-shift, NX)))  10.6 us
    ppermute x3, starting transfers between devices, on_device(): q_from[shift] = lax.ppermute(q_own, 'x', ring(shift, NX))  9.24 us
    unnamed x15, local copies, waits for them, and re-layouts  5.1 us
    ppermute x3, waiting for transfers between devices, on_device(): q_from[shift] = lax.ppermute(q_own, 'x', ring(shift, NX))  3.98 us
  transfers between devices with their start and end apart: 7, of which 1 were waited for; matrix products, arithmetic and copies ran while one was open for 0% of the time, Pallas kernels for 22%

profile of v1, /device:TPU:6, one launch (start us, length us, event | category | flops | bytes accessed | tf_op | source)
XLA Modules:
  0.0 133.4 jit_solution(12503203595283347037)
XLA Ops:
  0.0 0.0 copy-start.1
  0.0 0.9 copy.17
  0.9 0.8 copy.18
  1.7 0.0 copy-done.1
  1.7 0.2 copy.16
  2.0 0.2 copy.12
  2.2 24.9 %all_to_all.15 = bf16[8,20,1280]{2,1,0:T(8,128)(2,1)S(1)} all-to-all(bf16[8,20,1280]{2,1,0:T(8,128)(2,1)S(1)} %maximum_bitcast_fusion), channel_id=1, replica_groups=mesh['zl'=2,'x'=4,'y'=8,'zh'=4,'core'=2] {'zl','zh'}, dimensions={0} | all-to-all | bytes 819200 | tf_op jit(solution)/shard_map/all_to_all | solution.py:194
  27.2 0.1 reshape.25
  27.3 24.3 %all_to_all.16 = bf16[8,160,256]{2,1,0:T(8,128)(2,1)S(1)} all-to-all(bf16[8,160,256]{2,1,0:T(8,128)(2,1)S(1)} %broadcast_in_dim.2), channel_id=1, replica_groups=mesh['zl'=2,'x'=4,'y'=8,'zh'=4,'core'=2] {'y'}, dimensions={0} | all-to-all | bytes 1310720 | tf_op jit(solution)/shard_map/all_to_all | solution.py:201
  51.7 1.9 %collective-permute-start.1 = (bf16[1280,256]{1,0:T(8,128)(2,1)S(1)}, bf16[1280,256]{1,0:T(8,128)(2,1)S(1)}, u32[]{:S(2)}, u32[]{:S(2)}) collective-permute-start(bf16[1280,256]{1,0:T(8,128)(2,1)S(1)} %bitcast.19), channel_id=1, source_target_pairs={{0,1},{1,0},{2,3},{3,2},{4,5},{5,4},{6,7},{7,6},{8,9},{9,8},{10,11... | collective-permute-start | bytes 1966088 | tf_op jit(solution)/shard_map/ppermute | solution.py:204
  53.6 3.3 %collective-permute-start = (bf16[160,1024]{1,0:T(8,128)(2,1)S(1)}, bf16[160,1024]{1,0:T(8,128)(2,1)S(1)}, u32[]{:S(2)}, u32[]{:S(2)}) collective-permute-start(bf16[160,1024]{1,0:T(8,128)(2,1)S(1)} %slice.8.refs_1_), channel_id=1, source_target_pairs={{0,128},{64,192},{128,0},{192,64},{1,129},{65,193},{129,1},{193,65... | collective-permute-start | bytes 983048 | tf_op jit(solution)/shard_map/ppermute | solution.py:200
  56.9 4.0 %collective-permute-start.3 = (bf16[160,1024]{1,0:T(8,128)(2,1)S(1)}, bf16[160,1024]{1,0:T(8,128)(2,1)S(1)}, u32[]{:S(2)}, u32[]{:S(2)}) collective-permute-start(bf16[160,1024]{1,0:T(8,128)(2,1)S(1)} %slice.8.refs_1_), channel_id=1, source_target_pairs={{0,64},{64,128},{128,192},{192,0},{1,65},{65,129},{129,193},{193,1... | collective-permute-start | bytes 983048 | tf_op jit(solution)/shard_map/ppermute | solution.py:200
  61.0 1.9 %collective-permute-start.5 = (bf16[160,1024]{1,0:T(8,128)(2,1)S(1)}, bf16[160,1024]{1,0:T(8,128)(2,1)S(1)}, u32[]{:S(2)}, u32[]{:S(2)}) collective-permute-start(bf16[160,1024]{1,0:T(8,128)(2,1)S(1)} %slice.8.refs_1_), channel_id=1, source_target_pairs={{0,192},{64,0},{128,64},{192,128},{1,193},{65,1},{129,65},{193,129... | collective-permute-start | bytes 983048 | tf_op jit(solution)/shard_map/ppermute | solution.py:200
  62.9 0.0 copy-start.4
  62.9 0.6 copy-done.4
  63.5 0.1 concatenate.6.refs_0_
  63.6 4.0 %collective-permute-done.refs_1_ = bf16[160,1024]{1,0:T(8,128)(2,1)S(1)} collective-permute-done((bf16[160,1024]{1,0:T(8,128)(2,1)S(1)}, bf16[160,1024]{1,0:T(8,128)(2,1)S(1)}, u32[]{:S(2)}, u32[]{:S(2)}) %collective-permute-start) | collective-permute-done | bytes 327712 | tf_op jit(solution)/shard_map/ppermute | solution.py:200
  67.6 0.0 collective-permute-done.1.refs_3_
  67.6 7.4 %attend2.1 = bf16[160,1152]{1,0:T(8,128)(2,1)S(1)} custom-call(s32[136]{0:T(256)S(1)} %concatenate.6.refs_0_, bf16[160,1024]{1,0:T(8,128)(2,1)S(1)} %collective-permute-done.refs_1_, bf16[1280,256]{1,0:T(8,128)(2,1)S(1)} %bitcast.20, bf16[1280,256]{1,0:T(8,128)(2,1)S(1)} %collective-permute-done.1.refs_3_), custom_call_target="tpu_custom_call" | custom-call | tf_op jit(solution)/shard_map/attend2/pallas_call | solution.py:118
  75.0 3.4 %collective-permute-start.2 = (bf16[160,1152]{1,0:T(8,128)(2,1)S(1)}, bf16[160,1152]{1,0:T(8,128)(2,1)S(1)}, u32[]{:S(2)}, u32[]{:S(2)}) collective-permute-start(bf16[160,1152]{1,0:T(8,128)(2,1)S(1)} %attend2.1), channel_id=1, source_target_pairs={{0,128},{64,192},{128,0},{192,64},{1,129},{65,193},{129,1},{193,65... | collective-permute-start | bytes 1105928 | tf_op jit(solution)/shard_map/ppermute | solution.py:208
  78.4 0.0 collective-permute-done.3.refs_1_
  78.4 7.4 %attend1.1 = bf16[160,1152]{1,0:T(8,128)(2,1)S(1)} custom-call(s32[136]{0:T(256)S(1)} %concatenate.6.refs_0_, bf16[160,1024]{1,0:T(8,128)(2,1)S(1)} %collective-permute-done.3.refs_1_, bf16[1280,256]{1,0:T(8,128)(2,1)S(1)} %bitcast.21, bf16[1280,256]{1,0:T(8,128)(2,1)S(1)} %collective-permute-done.1.refs_3_), custom_call_target="tpu_custom_call" | custom-call | tf_op jit(solution)/shard_map/attend1/pallas_call | solution.py:118
  85.8 2.1 %collective-permute-start.4 = (bf16[160,1152]{1,0:T(8,128)(2,1)S(1)}, bf16[160,1152]{1,0:T(8,128)(2,1)S(1)}, u32[]{:S(2)}, u32[]{:S(2)}) collective-permute-start(bf16[160,1152]{1,0:T(8,128)(2,1)S(1)} %attend1.1), channel_id=1, source_target_pairs={{0,192},{64,0},{128,64},{192,128},{1,193},{65,1},{129,65},{193,129... | collective-permute-start | bytes 1105928 | tf_op jit(solution)/shard_map/ppermute | solution.py:208
  87.9 0.0 collective-permute-done.5.refs_1_
  87.9 7.4 %attend3.1 = bf16[160,1152]{1,0:T(8,128)(2,1)S(1)} custom-call(s32[136]{0:T(256)S(1)} %concatenate.6.refs_0_, bf16[160,1024]{1,0:T(8,128)(2,1)S(1)} %collective-permute-done.5.refs_1_, bf16[1280,256]{1,0:T(8,128)(2,1)S(1)} %bitcast.22, bf16[1280,256]{1,0:T(8,128)(2,1)S(1)} %collective-permute-done.1.refs_3_), custom_call_target="tpu_custom_call" | custom-call | tf_op jit(solution)/shard_map/attend3/pallas_call | solution.py:118
  95.3 5.1 %collective-permute-start.6 = (bf16[160,1152]{1,0:T(8,128)(2,1)S(1)}, bf16[160,1152]{1,0:T(8,128)(2,1)}, u32[]{:S(2)}, u32[]{:S(2)}) collective-permute-start(bf16[160,1152]{1,0:T(8,128)(2,1)S(1)} %attend3.1), channel_id=1, source_target_pairs={{0,64},{64,128},{128,192},{192,0},{1,65},{65,129},{129,193},{193,1... | collective-permute-start | bytes 1105928 | tf_op jit(solution)/shard_map/ppermute | solution.py:208
  100.4 7.4 %attend0.1.refs_3_ = bf16[160,1152]{1,0:T(8,128)(2,1)S(1)} custom-call(s32[136]{0:T(256)S(1)} %concatenate.6.refs_0_, bf16[160,1024]{1,0:T(8,128)(2,1)S(1)} %slice.8.refs_1_, bf16[1280,256]{1,0:T(8,128)(2,1)S(1)} %bitcast.23, bf16[1280,256]{1,0:T(8,128)(2,1)S(1)} %collective-permute-done.1.refs_3_), custom_call_target="tpu_custom_call" | custom-call | tf_op jit(solution)/shard_map/attend0/pallas_call | solution.py:118
  107.8 0.0 copy-start
  107.8 0.7 copy-done
  108.6 0.0 collective-permute-done.2.refs_0_
  108.6 0.0 copy-start.2
  108.6 0.0 collective-permute-done.4.refs_1_
  108.6 0.0 copy-start.3
  108.6 0.0 collective-permute-done.6.refs_2_
  108.6 0.7 copy-done.2
  109.3 0.1 copy-done.3
  109.4 3.2 %merge.1 = bf16[160,1024]{1,0:T(8,128)(2,1)} custom-call(bf16[160,1152]{1,0:T(8,128)(2,1)} %copy-done.2, bf16[160,1152]{1,0:T(8,128)(2,1)} %copy-done.3, bf16[160,1152]{1,0:T(8,128)(2,1)} %collective-permute-done.6.refs_2_, bf16[160,1152]{1,0:T(8,128)(2,1)} %copy-done), custom_call_target="tpu_custom_call" | custom-call | tf_op jit(solution)/shard_map/merge/pallas_call | solution.py:166
  112.6 1.0 reshape.27
  113.7 18.5 %all_to_all.17 = bf16[8,20,1024]{2,1,0:T(8,128)(2,1)S(1)} all-to-all(bf16[8,20,1024]{2,1,0:T(8,128)(2,1)S(1)} %reshape.27), channel_id=1, replica_groups=mesh['zl'=2,'x'=4,'y'=8,'zh'=4,'core'=2] {'zl','zh'}, dimensions={0} | all-to-all | bytes 655360 | tf_op jit(solution)/shard_map/all_to_all | solution.py:211
  132.2 0.2 copy.15
  132.4 1.0 copy.19
  (11 shorter events, 0.2 us)
Async XLA Ops:
  0.0 1.7 %copy-start.1 = (bf16[20,8192]{1,0:T(8,128)(2,1)S(1)}, bf16[20,8192]{1,0:T(8,128)(2,1)}, u32[]{:S(2)}) copy-start(bf16[20,8192]{1,0:T(8,128)(2,1)} %param.4) | copy-start | bytes 983044
  51.7 15.9 %collective-permute-start.1 = (bf16[1280,256]{1,0:T(8,128)(2,1)S(1)}, bf16[1280,256]{1,0:T(8,128)(2,1)S(1)}, u32[]{:S(2)}, u32[]{:S(2)}) collective-permute-start(bf16[1280,256]{1,0:T(8,128)(2,1)S(1)} %bitcast.19), channel_id=1, source_target_pairs={{0,1},{1,0},{2,3},{3,2},{4,5},{5,4},{6,7},{7,6},{8,9},{9,8},{10,11... | collective-permute-start | bytes 1966088 | tf_op jit(solution)/shard_map/ppermute | solution.py:204
  53.6 14.0 %collective-permute-start = (bf16[160,1024]{1,0:T(8,128)(2,1)S(1)}, bf16[160,1024]{1,0:T(8,128)(2,1)S(1)}, u32[]{:S(2)}, u32[]{:S(2)}) collective-permute-start(bf16[160,1024]{1,0:T(8,128)(2,1)S(1)} %slice.8.refs_1_), channel_id=1, source_target_pairs={{0,128},{64,192},{128,0},{192,64},{1,129},{65,193},{129,1},{193,65... | collective-permute-start | bytes 983048 | tf_op jit(solution)/shard_map/ppermute | solution.py:200
  56.9 21.4 %collective-permute-start.3 = (bf16[160,1024]{1,0:T(8,128)(2,1)S(1)}, bf16[160,1024]{1,0:T(8,128)(2,1)S(1)}, u32[]{:S(2)}, u32[]{:S(2)}) collective-permute-start(bf16[160,1024]{1,0:T(8,128)(2,1)S(1)} %slice.8.refs_1_), channel_id=1, source_target_pairs={{0,64},{64,128},{128,192},{192,0},{1,65},{65,129},{129,193},{193,1... | collective-permute-start | bytes 983048 | tf_op jit(solution)/shard_map/ppermute | solution.py:200
  61.0 26.9 %collective-permute-start.5 = (bf16[160,1024]{1,0:T(8,128)(2,1)S(1)}, bf16[160,1024]{1,0:T(8,128)(2,1)S(1)}, u32[]{:S(2)}, u32[]{:S(2)}) collective-permute-start(bf16[160,1024]{1,0:T(8,128)(2,1)S(1)} %slice.8.refs_1_), channel_id=1, source_target_pairs={{0,192},{64,0},{128,64},{192,128},{1,193},{65,1},{129,65},{193,129... | collective-permute-start | bytes 983048 | tf_op jit(solution)/shard_map/ppermute | solution.py:200
  62.9 0.7 copy-start.4
  75.0 33.6 %collective-permute-start.2 = (bf16[160,1152]{1,0:T(8,128)(2,1)S(1)}, bf16[160,1152]{1,0:T(8,128)(2,1)S(1)}, u32[]{:S(2)}, u32[]{:S(2)}) collective-permute-start(bf16[160,1152]{1,0:T(8,128)(2,1)S(1)} %attend2.1), channel_id=1, source_target_pairs={{0,128},{64,192},{128,0},{192,64},{1,129},{65,193},{129,1},{193,65... | collective-permute-start | bytes 1105928 | tf_op jit(solution)/shard_map/ppermute | solution.py:208
  85.8 22.8 %collective-permute-start.4 = (bf16[160,1152]{1,0:T(8,128)(2,1)S(1)}, bf16[160,1152]{1,0:T(8,128)(2,1)S(1)}, u32[]{:S(2)}, u32[]{:S(2)}) collective-permute-start(bf16[160,1152]{1,0:T(8,128)(2,1)S(1)} %attend1.1), channel_id=1, source_target_pairs={{0,192},{64,0},{128,64},{192,128},{1,193},{65,1},{129,65},{193,129... | collective-permute-start | bytes 1105928 | tf_op jit(solution)/shard_map/ppermute | solution.py:208
  95.3 13.3 %collective-permute-start.6 = (bf16[160,1152]{1,0:T(8,128)(2,1)S(1)}, bf16[160,1152]{1,0:T(8,128)(2,1)}, u32[]{:S(2)}, u32[]{:S(2)}) collective-permute-start(bf16[160,1152]{1,0:T(8,128)(2,1)S(1)} %attend3.1), channel_id=1, source_target_pairs={{0,64},{64,128},{128,192},{192,0},{1,65},{65,129},{129,193},{193,1... | collective-permute-start | bytes 1105928 | tf_op jit(solution)/shard_map/ppermute | solution.py:208
  107.8 0.8 copy-start
  108.6 0.7 copy-start.2
  108.6 0.8 copy-start.3

commit v2 on v1

v2 whole, which is shorter than its diff:
```python
import jax
import jax.numpy as jnp
from jax import lax
from jax.experimental import pallas as pl
from jax.experimental.pallas import tpu as pltpu
from jax.sharding import Mesh, PartitionSpec as P

HEAD_DIMENSION = 128
GROUP_HEADS = 8
PIECE = 20
BLOCK_TOKENS = 80
NX, NY, NZL, NZH = 4, 8, 2, 4
NZ = NZL * NZH
AXES = ("zl", "x", "y", "zh", "core")
LOG2E = 1.4426950408889634
SCALE = HEAD_DIMENSION ** (-0.5) * LOG2E
HIDDEN = -1e30
NB = NZL * NY * 2
KEYS = NB * BLOCK_TOKENS
TOKENS = NZ * PIECE
WIDTH = GROUP_HEADS * HEAD_DIMENSION
PART = 2 * PIECE
TILES = NX * NZL * 2
ROWS = GROUP_HEADS * PART
CHUNK = 512


def attend_kernel(meta, q_ref, own_ref, other_ref, out_ref, qa, ka, va, kp, qp, sc, mx, tb, acc):
    core = meta[0]

    def load_block(block, carry):
        rank = meta[8 + block]
        both = jnp.concatenate(
            [own_ref[block].astype(jnp.float32), other_ref[block].astype(jnp.float32)], axis=0
        ).astype(jnp.bfloat16)
        start = pl.multiple_of(rank * BLOCK_TOKENS, 16)
        ka[pl.ds(start, BLOCK_TOKENS), :] = both[:, 0:128]
        va[pl.ds(start, BLOCK_TOKENS), 0:128] = both[:, 128:256]
        return carry

    lax.fori_loop(0, NB, load_block, 0, unroll=4)
    va[:, 128:256] = jnp.ones((KEYS, 128), jnp.bfloat16)
    column = lax.broadcasted_iota(jnp.int32, (8, KEYS), 1)
    rank_of = column // BLOCK_TOKENS
    inner = column % BLOCK_TOKENS
    side = inner // PART
    inner = inner % PART
    key_core = jnp.where(side == 0, core, 1 - core)
    key_pos = (inner // PIECE) * PART + inner % PIECE + key_core * PIECE
    base = jnp.zeros((8, KEYS), jnp.int32)
    for rank in range(NB):
        base = jnp.where(rank_of == rank, meta[40 + rank], base)
    kp[...] = base * BLOCK_TOKENS + key_pos

    row = lax.broadcasted_iota(jnp.int32, (PART, 128), 0)
    row_offset = (row // PIECE) * PART + row % PIECE + core * PIECE
    lane = lax.broadcasted_iota(jnp.int32, (PART, 128), 1)
    hidden_row = jnp.full((ROWS, 128), -3e38, jnp.float32)

    def open_tile(tile):
        heads = [
            q_ref[tile, :, head * 128 : (head + 1) * 128].astype(jnp.float32)
            for head in range(GROUP_HEADS)
        ]
        qa[...] = jnp.concatenate(heads, axis=0).astype(jnp.bfloat16)
        pos = row_offset + meta[72 + tile] * BLOCK_TOKENS
        qp[...] = jnp.concatenate([pos] * GROUP_HEADS, axis=0)
        mx[...] = hidden_row

    def score(slot, j):
        start = pl.multiple_of(j * CHUNK, CHUNK)
        s = lax.dot_general(
            qa[...],
            ka[pl.ds(start, CHUNK), :],
            (((1,), (1,)), ((), ())),
            preferred_element_type=jnp.float32,
        )
        top = mx[...]
        own_pos = qp[...]
        for part in range(CHUNK // 128):
            at = pl.multiple_of(start + part * 128, 128)
            seen = kp[0:1, pl.ds(at, 128)] <= own_pos
            piece = jnp.where(seen, s[:, part * 128 : (part + 1) * 128], HIDDEN)
            sc[slot, j, :, part * 128 : (part + 1) * 128] = piece
            top = jnp.maximum(top, piece)
        mx[...] = top

    def mix(slot, j):
        start = pl.multiple_of(j * CHUNK, CHUNK)
        top = tb[...]
        weights = [
            jnp.exp2(sc[slot, j, :, part * 128 : (part + 1) * 128] * SCALE - top).astype(
                jnp.bfloat16
            )
            for part in range(CHUNK // 128)
        ]
        acc[...] += jnp.dot(
            jnp.concatenate(weights, axis=1),
            va[pl.ds(start, CHUNK), :],
            preferred_element_type=jnp.float32,
        )

    def start_mix():
        top = jnp.max(mx[...], axis=1, keepdims=True) * SCALE
        tb[...] = jnp.broadcast_to(top, (ROWS, 128))
        acc[...] = jnp.zeros((ROWS, 256), jnp.float32)

    def close_tile(tile):
        total = acc[:, 128:256]
        result = acc[:, 0:128] / total
        spread = tb[...] + jnp.log2(total)
        stats = jnp.zeros((PART, 128), jnp.float32)
        for head in range(GROUP_HEADS):
            rows = slice(head * PART, (head + 1) * PART)
            out_ref[tile, :, head * 128 : (head + 1) * 128] = result[rows].astype(jnp.bfloat16)
            level = spread[rows]
            high = level.astype(jnp.bfloat16).astype(jnp.float32)
            rest = level - high
            middle = rest.astype(jnp.bfloat16).astype(jnp.float32)
            low = rest - middle
            stats = jnp.where(lane == head, high, stats)
            stats = jnp.where(lane == 8 + head, middle, stats)
            stats = jnp.where(lane == 16 + head, low, stats)
        out_ref[tile, :, WIDTH : WIDTH + 128] = stats.astype(jnp.bfloat16)

    first = meta[88]
    open_tile(first)

    def first_step(j, carry):
        score(0, j)
        return carry

    lax.fori_loop(0, meta[104 + first], first_step, 0)
    start_mix()

    def one_tile(k, carry):
        tile = meta[88 + k]
        following = meta[88 + jnp.minimum(k + 1, TILES - 1)]
        open_tile(following)
        slot = lax.rem(k, 2)

        def step(j, inner_carry):
            score(1 - slot, j)
            mix(slot, j)
            return inner_carry

        lax.fori_loop(0, meta[104 + tile], step, 0)
        close_tile(tile)
        start_mix()
        return carry

    lax.fori_loop(0, TILES, one_tile, 0)


def attend(meta, q, own, other):
    return pl.pallas_call(
        attend_kernel,
        out_shape=jax.ShapeDtypeStruct((TILES, PART, WIDTH + 128), jnp.bfloat16),
        grid_spec=pltpu.PrefetchScalarGridSpec(
            num_scalar_prefetch=1,
            grid=(),
            in_specs=[pl.BlockSpec(memory_space=pltpu.VMEM)] * 3,
            out_specs=pl.BlockSpec(memory_space=pltpu.VMEM),
            scratch_shapes=[
                pltpu.VMEM((ROWS, 128), jnp.bfloat16),
                pltpu.VMEM((KEYS, 128), jnp.bfloat16),
                pltpu.VMEM((KEYS, 256), jnp.bfloat16),
                pltpu.VMEM((8, KEYS), jnp.int32),
                pltpu.VMEM((ROWS, 128), jnp.int32),
                pltpu.VMEM((2, KEYS // CHUNK, ROWS, CHUNK), jnp.float32),
                pltpu.VMEM((ROWS, 128), jnp.float32),
                pltpu.VMEM((ROWS, 128), jnp.float32),
                pltpu.VMEM((ROWS, 256), jnp.float32),
            ],
        ),
        compiler_params=pltpu.CompilerParams(vmem_limit_bytes=48 * 1024 * 1024),
        name="attend",
    )(meta, q, own, other)


def merge_kernel(parts, out_ref):
    stats = [parts[x, :, WIDTH : WIDTH + 128].astype(jnp.float32) for x in range(NX)]
    for head in range(GROUP_HEADS):
        levels = [
            (s[:, head : head + 1] + s[:, 8 + head : 9 + head]) + s[:, 16 + head : 17 + head]
            for s in stats
        ]
        top = levels[0]
        for level in levels[1:]:
            top = jnp.maximum(top, level)
        shares = [jnp.exp2(level - top) for level in levels]
        total = shares[0]
        for share in shares[1:]:
            total = total + share
        columns = slice(head * 128, (head + 1) * 128)
        mixed = sum(
            parts[x, :, columns].astype(jnp.float32) * (share / total)
            for x, share in enumerate(shares)
        )
        for z in range(NZ):
            out_ref[z, :, columns] = mixed[z * PIECE : (z + 1) * PIECE].astype(jnp.bfloat16)


def merge(parts):
    return pl.pallas_call(
        merge_kernel,
        out_shape=jax.ShapeDtypeStruct((NZ, PIECE, WIDTH), jnp.bfloat16),
        name="merge",
    )(parts)


def schedule(block_order):
    table = block_order.reshape(NZL, NX, NY, 2)
    key_block = lax.dynamic_index_in_dim(table, lax.axis_index("x"), 1, keepdims=False)
    key_block = key_block.transpose(1, 0, 2).reshape(NB)
    query_block = lax.dynamic_index_in_dim(table, lax.axis_index("y"), 2, keepdims=False)
    query_block = query_block.transpose(1, 0, 2).reshape(TILES)
    rank = jnp.sum((key_block[None, :] < key_block[:, None]).astype(jnp.int32), axis=1)
    numbers = jnp.arange(NB, dtype=jnp.int32)
    in_order = jnp.sum(
        jnp.where(rank[None, :] == numbers[:, None], key_block[None, :], 0), axis=1
    )
    seen = jnp.sum((key_block[None, :] <= query_block[:, None]).astype(jnp.int32), axis=1)
    chunks = jnp.maximum((seen * BLOCK_TOKENS + CHUNK - 1) // CHUNK, 1)
    tiles = jnp.arange(TILES, dtype=jnp.int32)
    weight = chunks * TILES + tiles
    place = jnp.sum((weight[None, :] > weight[:, None]).astype(jnp.int32), axis=1)
    tile_at = jnp.sum(jnp.where(place[None, :] == tiles[:, None], tiles[None, :], 0), axis=1)
    head = jnp.broadcast_to(lax.axis_index("core"), (8,)).astype(jnp.int32)
    return jnp.concatenate([head, rank, in_order, query_block, tile_at, chunks])


def ring(shift, size):
    return [(i, (i + shift) % size) for i in range(size)]


def over(x, axes):
    return lax.all_to_all(x, axes, split_axis=0, concat_axis=0, tiled=True)


def on_device(queries, keys, values, block_order):
    z_axes = ("zl", "zh")
    kv = jnp.concatenate(
        [keys.reshape(PIECE, NZ, HEAD_DIMENSION), values.reshape(PIECE, NZ, HEAD_DIMENSION)],
        axis=2,
    ).transpose(1, 0, 2)
    kv = over(kv, z_axes).reshape(TOKENS, 256)
    q = over(queries.reshape(PIECE, NZ, WIDTH).transpose(1, 0, 2), z_axes)
    own = over(jnp.broadcast_to(kv[None], (NY, TOKENS, 256)), "y").reshape(NB, PART, 256)
    q = over(jnp.broadcast_to(q.reshape(1, TOKENS, WIDTH), (NX, TOKENS, WIDTH)), "x")
    other = lax.ppermute(own, "core", ring(1, 2))
    meta = schedule(block_order)
    parts = attend(meta, q.reshape(TILES, PART, WIDTH), own, other)
    parts = over(parts.reshape(NX, TOKENS, WIDTH + 128), "x")
    attended = over(merge(parts), z_axes)
    return attended.transpose(1, 0, 2).reshape(PIECE, NZ * WIDTH)


def solution(mesh):
    fine = Mesh(mesh.devices.reshape(NZL, NX, NY, NZH, 2), AXES)
    rows = P(AXES, None)
    return jax.shard_map(
        on_device, mesh=fine, in_specs=(rows, rows, rows, P()), out_specs=rows, check_vma=False
    )
```

time: 134 us -> 173 us (1.29)
  the two profiles are of different devices: /device:TPU:6 before, /device:TPU:2 now
where the time goes in v2:
time: 173 us; the launch traced here: 170 us
  waiting for transfers between devices  47.5 us (27%)
  blocking collectives  45.1 us (26%)
  Pallas kernels  40.2 us (23%)
  starting transfers between devices  27.7 us (16%)
  local copies, waits for them, and re-layouts  7.62 us (4%)
    all_to_all x4, waiting for transfers between devices, over(): return lax.all_to_all(x, axes, split_axis=0, concat_axis=0, tiled=True)  47.5 us
    all_to_all x2, blocking collectives, over(): return lax.all_to_all(x, axes, split_axis=0, concat_axis=0, tiled=True)  45.1 us
    pallas_call x1, Pallas kernels, attend(): pl.pallas_call(attend_kernel, out_shape=jax.ShapeDtypeStruct((TILES, PART...  37.1 us
    all_to_all x4, starting transfers between devices, over(): return lax.all_to_all(x, axes, split_axis=0, concat_axis=0, tiled=True)  25.8 us
    unnamed x7, local copies, waits for them, and re-layouts  3.84 us
  transfers between devices with their start and end apart: 5, of which 4 were waited for; matrix products, arithmetic and copies ran while one was open for 2% of the time, Pallas kernels for 0%

profile of v2, /device:TPU:2, one launch (start us, length us, event | category | flops | bytes accessed | tf_op | source)
XLA Modules:
  0.0 169.7 jit_solution(3729428487763366503)
XLA Ops:
  0.0 0.8 copy.28
  0.8 0.8 copy.29
  1.7 0.6 maximum_bitcast_fusion
  2.3 10.3 %all-to-all-start.2 = ((bf16[8,20,256]{2,1,0:T(8,128)(2,1)}), bf16[8,20,256]{2,1,0:T(8,128)(2,1)S(1)}, u32[]{:S(2)}, u32[]{:S(2)}) async-start(bf16[8,20,256]{2,1,0:T(8,128)(2,1)} %maximum_bitcast_fusion), calls=%async_computation.2 | async-start | bytes 196608 | tf_op jit(solution)/shard_map/all_to_all | solution.py:238
  12.6 1.2 copy.27
  13.9 0.9 copy.34
  14.8 5.6 %all-to-all-done.2 = bf16[8,20,256]{2,1,0:T(8,128)(2,1)S(1)} async-done(((bf16[8,20,256]{2,1,0:T(8,128)(2,1)}), bf16[8,20,256]{2,1,0:T(8,128)(2,1)S(1)}, u32[]{:S(2)}, u32[]{:S(2)}) %all-to-all-start.2) | async-done | bytes 81952 | tf_op jit(solution)/shard_map/all_to_all | solution.py:238
  20.4 0.0 copy-start
  20.4 3.6 %all-to-all-start = ((bf16[8,20,1024]{2,1,0:T(8,128)(2,1)}), bf16[8,20,1024]{2,1,0:T(8,128)(2,1)S(1)}, u32[]{:S(2)}, u32[]{:S(2)}) async-start(bf16[8,20,1024]{2,1,0:T(8,128)(2,1)} %bitcast.28), calls=%async_computation | async-start | bytes 786432 | tf_op jit(solution)/shard_map/all_to_all | solution.py:238
  24.1 11.0 %all-to-all-done = bf16[8,20,1024]{2,1,0:T(8,128)(2,1)S(1)} async-done(((bf16[8,20,1024]{2,1,0:T(8,128)(2,1)}), bf16[8,20,1024]{2,1,0:T(8,128)(2,1)S(1)}, u32[]{:S(2)}, u32[]{:S(2)}) %all-to-all-start) | async-done | bytes 327712 | tf_op jit(solution)/shard_map/all_to_all | solution.py:238
  35.1 0.9 broadcast_in_dim.53
  35.9 7.1 %all-to-all-start.3 = ((bf16[8,160,256]{2,1,0:T(8,128)(2,1)}), bf16[8,160,256]{2,1,0:T(8,128)(2,1)S(1)}, u32[]{:S(2)}, u32[]{:S(2)}) async-start(bf16[8,160,256]{2,1,0:T(8,128)(2,1)} %broadcast_in_dim.53), calls=%async_computation.3 | async-start | bytes 1310720 | tf_op jit(solution)/shard_map/all_to_all | solution.py:238
  43.0 0.0 copy-done
  43.0 0.1 reshape.85
  43.2 0.1 broadcast_in_dim.50
  43.3 19.0 %all-to-all-done.3 = bf16[8,160,256]{2,1,0:T(8,128)(2,1)S(1)} async-done(((bf16[8,160,256]{2,1,0:T(8,128)(2,1)}), bf16[8,160,256]{2,1,0:T(8,128)(2,1)S(1)}, u32[]{:S(2)}, u32[]{:S(2)}) %all-to-all-start.3) | async-done | bytes 655392 | tf_op jit(solution)/shard_map/all_to_all | solution.py:238
  62.3 1.2 broadcast_in_dim.51
  63.5 4.8 %all-to-all-start.1 = ((bf16[4,160,1024]{2,1,0:T(8,128)(2,1)}), bf16[4,160,1024]{2,1,0:T(8,128)(2,1)S(1)}, u32[]{:S(2)}, u32[]{:S(2)}) async-start(bf16[4,160,1024]{2,1,0:T(8,128)(2,1)} %broadcast_in_dim.51), calls=%async_computation.1 | async-start | bytes 2621440 | tf_op jit(solution)/shard_map/all_to_all | solution.py:238
  68.3 0.1 lt.24
  68.5 0.1 reshape.86
  68.5 0.2 convert_reduce_fusion.2
  68.7 1.9 %collective-permute-start = (bf16[32,40,256]{2,1,0:T(8,128)(2,1)S(1)}, bf16[32,40,256]{2,1,0:T(8,128)(2,1)S(1)}, u32[]{:S(2)}, u32[]{:S(2)}) collective-permute-start(bf16[32,40,256]{2,1,0:T(8,128)(2,1)S(1)} %bitcast.33), channel_id=1, source_target_pairs={{0,1},{1,0},{2,3},{3,2},{4,5},{5,4},{6,7},{7,6},{8,9},{9,8},{10,11... | collective-permute-start | bytes 1966088 | tf_op jit(solution)/shard_map/ppermute | solution.py:251
  70.7 0.2 convert_reduce_fusion.1
  70.9 0.1 select_reduce_fusion.1
  71.0 0.2 convert_reduce_fusion
  71.2 0.1 select_reduce_fusion
  71.3 0.1 concatenate.6.meta
  71.4 11.8 %all-to-all-done.1 = bf16[4,160,1024]{2,1,0:T(8,128)(2,1)S(1)} async-done(((bf16[4,160,1024]{2,1,0:T(8,128)(2,1)}), bf16[4,160,1024]{2,1,0:T(8,128)(2,1)S(1)}, u32[]{:S(2)}, u32[]{:S(2)}) %all-to-all-start.1) | async-done | bytes 1310752 | tf_op jit(solution)/shard_map/all_to_all | solution.py:238
  83.2 0.0 collective-permute-done.other_ref
  83.2 37.1 %attend.1 = bf16[16,40,1152]{2,1,0:T(8,128)(2,1)S(1)} custom-call(s32[120]{0:T(128)S(1)} %concatenate.6.meta, bf16[16,40,1024]{2,1,0:T(8,128)(2,1)S(1)} %bitcast.32, bf16[32,40,256]{2,1,0:T(8,128)(2,1)S(1)} %bitcast.34, bf16[32,40,256]{2,1,0:T(8,128)(2,1)S(1)} %collective-permute-done.other_ref), custom_call_target="tpu_custom_call" | custom-call | tf_op jit(solution)/shard_map/attend/pallas_call | solution.py:156
  120.3 24.7 %all_to_all.30.parts = bf16[4,160,1152]{2,1,0:T(8,128)(2,1)} all-to-all(bf16[4,160,1152]{2,1,0:T(8,128)(2,1)S(1)} %bitcast.31), channel_id=1, replica_groups=mesh['zl'=2,'x'=4,'y'=8,'zh'=4,'core'=2] {'x'}, dimensions={0} | all-to-all | bytes 2949120 | tf_op jit(solution)/shard_map/all_to_all | solution.py:238
  145.0 3.1 %merge.1 = bf16[8,20,1024]{2,1,0:T(8,128)(2,1)} custom-call(bf16[4,160,1152]{2,1,0:T(8,128)(2,1)} %all_to_all.30.parts), custom_call_target="tpu_custom_call" | custom-call | tf_op jit(solution)/shard_map/merge/pallas_call | solution.py:205
  148.1 20.4 %all_to_all.31 = bf16[8,20,1024]{2,1,0:T(8,128)(2,1)S(1)} all-to-all(bf16[8,20,1024]{2,1,0:T(8,128)(2,1)} %merge.1), channel_id=1, replica_groups=mesh['zl'=2,'x'=4,'y'=8,'zh'=4,'core'=2] {'zl','zh'}, dimensions={0} | all-to-all | bytes 655360 | tf_op jit(solution)/shard_map/all_to_all | solution.py:238
  168.5 0.2 copy.24
  168.7 1.0 copy.30
  (13 shorter events, 0.2 us)
Async XLA Ops:
  2.3 18.1 %all-to-all-start.2 = ((bf16[8,20,256]{2,1,0:T(8,128)(2,1)}), bf16[8,20,256]{2,1,0:T(8,128)(2,1)S(1)}, u32[]{:S(2)}, u32[]{:S(2)}) async-start(bf16[8,20,256]{2,1,0:T(8,128)(2,1)} %maximum_bitcast_fusion), calls=%async_computation.2 | async-start | bytes 196608 | tf_op jit(solution)/shard_map/all_to_all | solution.py:238
  20.4 22.6 %copy-start = (s32[128]{0:T(128)S(1)}, s32[128]{0:T(128)}, u32[]{:S(2)}) copy-start(s32[128]{0:T(128)} %param.7) | copy-start | bytes 1540
  20.4 14.6 %all-to-all-start = ((bf16[8,20,1024]{2,1,0:T(8,128)(2,1)}), bf16[8,20,1024]{2,1,0:T(8,128)(2,1)S(1)}, u32[]{:S(2)}, u32[]{:S(2)}) async-start(bf16[8,20,1024]{2,1,0:T(8,128)(2,1)} %bitcast.28), calls=%async_computation | async-start | bytes 786432 | tf_op jit(solution)/shard_map/all_to_all | solution.py:238
  35.9 26.3 %all-to-all-start.3 = ((bf16[8,160,256]{2,1,0:T(8,128)(2,1)}), bf16[8,160,256]{2,1,0:T(8,128)(2,1)S(1)}, u32[]{:S(2)}, u32[]{:S(2)}) async-start(bf16[8,160,256]{2,1,0:T(8,128)(2,1)} %broadcast_in_dim.53), calls=%async_computation.3 | async-start | bytes 1310720 | tf_op jit(solution)/shard_map/all_to_all | solution.py:238
  63.5 19.7 %all-to-all-start.1 = ((bf16[4,160,1024]{2,1,0:T(8,128)(2,1)}), bf16[4,160,1024]{2,1,0:T(8,128)(2,1)S(1)}, u32[]{:S(2)}, u32[]{:S(2)}) async-start(bf16[4,160,1024]{2,1,0:T(8,128)(2,1)} %broadcast_in_dim.51), calls=%async_computation.1 | async-start | bytes 2621440 | tf_op jit(solution)/shard_map/all_to_all | solution.py:238
  68.7 14.5 %collective-permute-start = (bf16[32,40,256]{2,1,0:T(8,128)(2,1)S(1)}, bf16[32,40,256]{2,1,0:T(8,128)(2,1)S(1)}, u32[]{:S(2)}, u32[]{:S(2)}) collective-permute-start(bf16[32,40,256]{2,1,0:T(8,128)(2,1)S(1)} %bitcast.33), channel_id=1, source_target_pairs={{0,1},{1,0},{2,3},{3,2},{4,5},{5,4},{6,7},{7,6},{8,9},{9,8},{10,11... | collective-permute-start | bytes 1966088 | tf_op jit(solution)/shard_map/ppermute | solution.py:251

commit v3 on v2

--- a/solution.py
+++ b/solution.py
@@ -4,6 +4,7 @@
 from jax.experimental import pallas as pl
 from jax.experimental.pallas import tpu as pltpu
 from jax.sharding import Mesh, PartitionSpec as P
+
 
 HEAD_DIMENSION = 128
 GROUP_HEADS = 8
@@ -23,9 +24,12 @@
 TILES = NX * NZL * 2
 ROWS = GROUP_HEADS * PART
 CHUNK = 512
-
-
-def attend_kernel(meta, q_ref, own_ref, other_ref, out_ref, qa, ka, va, kp, qp, sc, mx, tb, acc):
+STRIP = 160
+
+
+def attend_kernel(
+    meta, q_ref, own_ref, other_ref, out_ref, qa, ka, va, kp, qp, sc_even, sc_odd, mx, tb, acc
+):
     core = meta[0]
 
     def load_block(block, carry):
@@ -67,38 +71,37 @@
         qp[...] = jnp.concatenate([pos] * GROUP_HEADS, axis=0)
         mx[...] = hidden_row
 
-    def score(slot, j):
+    def both(score_to, mix_from, j):
         start = pl.multiple_of(j * CHUNK, CHUNK)
-        s = lax.dot_general(
-            qa[...],
-            ka[pl.ds(start, CHUNK), :],
-            (((1,), (1,)), ((), ())),
-            preferred_element_type=jnp.float32,
-        )
-        top = mx[...]
-        own_pos = qp[...]
-        for part in range(CHUNK // 128):
-            at = pl.multiple_of(start + part * 128, 128)
-            seen = kp[0:1, pl.ds(at, 128)] <= own_pos
-            piece = jnp.where(seen, s[:, part * 128 : (part + 1) * 128], HIDDEN)
-            sc[slot, j, :, part * 128 : (part + 1) * 128] = piece
-            top = jnp.maximum(top, piece)
-        mx[...] = top
-
-    def mix(slot, j):
-        start = pl.multiple_of(j * CHUNK, CHUNK)
-        top = tb[...]
-        weights = [
-            jnp.exp2(sc[slot, j, :, part * 128 : (part + 1) * 128] * SCALE - top).astype(
-                jnp.bfloat16
-            )
+        parts = [slice(part * 128, (part + 1) * 128) for part in range(CHUNK // 128)]
+        keys = ka[pl.ds(start, CHUNK), :]
+        key_pos = [
+            kp[0:1, pl.ds(pl.multiple_of(start + part * 128, 128), 128)]
             for part in range(CHUNK // 128)
         ]
-        acc[...] += jnp.dot(
-            jnp.concatenate(weights, axis=1),
-            va[pl.ds(start, CHUNK), :],
-            preferred_element_type=jnp.float32,
-        )
+        values = va[pl.ds(start, CHUNK), :]
+        for at in range(0, ROWS, STRIP):
+            rows = slice(at, at + STRIP)
+            if mix_from is not None:
+                level = tb[rows, :]
+                weights = [
+                    jnp.exp2(mix_from[j, rows, part] * SCALE - level).astype(jnp.bfloat16)
+                    for part in parts
+                ]
+            s = lax.dot_general(
+                qa[rows, :], keys, (((1,), (1,)), ((), ())), preferred_element_type=jnp.float32
+            )
+            if mix_from is not None:
+                acc[rows, :] += jnp.dot(
+                    jnp.concatenate(weights, axis=1), values, preferred_element_type=jnp.float32
+                )
+            top = mx[rows, :]
+            query_pos = qp[rows, :]
+            for part, pos in zip(parts, key_pos):
+                piece = jnp.where(pos <= query_pos, s[:, part], HIDDEN)
+                score_to[j, rows, part] = piece
+                top = jnp.maximum(top, piece)
+            mx[rows, :] = top
 
     def start_mix():
         top = jnp.max(mx[...], axis=1, keepdims=True) * SCALE
@@ -127,29 +130,29 @@
     open_tile(first)
 
     def first_step(j, carry):
-        score(0, j)
+        both(sc_even, None, j)
         return carry
 
     lax.fori_loop(0, meta[104 + first], first_step, 0)
     start_mix()
 
-    def one_tile(k, carry):
-        tile = meta[88 + k]
-        following = meta[88 + jnp.minimum(k + 1, TILES - 1)]
-        open_tile(following)
-        slot = lax.rem(k, 2)
-
-        def step(j, inner_carry):
-            score(1 - slot, j)
-            mix(slot, j)
-            return inner_carry
-
-        lax.fori_loop(0, meta[104 + tile], step, 0)
-        close_tile(tile)
-        start_mix()
+    def two_tiles(pair, carry):
+        for odd in range(2):
+            k = pair * 2 + odd
+            tile = meta[88 + k]
+            open_tile(meta[88 + jnp.minimum(k + 1, TILES - 1)])
+            mix_from, score_to = (sc_odd, sc_even) if odd else (sc_even, sc_odd)
+
+            def step(j, inner_carry):
+                both(score_to, mix_from, j)
+                return inner_carry
+
+            lax.fori_loop(0, meta[104 + tile], step, 0)
+            close_tile(tile)
+            start_mix()
         return carry
 
-    lax.fori_loop(0, TILES, one_tile, 0)
+    lax.fori_loop(0, TILES // 2, two_tiles, 0)
 
 
 def attend(meta, q, own, other):
@@ -167,7 +170,8 @@
                 pltpu.VMEM((KEYS, 256), jnp.bfloat16),
                 pltpu.VMEM((8, KEYS), jnp.int32),
                 pltpu.VMEM((ROWS, 128), jnp.int32),
-                pltpu.VMEM((2, KEYS // CHUNK, ROWS, CHUNK), jnp.float32),
+                pltpu.VMEM((KEYS // CHUNK, ROWS, CHUNK), jnp.float32),
+                pltpu.VMEM((KEYS // CHUNK, ROWS, CHUNK), jnp.float32),
                 pltpu.VMEM((ROWS, 128), jnp.float32),
                 pltpu.VMEM((ROWS, 128), jnp.float32),
                 pltpu.VMEM((ROWS, 256), jnp.float32),
@@ -240,14 +244,19 @@
 
 def on_device(queries, keys, values, block_order):
     z_axes = ("zl", "zh")
-    kv = jnp.concatenate(
-        [keys.reshape(PIECE, NZ, HEAD_DIMENSION), values.reshape(PIECE, NZ, HEAD_DIMENSION)],
+    packed = jnp.concatenate(
+        [
+            queries.reshape(PIECE, NZ, WIDTH),
+            keys.reshape(PIECE, NZ, HEAD_DIMENSION),
+            values.reshape(PIECE, NZ, HEAD_DIMENSION),
+        ],
         axis=2,
     ).transpose(1, 0, 2)
-    kv = over(kv, z_axes).reshape(TOKENS, 256)
-    q = over(queries.reshape(PIECE, NZ, WIDTH).transpose(1, 0, 2), z_axes)
-    own = over(jnp.broadcast_to(kv[None], (NY, TOKENS, 256)), "y").reshape(NB, PART, 256)
-    q = over(jnp.broadcast_to(q.reshape(1, TOKENS, WIDTH), (NX, TOKENS, WIDTH)), "x")
+    packed = over(packed, z_axes).reshape(TOKENS, WIDTH + 256)
+    kv = packed[:, WIDTH:]
+    q = over(jnp.broadcast_to(packed[None, :, :WIDTH], (NX, TOKENS, WIDTH)), "x")
+    own = lax.all_gather(kv, "y", axis=0, tiled=True)
+    own = own.reshape(NB, PART, 256)
     other = lax.ppermute(own, "core", ring(1, 2))
     meta = schedule(block_order)
     parts = attend(meta, q.reshape(TILES, PART, WIDTH), own, other)

time: 173 us -> 137 us (0.79)
  the two profiles are of different devices: /device:TPU:2 before, /device:TPU:56 now
where the time goes in v3:
time: 137 us
  blocking collectives  69.7 us (51%)
  Pallas kernels  27.6 us (20%)
  starting transfers between devices  16.5 us (12%)
  waiting for transfers between devices  15.1 us (11%)
  local copies, waits for them, and re-layouts  6.04 us (4%)
  other arithmetic  1.6 us (1%)
    all_to_all x2, blocking collectives, over(): return lax.all_to_all(x, axes, split_axis=0, concat_axis=0, tiled=True)  43.9 us
    all_gather x1, blocking collectives, on_device(): own = lax.all_gather(kv, 'y', axis=0, tiled=True)  25.8 us
    pallas_call x1, Pallas kernels, attend(): pl.pallas_call(attend_kernel, out_shape=jax.ShapeDtypeStruct((TILES, PART...  24.5 us
    all_to_all x2, starting transfers between devices, over(): return lax.all_to_all(x, axes, split_axis=0, concat_axis=0, tiled=True)  14.6 us
    all_to_all x2, waiting for transfers between devices, over(): return lax.all_to_all(x, axes, split_axis=0, concat_axis=0, tiled=True)  13.7 us
    unnamed x7, local copies, waits for them, and re-layouts  3.84 us
    pallas_call x1, Pallas kernels, merge(): pl.pallas_call(merge_kernel, out_shape=jax.ShapeDtypeStruct((NZ, PIECE, W...  3.1 us
  transfers between devices with their start and end apart: 3, of which 2 were waited for; matrix products, arithmetic and copies ran while one was open for 1% of the time, Pallas kernels for 0%

profile of v3, /device:TPU:56, one launch (start us, length us, event | category | flops | bytes accessed | tf_op | source)
XLA Modules:
  0.0 136.6 jit_solution(15433213052955372040)
XLA Ops:
  0.0 0.8 copy.29
  0.8 0.8 copy.30
  1.7 1.2 copy.28
  2.9 0.0 copy-start
  2.9 0.2 copy.22
  3.1 0.8 maximum_bitcast_fusion
  3.9 10.3 %all-to-all-start = ((bf16[8,20,1280]{2,1,0:T(8,128)(2,1)}), bf16[8,20,1280]{2,1,0:T(8,128)(2,1)S(1)}, u32[]{:S(2)}, u32[]{:S(2)}) async-start(bf16[8,20,1280]{2,1,0:T(8,128)(2,1)} %maximum_bitcast_fusion), calls=%async_computation | async-start | bytes 983040 | tf_op jit(solution)/shard_map/all_to_all | solution.py:242
  14.3 0.0 copy-done
  14.3 0.1 reshape.86
  14.4 0.1 lt.24
  14.6 0.1 reshape.87
  14.6 13.7 %all-to-all-done = bf16[8,20,1280]{2,1,0:T(8,128)(2,1)S(1)} async-done(((bf16[8,20,1280]{2,1,0:T(8,128)(2,1)}), bf16[8,20,1280]{2,1,0:T(8,128)(2,1)S(1)}, u32[]{:S(2)}, u32[]{:S(2)}) %all-to-all-start) | async-done | bytes 409632 | tf_op jit(solution)/shard_map/all_to_all | solution.py:242
  28.4 0.1 reshape.91
  28.5 1.2 broadcast_in_dim.42
  29.7 4.3 %all-to-all-start.1 = ((bf16[4,160,1024]{2,1,0:T(8,128)(2,1)}), bf16[4,160,1024]{2,1,0:T(8,128)(2,1)S(1)}, u32[]{:S(2)}, u32[]{:S(2)}) async-start(bf16[4,160,1024]{2,1,0:T(8,128)(2,1)} %broadcast_in_dim.42), calls=%async_computation.1 | async-start | bytes 2621440 | tf_op jit(solution)/shard_map/all_to_all | solution.py:242
  34.0 0.2 convert_reduce_fusion.2
  34.2 25.8 %all_gather.3 = bf16[1280,256]{1,0:T(8,128)(2,1)S(1)} all-gather(bf16[160,256]{1,0:T(8,128)(2,1)S(1)} %slice.9), channel_id=1, replica_groups=mesh['zl'=2,'x'=4,'y'=8,'zh'=4,'core'=2] {'y'}, dimensions={0}, use_global_device_ids=true | all-gather | bytes 737280 | tf_op jit(solution)/shard_map/all_gather | solution.py:258
  60.0 1.9 %collective-permute-start = (bf16[32,40,256]{2,1,0:T(8,128)(2,1)S(1)}, bf16[32,40,256]{2,1,0:T(8,128)(2,1)S(1)}, u32[]{:S(2)}, u32[]{:S(2)}) collective-permute-start(bf16[32,40,256]{2,1,0:T(8,128)(2,1)S(1)} %bitcast.30), channel_id=1, source_target_pairs={{0,1},{1,0},{2,3},{3,2},{4,5},{5,4},{6,7},{7,6},{8,9},{9,8},{10,11... | collective-permute-start | bytes 1966088 | tf_op jit(solution)/shard_map/ppermute | solution.py:260
  61.9 0.2 convert_reduce_fusion.1
  62.1 0.1 select_reduce_fusion.1
  62.2 0.2 convert_reduce_fusion
  62.4 0.1 select_reduce_fusion
  62.5 0.1 concatenate.6.meta
  62.6 1.3 collective-permute-done.other_ref
  64.0 0.0 all-to-all-done.1
  64.0 24.5 %attend.1 = bf16[16,40,1152]{2,1,0:T(8,128)(2,1)S(1)} custom-call(s32[120]{0:T(128)S(1)} %concatenate.6.meta, bf16[16,40,1024]{2,1,0:T(8,128)(2,1)S(1)} %bitcast.29, bf16[32,40,256]{2,1,0:T(8,128)(2,1)S(1)} %bitcast.31, bf16[32,40,256]{2,1,0:T(8,128)(2,1)S(1)} %collective-permute-done.other_ref), custom_call_target="tpu_custom_call" | custom-call | tf_op jit(solution)/shard_map/attend/pallas_call | solution.py:159
  88.4 26.1 %all_to_all.20.parts = bf16[4,160,1152]{2,1,0:T(8,128)(2,1)} all-to-all(bf16[4,160,1152]{2,1,0:T(8,128)(2,1)S(1)} %bitcast.28), channel_id=1, replica_groups=mesh['zl'=2,'x'=4,'y'=8,'zh'=4,'core'=2] {'x'}, dimensions={0} | all-to-all | bytes 2949120 | tf_op jit(solution)/shard_map/all_to_all | solution.py:242
  114.5 3.1 %merge.1 = bf16[8,20,1024]{2,1,0:T(8,128)(2,1)} custom-call(bf16[4,160,1152]{2,1,0:T(8,128)(2,1)} %all_to_all.20.parts), custom_call_target="tpu_custom_call" | custom-call | tf_op jit(solution)/shard_map/merge/pallas_call | solution.py:209
  117.6 17.8 %all_to_all.21 = bf16[8,20,1024]{2,1,0:T(8,128)(2,1)S(1)} all-to-all(bf16[8,20,1024]{2,1,0:T(8,128)(2,1)} %merge.1), channel_id=1, replica_groups=mesh['zl'=2,'x'=4,'y'=8,'zh'=4,'core'=2] {'zl','zh'}, dimensions={0} | all-to-all | bytes 655360 | tf_op jit(solution)/shard_map/all_to_all | solution.py:242
  135.4 0.2 copy.25
  135.7 1.0 copy.31
  (14 shorter events, 0.2 us)
Async XLA Ops:
  2.9 11.3 %copy-start = (s32[128]{0:T(128)S(1)}, s32[128]{0:T(128)}, u32[]{:S(2)}) copy-start(s32[128]{0:T(128)} %param.7) | copy-start | bytes 1540
  3.9 24.4 %all-to-all-start = ((bf16[8,20,1280]{2,1,0:T(8,128)(2,1)}), bf16[8,20,1280]{2,1,0:T(8,128)(2,1)S(1)}, u32[]{:S(2)}, u32[]{:S(2)}) async-start(bf16[8,20,1280]{2,1,0:T(8,128)(2,1)} %maximum_bitcast_fusion), calls=%async_computation | async-start | bytes 983040 | tf_op jit(solution)/shard_map/all_to_all | solution.py:242
  29.7 34.3 %all-to-all-start.1 = ((bf16[4,160,1024]{2,1,0:T(8,128)(2,1)}), bf16[4,160,1024]{2,1,0:T(8,128)(2,1)S(1)}, u32[]{:S(2)}, u32[]{:S(2)}) async-start(bf16[4,160,1024]{2,1,0:T(8,128)(2,1)} %broadcast_in_dim.42), calls=%async_computation.1 | async-start | bytes 2621440 | tf_op jit(solution)/shard_map/all_to_all | solution.py:242
  60.0 4.0 %collective-permute-start = (bf16[32,40,256]{2,1,0:T(8,128)(2,1)S(1)}, bf16[32,40,256]{2,1,0:T(8,128)(2,1)S(1)}, u32[]{:S(2)}, u32[]{:S(2)}) collective-permute-start(bf16[32,40,256]{2,1,0:T(8,128)(2,1)S(1)} %bitcast.30), channel_id=1, source_target_pairs={{0,1},{1,0},{2,3},{3,2},{4,5},{5,4},{6,7},{7,6},{8,9},{9,8},{10,11... | collective-permute-start | bytes 1966088 | tf_op jit(solution)/shard_map/ppermute | solution.py:260

commit v4 on v3

--- a/solution.py
+++ b/solution.py
@@ -21,14 +21,16 @@
 TOKENS = NZ * PIECE
 WIDTH = GROUP_HEADS * HEAD_DIMENSION
 PART = 2 * PIECE
-TILES = NX * NZL * 2
+OWN_TILES = NZL * 2
+TILES = NX * OWN_TILES
 ROWS = GROUP_HEADS * PART
 CHUNK = 512
 STRIP = 160
 
 
 def attend_kernel(
-    meta, q_ref, own_ref, other_ref, out_ref, qa, ka, va, kp, qp, sc_even, sc_odd, mx, tb, acc
+    tiles, first_place, meta, q_ref, own_ref, other_ref, kp, out_ref, qa, ka, va, qp, sc_even,
+    sc_odd, mx, tb, acc
 ):
     core = meta[0]
 
@@ -44,18 +46,6 @@
 
     lax.fori_loop(0, NB, load_block, 0, unroll=4)
     va[:, 128:256] = jnp.ones((KEYS, 128), jnp.bfloat16)
-    column = lax.broadcasted_iota(jnp.int32, (8, KEYS), 1)
-    rank_of = column // BLOCK_TOKENS
-    inner = column % BLOCK_TOKENS
-    side = inner // PART
-    inner = inner % PART
-    key_core = jnp.where(side == 0, core, 1 - core)
-    key_pos = (inner // PIECE) * PART + inner % PIECE + key_core * PIECE
-    base = jnp.zeros((8, KEYS), jnp.int32)
-    for rank in range(NB):
-        base = jnp.where(rank_of == rank, meta[40 + rank], base)
-    kp[...] = base * BLOCK_TOKENS + key_pos
-
     row = lax.broadcasted_iota(jnp.int32, (PART, 128), 0)
     row_offset = (row // PIECE) * PART + row % PIECE + core * PIECE
     lane = lax.broadcasted_iota(jnp.int32, (PART, 128), 1)
@@ -109,13 +99,14 @@
         acc[...] = jnp.zeros((ROWS, 256), jnp.float32)
 
     def close_tile(tile):
+        place = lax.rem(tile, OWN_TILES) if tiles == OWN_TILES else tile
         total = acc[:, 128:256]
         result = acc[:, 0:128] / total
         spread = tb[...] + jnp.log2(total)
         stats = jnp.zeros((PART, 128), jnp.float32)
         for head in range(GROUP_HEADS):
             rows = slice(head * PART, (head + 1) * PART)
-            out_ref[tile, :, head * 128 : (head + 1) * 128] = result[rows].astype(jnp.bfloat16)
+            out_ref[place, :, head * 128 : (head + 1) * 128] = result[rows].astype(jnp.bfloat16)
             level = spread[rows]
             high = level.astype(jnp.bfloat16).astype(jnp.float32)
             rest = level - high
@@ -124,9 +115,9 @@
             stats = jnp.where(lane == head, high, stats)
             stats = jnp.where(lane == 8 + head, middle, stats)
             stats = jnp.where(lane == 16 + head, low, stats)
-        out_ref[tile, :, WIDTH : WIDTH + 128] = stats.astype(jnp.bfloat16)
-
-    first = meta[88]
+        out_ref[place, :, WIDTH : WIDTH + 128] = stats.astype(jnp.bfloat16)
+
+    first = meta[88 + first_place]
     open_tile(first)
 
     def first_step(j, carry):
@@ -136,11 +127,17 @@
     lax.fori_loop(0, meta[104 + first], first_step, 0)
     start_mix()
 
+    if tiles == TILES - OWN_TILES:
+        own_x = meta[1]
+        out_ref[pl.ds(own_x * OWN_TILES, OWN_TILES)] = jnp.zeros(
+            (OWN_TILES, PART, WIDTH + 128), jnp.bfloat16
+        )
+
     def two_tiles(pair, carry):
         for odd in range(2):
             k = pair * 2 + odd
-            tile = meta[88 + k]
-            open_tile(meta[88 + jnp.minimum(k + 1, TILES - 1)])
+            tile = meta[88 + first_place + k]
+            open_tile(meta[88 + first_place + jnp.minimum(k + 1, tiles - 1)])
             mix_from, score_to = (sc_odd, sc_even) if odd else (sc_even, sc_odd)
 
             def step(j, inner_carry):
@@ -152,23 +149,30 @@
             start_mix()
         return carry
 
-    lax.fori_loop(0, TILES // 2, two_tiles, 0)
-
-
-def attend(meta, q, own, other):
+    lax.fori_loop(0, tiles // 2, two_tiles, 0)
+
+
+def attend(mine, meta, q, own, other, key_pos):
+    tiles = OWN_TILES if mine else TILES - OWN_TILES
+    first_place = TILES - OWN_TILES if mine else 0
+
+    def kernel(*refs):
+        attend_kernel(tiles, first_place, *refs)
+
     return pl.pallas_call(
-        attend_kernel,
-        out_shape=jax.ShapeDtypeStruct((TILES, PART, WIDTH + 128), jnp.bfloat16),
+        kernel,
+        out_shape=jax.ShapeDtypeStruct(
+            (OWN_TILES if mine else TILES, PART, WIDTH + 128), jnp.bfloat16
+        ),
         grid_spec=pltpu.PrefetchScalarGridSpec(
             num_scalar_prefetch=1,
             grid=(),
-            in_specs=[pl.BlockSpec(memory_space=pltpu.VMEM)] * 3,
+            in_specs=[pl.BlockSpec(memory_space=pltpu.VMEM)] * 4,
             out_specs=pl.BlockSpec(memory_space=pltpu.VMEM),
             scratch_shapes=[
                 pltpu.VMEM((ROWS, 128), jnp.bfloat16),
                 pltpu.VMEM((KEYS, 128), jnp.bfloat16),
                 pltpu.VMEM((KEYS, 256), jnp.bfloat16),
-                pltpu.VMEM((8, KEYS), jnp.int32),
                 pltpu.VMEM((ROWS, 128), jnp.int32),
                 pltpu.VMEM((KEYS // CHUNK, ROWS, CHUNK), jnp.float32),
                 pltpu.VMEM((KEYS // CHUNK, ROWS, CHUNK), jnp.float32),
@@ -178,39 +182,49 @@
             ],
         ),
         compiler_params=pltpu.CompilerParams(vmem_limit_bytes=48 * 1024 * 1024),
-        name="attend",
-    )(meta, q, own, other)
-
-
-def merge_kernel(parts, out_ref):
-    stats = [parts[x, :, WIDTH : WIDTH + 128].astype(jnp.float32) for x in range(NX)]
+        name="attend_own" if mine else "attend_rest",
+    )(meta, q, own, other, key_pos)
+
+
+def merge_kernel(own_x, parts, mine, out_ref):
+    levels = []
+    for x in range(NX):
+        stats = jnp.where(
+            own_x[0] == x,
+            mine[:, WIDTH : WIDTH + 128].astype(jnp.float32),
+            parts[x, :, WIDTH : WIDTH + 128].astype(jnp.float32),
+        )
+        levels.append((stats + pltpu.roll(stats, 120, 1)) + pltpu.roll(stats, 112, 1))
+    top = levels[0]
+    for level in levels[1:]:
+        top = jnp.maximum(top, level)
+    shares = [jnp.exp2(level - top) for level in levels]
+    total = shares[0]
+    for share in shares[1:]:
+        total = total + share
+    shares = [share / total for share in shares]
+    keep = [jnp.where(own_x[0] == x, 0.0, share) for x, share in enumerate(shares)]
+    home = sum(share - other for share, other in zip(shares, keep))
     for head in range(GROUP_HEADS):
-        levels = [
-            (s[:, head : head + 1] + s[:, 8 + head : 9 + head]) + s[:, 16 + head : 17 + head]
-            for s in stats
-        ]
-        top = levels[0]
-        for level in levels[1:]:
-            top = jnp.maximum(top, level)
-        shares = [jnp.exp2(level - top) for level in levels]
-        total = shares[0]
-        for share in shares[1:]:
-            total = total + share
         columns = slice(head * 128, (head + 1) * 128)
-        mixed = sum(
-            parts[x, :, columns].astype(jnp.float32) * (share / total)
-            for x, share in enumerate(shares)
-        )
+        mixed = mine[:, columns].astype(jnp.float32) * home[:, head : head + 1]
+        for x in range(NX):
+            mixed += parts[x, :, columns].astype(jnp.float32) * keep[x][:, head : head + 1]
         for z in range(NZ):
             out_ref[z, :, columns] = mixed[z * PIECE : (z + 1) * PIECE].astype(jnp.bfloat16)
 
 
-def merge(parts):
+def merge(own_x, parts, mine):
     return pl.pallas_call(
         merge_kernel,
         out_shape=jax.ShapeDtypeStruct((NZ, PIECE, WIDTH), jnp.bfloat16),
+        in_specs=[
+            pl.BlockSpec(memory_space=pltpu.SMEM),
+            pl.BlockSpec(memory_space=pltpu.VMEM),
+            pl.BlockSpec(memory_space=pltpu.VMEM),
+        ],
         name="merge",
-    )(parts)
+    )(own_x, parts, mine)
 
 
 def schedule(block_order):
@@ -227,11 +241,20 @@
     seen = jnp.sum((key_block[None, :] <= query_block[:, None]).astype(jnp.int32), axis=1)
     chunks = jnp.maximum((seen * BLOCK_TOKENS + CHUNK - 1) // CHUNK, 1)
     tiles = jnp.arange(TILES, dtype=jnp.int32)
-    weight = chunks * TILES + tiles
+    own_x = lax.axis_index("x")
+    remote = (tiles // OWN_TILES != own_x).astype(jnp.int32)
+    weight = (remote * 64 + chunks) * TILES + tiles
     place = jnp.sum((weight[None, :] > weight[:, None]).astype(jnp.int32), axis=1)
     tile_at = jnp.sum(jnp.where(place[None, :] == tiles[:, None], tiles[None, :], 0), axis=1)
-    head = jnp.broadcast_to(lax.axis_index("core"), (8,)).astype(jnp.int32)
-    return jnp.concatenate([head, rank, in_order, query_block, tile_at, chunks])
+    spot = jnp.arange(BLOCK_TOKENS, dtype=jnp.int32)
+    core = lax.axis_index("core")
+    key_core = jnp.where(spot < PART, core, 1 - core)
+    inner = spot % PART
+    place = (inner // PIECE) * PART + inner % PIECE + key_core * PIECE
+    key_pos = in_order[:, None] * BLOCK_TOKENS + place[None, :]
+    head = jnp.concatenate([core.reshape(1), own_x.reshape(1), jnp.zeros((6,), jnp.int32)])
+    meta = jnp.concatenate([head, rank, in_order, query_block, tile_at, chunks])
+    return meta, key_pos.reshape(1, KEYS)
 
 
 def ring(shift, size):
@@ -258,10 +281,12 @@
     own = lax.all_gather(kv, "y", axis=0, tiled=True)
     own = own.reshape(NB, PART, 256)
     other = lax.ppermute(own, "core", ring(1, 2))
-    meta = schedule(block_order)
-    parts = attend(meta, q.reshape(TILES, PART, WIDTH), own, other)
+    meta, key_pos = schedule(block_order)
+    q = q.reshape(TILES, PART, WIDTH)
+    parts = attend(False, meta, q, own, other, key_pos)
     parts = over(parts.reshape(NX, TOKENS, WIDTH + 128), "x")
-    attended = over(merge(parts), z_axes)
+    mine = attend(True, meta, q, own, other, key_pos).reshape(TOKENS, WIDTH + 128)
+    attended = over(merge(meta[1:2], parts, mine), z_axes)
     return attended.transpose(1, 0, 2).reshape(PIECE, NZ * WIDTH)
 
 

time: 137 us -> 134 us (0.978)
  blocking collectives: 69.7 us -> 43.7 us
  waiting for transfers between devices: 15.1 us -> 25.4 us
  starting transfers between devices: 16.5 us -> 24.4 us
  Pallas kernels: 27.6 us -> 30.9 us
    all_to_all x2 -> x1, blocking collectives: 43.9 us -> 17.9 us  [over(): return lax.all_to_all(x, axes, split_axis=0, concat_axis=0, tiled=True)]
    all_to_all x2 -> x3, waiting for transfers between devices: 13.7 us -> 24.2 us  [over(): return lax.all_to_all(x, axes, split_axis=0, concat_axis=0, tiled=True)]
    all_to_all x2 -> x3, starting transfers between devices: 14.6 us -> 22.4 us  [over(): return lax.all_to_all(x, axes, split_axis=0, concat_axis=0, tiled=True)]
    pallas_call x1 -> x2, Pallas kernels: 24.5 us -> 27.5 us  [attend(): pl.pallas_call(kernel, out_shape=jax.ShapeDtypeStruct((OWN_TILES if mine...]
    unnamed x7 -> x9, local copies, waits for them, and re-layouts: 3.84 us -> 4.58 us
  transfers between devices with their start and end apart: 3 -> 4, of which waited for: 2 -> 3; matrix products, arithmetic and copies ran while one was open for 1% -> 1% of each run, Pallas kernels for 0% -> 7%
where the time goes in v4:
time: 134 us; the launch traced here: 133 us
  blocking collectives  43.7 us (33%)
  Pallas kernels  30.9 us (23%)
  waiting for transfers between devices  25.4 us (19%)
  starting transfers between devices  24.4 us (18%)
  local copies, waits for them, and re-layouts  6.86 us (5%)
  other arithmetic  1.7 us (1%)
    pallas_call x2, Pallas kernels, attend(): pl.pallas_call(kernel, out_shape=jax.ShapeDtypeStruct((OWN_TILES if mine...  27.5 us
    all_gather x1, blocking collectives, on_device(): own = lax.all_gather(kv, 'y', axis=0, tiled=True)  25.8 us
    all_to_all x3, waiting for transfers between devices, over(): return lax.all_to_all(x, axes, split_axis=0, concat_axis=0, tiled=True)  24.2 us
    all_to_all x3, starting transfers between devices, over(): return lax.all_to_all(x, axes, split_axis=0, concat_axis=0, tiled=True)  22.4 us
    all_to_all x1, blocking collectives, over(): return lax.all_to_all(x, axes, split_axis=0, concat_axis=0, tiled=True)  17.9 us
    unnamed x9, local copies, waits for them, and re-layouts  4.58 us
    pallas_call x1, Pallas kernels, merge(): pl.pallas_call(merge_kernel, out_shape=jax.ShapeDtypeStruct((NZ, PIECE, W...  3.38 us
  transfers between devices with their start and end apart: 4, of which 3 were waited for; matrix products, arithmetic and copies ran while one was open for 1% of the time, Pallas kernels for 7%

profile of v4, /device:TPU:56, one launch (start us, length us, event | category | flops | bytes accessed | tf_op | source)
XLA Modules:
  0.0 133.2 jit_solution(16886067802707311744)
XLA Ops:
  0.0 0.8 copy.29
  0.8 0.8 copy.30
  1.7 1.2 copy.28
  2.9 0.0 copy-start.1
  2.9 0.2 copy.22
  3.1 0.8 maximum_bitcast_fusion
  3.9 10.3 %all-to-all-start = ((bf16[8,20,1280]{2,1,0:T(8,128)(2,1)}), bf16[8,20,1280]{2,1,0:T(8,128)(2,1)S(1)}, u32[]{:S(2)}, u32[]{:S(2)}) async-start(bf16[8,20,1280]{2,1,0:T(8,128)(2,1)} %maximum_bitcast_fusion), calls=%async_computation | async-start | bytes 983040 | tf_op jit(solution)/shard_map/all_to_all | solution.py:265
  14.3 0.0 copy-done.1
  14.3 0.1 reshape.180
  14.4 0.1 lt.41
  14.6 0.2 convert_reduce_fusion
  14.7 0.1 select_reduce_fusion
  14.9 13.5 %all-to-all-done = bf16[8,20,1280]{2,1,0:T(8,128)(2,1)S(1)} async-done(((bf16[8,20,1280]{2,1,0:T(8,128)(2,1)}), bf16[8,20,1280]{2,1,0:T(8,128)(2,1)S(1)}, u32[]{:S(2)}, u32[]{:S(2)}) %all-to-all-start) | async-done | bytes 409632 | tf_op jit(solution)/shard_map/all_to_all | solution.py:265
  28.4 0.1 reshape.185
  28.5 1.2 broadcast_in_dim.48
  29.7 4.3 %all-to-all-start.1 = ((bf16[4,160,1024]{2,1,0:T(8,128)(2,1)}), bf16[4,160,1024]{2,1,0:T(8,128)(2,1)S(1)}, u32[]{:S(2)}, u32[]{:S(2)}) async-start(bf16[4,160,1024]{2,1,0:T(8,128)(2,1)} %broadcast_in_dim.48), calls=%async_computation.1 | async-start | bytes 2621440 | tf_op jit(solution)/shard_map/all_to_all | solution.py:265
  34.0 0.1 broadcast_add_fusion
  34.1 25.8 %all_gather.3 = bf16[1280,256]{1,0:T(8,128)(2,1)S(1)} all-gather(bf16[160,256]{1,0:T(8,128)(2,1)S(1)} %slice.9), channel_id=1, replica_groups=mesh['zl'=2,'x'=4,'y'=8,'zh'=4,'core'=2] {'y'}, dimensions={0}, use_global_device_ids=true | all-gather | bytes 737280 | tf_op jit(solution)/shard_map/all_gather | solution.py:281
  59.9 1.9 %collective-permute-start = (bf16[32,40,256]{2,1,0:T(8,128)(2,1)S(1)}, bf16[32,40,256]{2,1,0:T(8,128)(2,1)S(1)}, u32[]{:S(2)}, u32[]{:S(2)}) collective-permute-start(bf16[32,40,256]{2,1,0:T(8,128)(2,1)S(1)} %bitcast.33), channel_id=1, source_target_pairs={{0,1},{1,0},{2,3},{3,2},{4,5},{5,4},{6,7},{7,6},{8,9},{9,8},{10,11... | collective-permute-start | bytes 1966088 | tf_op jit(solution)/shard_map/ppermute | solution.py:283
  61.9 0.1 reshape.181
  62.0 0.1 add.137.refs_4_
  62.1 0.2 convert_reduce_fusion.2
  62.3 0.2 convert_reduce_fusion.1
  62.4 0.1 select_reduce_fusion.1
  62.6 0.1 concatenate.6.refs_0_
  62.6 1.3 collective-permute-done.refs_3_
  63.9 0.0 all-to-all-done.1
  63.9 18.8 %attend_rest.1 = bf16[16,40,1152]{2,1,0:T(8,128)(2,1)} custom-call(s32[120]{0:T(128)S(1)} %concatenate.6.refs_0_, bf16[16,40,1024]{2,1,0:T(8,128)(2,1)S(1)} %bitcast.31, bf16[32,40,256]{2,1,0:T(8,128)(2,1)S(1)} %bitcast.34, bf16[32,40,256]{2,1,0:T(8,128)(2,1)S(1)} %collective-permute-done.refs_3_, s32[1,2560]{1,0:T(1,128)S(1)} %add.137.refs_4_), custom_call_target="tpu_custom_call" | custom-call | tf_op jit(solution)/shard_map/attend_rest/pallas_call | solution.py:162
  82.8 7.8 %all-to-all-start.2 = ((bf16[4,160,1152]{2,1,0:T(8,128)(2,1)}), bf16[4,160,1152]{2,1,0:T(8,128)(2,1)}, u32[]{:S(2)}, u32[]{:S(2)}) async-start(bf16[4,160,1152]{2,1,0:T(8,128)(2,1)} %bitcast.11), calls=%async_computation.2 | async-start | bytes 2949120 | tf_op jit(solution)/shard_map/all_to_all | solution.py:265
  90.6 8.7 %attend_own.1 = bf16[4,40,1152]{2,1,0:T(8,128)(2,1)S(1)} custom-call(s32[120]{0:T(128)S(1)} %concatenate.6.refs_0_, bf16[16,40,1024]{2,1,0:T(8,128)(2,1)S(1)} %bitcast.32, bf16[32,40,256]{2,1,0:T(8,128)(2,1)S(1)} %bitcast.35, bf16[32,40,256]{2,1,0:T(8,128)(2,1)S(1)} %collective-permute-done.refs_3_, s32[1,2560]{1,0:T(1,128)S(1)} %add.137.refs_4_), custom_call_target="tpu_custom_call" | custom-call | tf_op jit(solution)/shard_map/attend_own/pallas_call | solution.py:162
  99.3 0.0 copy-start
  99.3 0.7 copy-done
  100.0 10.7 %all-to-all-done.2.parts = bf16[4,160,1152]{2,1,0:T(8,128)(2,1)} async-done(((bf16[4,160,1152]{2,1,0:T(8,128)(2,1)}), bf16[4,160,1152]{2,1,0:T(8,128)(2,1)}, u32[]{:S(2)}, u32[]{:S(2)}) %all-to-all-start.2) | async-done | bytes 1474592 | tf_op jit(solution)/shard_map/all_to_all | solution.py:265
  110.7 3.4 %merge.1 = bf16[8,20,1024]{2,1,0:T(8,128)(2,1)} custom-call(s32[1]{0:T(128)} %bitcast.own_x, bf16[4,160,1152]{2,1,0:T(8,128)(2,1)} %all-to-all-done.2.parts, bf16[160,1152]{1,0:T(8,128)(2,1)} %bitcast.36), custom_call_target="tpu_custom_call" | custom-call | tf_op jit(solution)/shard_map/merge/pallas_call | solution.py:218
  114.1 17.9 %all_to_all.20 = bf16[8,20,1024]{2,1,0:T(8,128)(2,1)S(1)} all-to-all(bf16[8,20,1024]{2,1,0:T(8,128)(2,1)} %merge.1), channel_id=1, replica_groups=mesh['zl'=2,'x'=4,'y'=8,'zh'=4,'core'=2] {'zl','zh'}, dimensions={0} | all-to-all | bytes 655360 | tf_op jit(solution)/shard_map/all_to_all | solution.py:265
  132.0 0.2 copy.25
  132.2 1.0 copy.31
  (16 shorter events, 0.2 us)
Async XLA Ops:
  2.9 11.3 %copy-start.1 = (s32[128]{0:T(128)S(1)}, s32[128]{0:T(128)}, u32[]{:S(2)}) copy-start(s32[128]{0:T(128)} %param.7) | copy-start | bytes 1540
  3.9 24.4 %all-to-all-start = ((bf16[8,20,1280]{2,1,0:T(8,128)(2,1)}), bf16[8,20,1280]{2,1,0:T(8,128)(2,1)S(1)}, u32[]{:S(2)}, u32[]{:S(2)}) async-start(bf16[8,20,1280]{2,1,0:T(8,128)(2,1)} %maximum_bitcast_fusion), calls=%async_computation | async-start | bytes 983040 | tf_op jit(solution)/shard_map/all_to_all | solution.py:265
  29.7 34.2 %all-to-all-start.1 = ((bf16[4,160,1024]{2,1,0:T(8,128)(2,1)}), bf16[4,160,1024]{2,1,0:T(8,128)(2,1)S(1)}, u32[]{:S(2)}, u32[]{:S(2)}) async-start(bf16[4,160,1024]{2,1,0:T(8,128)(2,1)} %broadcast_in_dim.48), calls=%async_computation.1 | async-start | bytes 2621440 | tf_op jit(solution)/shard_map/all_to_all | solution.py:265
  59.9 4.0 %collective-permute-start = (bf16[32,40,256]{2,1,0:T(8,128)(2,1)S(1)}, bf16[32,40,256]{2,1,0:T(8,128)(2,1)S(1)}, u32[]{:S(2)}, u32[]{:S(2)}) collective-permute-start(bf16[32,40,256]{2,1,0:T(8,128)(2,1)S(1)} %bitcast.33), channel_id=1, source_target_pairs={{0,1},{1,0},{2,3},{3,2},{4,5},{5,4},{6,7},{7,6},{8,9},{9,8},{10,11... | collective-permute-start | bytes 1966088 | tf_op jit(solution)/shard_map/ppermute | solution.py:283
  82.8 28.0 %all-to-all-start.2 = ((bf16[4,160,1152]{2,1,0:T(8,128)(2,1)}), bf16[4,160,1152]{2,1,0:T(8,128)(2,1)}, u32[]{:S(2)}, u32[]{:S(2)}) async-start(bf16[4,160,1152]{2,1,0:T(8,128)(2,1)} %bitcast.11), calls=%async_computation.2 | async-start | bytes 2949120 | tf_op jit(solution)/shard_map/all_to_all | solution.py:265
  99.3 0.7 copy-start

commit v5 on v4

--- a/solution.py
+++ b/solution.py
@@ -1,3 +1,5 @@
+import functools
+
 import jax
 import jax.numpy as jnp
 from jax import lax
@@ -29,10 +31,12 @@
 
 
 def attend_kernel(
-    tiles, first_place, meta, q_ref, own_ref, other_ref, kp, out_ref, qa, ka, va, qp, sc_even,
-    sc_odd, mx, tb, acc
+    tiles, first_place, meta, q_ref, own_ref, other_ref, kp, *refs
 ):
+    out_refs = refs[: tiles // OWN_TILES]
+    out_ref, qa, ka, va, qp, sc_even, sc_odd, mx, tb, acc = refs[tiles // OWN_TILES :]
     core = meta[0]
+    own_x = meta[1]
 
     def load_block(block, carry):
         rank = meta[8 + block]
@@ -61,7 +65,7 @@
         qp[...] = jnp.concatenate([pos] * GROUP_HEADS, axis=0)
         mx[...] = hidden_row
 
-    def both(score_to, mix_from, j):
+    def both(score_to, mix_from, masked, j):
         start = pl.multiple_of(j * CHUNK, CHUNK)
         parts = [slice(part * 128, (part + 1) * 128) for part in range(CHUNK // 128)]
         keys = ka[pl.ds(start, CHUNK), :]
@@ -88,7 +92,9 @@
             top = mx[rows, :]
             query_pos = qp[rows, :]
             for part, pos in zip(parts, key_pos):
-                piece = jnp.where(pos <= query_pos, s[:, part], HIDDEN)
+                piece = s[:, part]
+                if masked:
+                    piece = jnp.where(pos <= query_pos, piece, HIDDEN)
                 score_to[j, rows, part] = piece
                 top = jnp.maximum(top, piece)
             mx[rows, :] = top
@@ -99,7 +105,8 @@
         acc[...] = jnp.zeros((ROWS, 256), jnp.float32)
 
     def close_tile(tile):
-        place = lax.rem(tile, OWN_TILES) if tiles == OWN_TILES else tile
+        shift = lax.rem(own_x + NX - tile // OWN_TILES, NX)
+        place = jnp.maximum(shift - 1, 0) * OWN_TILES + lax.rem(tile, OWN_TILES)
         total = acc[:, 128:256]
         result = acc[:, 0:128] / total
         spread = tb[...] + jnp.log2(total)
@@ -120,36 +127,32 @@
     first = meta[88 + first_place]
     open_tile(first)
 
-    def first_step(j, carry):
-        both(sc_even, None, j)
-        return carry
-
-    lax.fori_loop(0, meta[104 + first], first_step, 0)
+    def run(score_to, mix_from, clear, count):
+        def step(masked, j, carry):
+            both(score_to, mix_from, masked, j)
+            return carry
+
+        lax.fori_loop(0, clear, functools.partial(step, False), 0)
+        lax.fori_loop(clear, count, functools.partial(step, True), 0)
+
+    run(sc_even, None, meta[120 + first], meta[104 + first])
     start_mix()
-
-    if tiles == TILES - OWN_TILES:
-        own_x = meta[1]
-        out_ref[pl.ds(own_x * OWN_TILES, OWN_TILES)] = jnp.zeros(
-            (OWN_TILES, PART, WIDTH + 128), jnp.bfloat16
-        )
 
     def two_tiles(pair, carry):
         for odd in range(2):
             k = pair * 2 + odd
             tile = meta[88 + first_place + k]
-            open_tile(meta[88 + first_place + jnp.minimum(k + 1, tiles - 1)])
+            following = meta[88 + first_place + jnp.minimum(k + 1, tiles - 1)]
+            open_tile(following)
             mix_from, score_to = (sc_odd, sc_even) if odd else (sc_even, sc_odd)
-
-            def step(j, inner_carry):
-                both(score_to, mix_from, j)
-                return inner_carry
-
-            lax.fori_loop(0, meta[104 + tile], step, 0)
+            run(score_to, mix_from, meta[120 + following], meta[104 + tile])
             close_tile(tile)
             start_mix()
         return carry
 
     lax.fori_loop(0, tiles // 2, two_tiles, 0)
+    for number, target in enumerate(out_refs):
+        target[...] = out_ref[number * OWN_TILES : (number + 1) * OWN_TILES]
 
 
 def attend(mine, meta, q, own, other, key_pos):
@@ -161,15 +164,15 @@
 
     return pl.pallas_call(
         kernel,
-        out_shape=jax.ShapeDtypeStruct(
-            (OWN_TILES if mine else TILES, PART, WIDTH + 128), jnp.bfloat16
-        ),
+        out_shape=[jax.ShapeDtypeStruct((OWN_TILES, PART, WIDTH + 128), jnp.bfloat16)]
+        * (tiles // OWN_TILES),
         grid_spec=pltpu.PrefetchScalarGridSpec(
             num_scalar_prefetch=1,
             grid=(),
             in_specs=[pl.BlockSpec(memory_space=pltpu.VMEM)] * 4,
-            out_specs=pl.BlockSpec(memory_space=pltpu.VMEM),
+            out_specs=[pl.BlockSpec(memory_space=pltpu.VMEM)] * (tiles // OWN_TILES),
             scratch_shapes=[
+                pltpu.VMEM((tiles, PART, WIDTH + 128), jnp.bfloat16),
                 pltpu.VMEM((ROWS, 128), jnp.bfloat16),
                 pltpu.VMEM((KEYS, 128), jnp.bfloat16),
                 pltpu.VMEM((KEYS, 256), jnp.bfloat16),
@@ -186,14 +189,11 @@
     )(meta, q, own, other, key_pos)
 
 
-def merge_kernel(own_x, parts, mine, out_ref):
+def merge_kernel(*refs):
+    parts, out_ref = refs[:NX], refs[NX]
     levels = []
-    for x in range(NX):
-        stats = jnp.where(
-            own_x[0] == x,
-            mine[:, WIDTH : WIDTH + 128].astype(jnp.float32),
-            parts[x, :, WIDTH : WIDTH + 128].astype(jnp.float32),
-        )
+    for part in parts:
+        stats = part[:, WIDTH : WIDTH + 128].astype(jnp.float32)
         levels.append((stats + pltpu.roll(stats, 120, 1)) + pltpu.roll(stats, 112, 1))
     top = levels[0]
     for level in levels[1:]:
@@ -203,28 +203,38 @@
     for share in shares[1:]:
         total = total + share
     shares = [share / total for share in shares]
-    keep = [jnp.where(own_x[0] == x, 0.0, share) for x, share in enumerate(shares)]
-    home = sum(share - other for share, other in zip(shares, keep))
     for head in range(GROUP_HEADS):
         columns = slice(head * 128, (head + 1) * 128)
-        mixed = mine[:, columns].astype(jnp.float32) * home[:, head : head + 1]
-        for x in range(NX):
-            mixed += parts[x, :, columns].astype(jnp.float32) * keep[x][:, head : head + 1]
+        mixed = sum(
+            part[:, columns].astype(jnp.float32) * share[:, head : head + 1]
+            for part, share in zip(parts, shares)
+        )
         for z in range(NZ):
             out_ref[z, :, columns] = mixed[z * PIECE : (z + 1) * PIECE].astype(jnp.bfloat16)
 
 
-def merge(own_x, parts, mine):
+def merge(parts):
     return pl.pallas_call(
         merge_kernel,
         out_shape=jax.ShapeDtypeStruct((NZ, PIECE, WIDTH), jnp.bfloat16),
-        in_specs=[
-            pl.BlockSpec(memory_space=pltpu.SMEM),
-            pl.BlockSpec(memory_space=pltpu.VMEM),
-            pl.BlockSpec(memory_space=pltpu.VMEM),
-        ],
         name="merge",
-    )(own_x, parts, mine)
+    )(*parts)
+
+
+def pack_kernel(q_ref, k_ref, v_ref, out_ref):
+    for z in range(NZ):
+        out_ref[z, :, 0:WIDTH] = q_ref[:, z * WIDTH : (z + 1) * WIDTH]
+        columns = slice(z * HEAD_DIMENSION, (z + 1) * HEAD_DIMENSION)
+        out_ref[z, :, WIDTH : WIDTH + 128] = k_ref[:, columns]
+        out_ref[z, :, WIDTH + 128 : WIDTH + 256] = v_ref[:, columns]
+
+
+def pack(queries, keys, values):
+    return pl.pallas_call(
+        pack_kernel,
+        out_shape=jax.ShapeDtypeStruct((NZ, PIECE, WIDTH + 256), jnp.bfloat16),
+        name="pack",
+    )(queries, keys, values)
 
 
 def schedule(block_order):
@@ -240,6 +250,8 @@
     )
     seen = jnp.sum((key_block[None, :] <= query_block[:, None]).astype(jnp.int32), axis=1)
     chunks = jnp.maximum((seen * BLOCK_TOKENS + CHUNK - 1) // CHUNK, 1)
+    strict = jnp.sum((key_block[None, :] < query_block[:, None]).astype(jnp.int32), axis=1)
+    clear = strict * BLOCK_TOKENS // CHUNK
     tiles = jnp.arange(TILES, dtype=jnp.int32)
     own_x = lax.axis_index("x")
     remote = (tiles // OWN_TILES != own_x).astype(jnp.int32)
@@ -253,7 +265,7 @@
     place = (inner // PIECE) * PART + inner % PIECE + key_core * PIECE
     key_pos = in_order[:, None] * BLOCK_TOKENS + place[None, :]
     head = jnp.concatenate([core.reshape(1), own_x.reshape(1), jnp.zeros((6,), jnp.int32)])
-    meta = jnp.concatenate([head, rank, in_order, query_block, tile_at, chunks])
+    meta = jnp.concatenate([head, rank, in_order, query_block, tile_at, chunks, clear])
     return meta, key_pos.reshape(1, KEYS)
 
 
@@ -267,14 +279,7 @@
 
 def on_device(queries, keys, values, block_order):
     z_axes = ("zl", "zh")
-    packed = jnp.concatenate(
-        [
-            queries.reshape(PIECE, NZ, WIDTH),
-            keys.reshape(PIECE, NZ, HEAD_DIMENSION),
-            values.reshape(PIECE, NZ, HEAD_DIMENSION),
-        ],
-        axis=2,
-    ).transpose(1, 0, 2)
+    packed = pack(queries, keys, values)
     packed = over(packed, z_axes).reshape(TOKENS, WIDTH + 256)
     kv = packed[:, WIDTH:]
     q = over(jnp.broadcast_to(packed[None, :, :WIDTH], (NX, TOKENS, WIDTH)), "x")
@@ -283,10 +288,14 @@
     other = lax.ppermute(own, "core", ring(1, 2))
     meta, key_pos = schedule(block_order)
     q = q.reshape(TILES, PART, WIDTH)
-    parts = attend(False, meta, q, own, other, key_pos)
-    parts = over(parts.reshape(NX, TOKENS, WIDTH + 128), "x")
-    mine = attend(True, meta, q, own, other, key_pos).reshape(TOKENS, WIDTH + 128)
-    attended = over(merge(meta[1:2], parts, mine), z_axes)
+    shape = (TOKENS, WIDTH + 128)
+    rest = attend(False, meta, q, own, other, key_pos)
+    parts = [
+        lax.ppermute(rest[shift - 1].reshape(shape), "x", ring(-shift, NX)) for shift in (2, 1, 3)
+    ]
+    mine = attend(True, meta, q, own, other, key_pos)
+    parts.append(mine[0].reshape(shape))
+    attended = over(merge(parts), z_axes)
     return attended.transpose(1, 0, 2).reshape(PIECE, NZ * WIDTH)
 
 

time: 134 us -> 133 us (level)
  starting transfers between devices: 24.4 us -> 30.3 us
  waiting for transfers between devices: 25.4 us -> 20.2 us
  local copies, waits for them, and re-layouts: 6.86 us -> 4.52 us
    ppermute x0 -> x3, starting transfers between devices: none -> 13.8 us  [on_device(): lax.ppermute(rest[shift - 1].reshape(shape), 'x', ring(-shift, NX))]
    all_to_all x3 -> x2, waiting for transfers between devices: 24.2 us -> 13.3 us  [over(): return lax.all_to_all(x, axes, split_axis=0, concat_axis=0, tiled=True)]
    all_to_all x3 -> x2, starting transfers between devices: 22.4 us -> 14.6 us  [over(): return lax.all_to_all(x, axes, split_axis=0, concat_axis=0, tiled=True)]
    ppermute x0 -> x3, waiting for transfers between devices: none -> 5.21 us  [on_device(): lax.ppermute(rest[shift - 1].reshape(shape), 'x', ring(-shift, NX))]
    unnamed x9 -> x12, local copies, waits for them, and re-layouts: 4.58 us -> 2.48 us
    pallas_call x2 -> x3, Pallas kernels: 27.5 us -> 28.8 us  [the longest x2 27 us: attend(): pl.pallas_call(kernel, out_shape=[jax.ShapeDtypeStruct((OWN_TILES, PART,...]
  transfers between devices with their start and end apart: 4 -> 6, of which waited for: 3 -> 3; matrix products, arithmetic and copies ran while one was open for 1% -> 1% of each run, Pallas kernels for 7% -> 7%
where the time goes in v5:
time: 133 us
  blocking collectives  44.9 us (34%)
  Pallas kernels  31.9 us (24%)
  starting transfers between devices  30.3 us (23%)
  waiting for transfers between devices  20.2 us (15%)
  local copies, waits for them, and re-layouts  4.52 us (3%)
    pallas_call x2, Pallas kernels, attend(): pl.pallas_call(kernel, out_shape=[jax.ShapeDtypeStruct((OWN_TILES, PART,...  27 us
    all_gather x1, blocking collectives, on_device(): own = lax.all_gather(kv, 'y', axis=0, tiled=True)  25.8 us
    all_to_all x1, blocking collectives, over(): return lax.all_to_all(x, axes, split_axis=0, concat_axis=0, tiled=True)  19.1 us
    all_to_all x2, starting transfers between devices, over(): return lax.all_to_all(x, axes, split_axis=0, concat_axis=0, tiled=True)  14.6 us
    ppermute x3, starting transfers between devices, on_device(): lax.ppermute(rest[shift - 1].reshape(shape), 'x', ring(-shift, NX))  13.8 us
    all_to_all x2, waiting for transfers between devices, over(): return lax.all_to_all(x, axes, split_axis=0, concat_axis=0, tiled=True)  13.3 us
    ppermute x3, waiting for transfers between devices, on_device(): lax.ppermute(rest[shift - 1].reshape(shape), 'x', ring(-shift, NX))  5.21 us
    pallas_call x1, Pallas kernels, merge(): pl.pallas_call(merge_kernel, out_shape=jax.ShapeDtypeStruct((NZ, PIECE, W...  3.05 us
  transfers between devices with their start and end apart: 6, of which 3 were waited for; matrix products, arithmetic and copies ran while one was open for 1% of the time, Pallas kernels for 7%

profile of v5, /device:TPU:56, one launch (start us, length us, event | category | flops | bytes accessed | tf_op | source)
XLA Modules:
  0.0 132.9 jit_solution(3993204845995277622)
XLA Ops:
  0.0 0.0 copy-start.4
  0.0 1.9 %pack.1 = bf16[8,20,1280]{2,1,0:T(8,128)(2,1)} custom-call(bf16[20,8192]{1,0:T(8,128)(2,1)} %q_ref.1, bf16[20,1024]{1,0:T(8,128)(2,1)} %k_ref.1, bf16[20,1024]{1,0:T(8,128)(2,1)} %v_ref.1), custom_call_target="tpu_custom_call" | custom-call | tf_op jit(solution)/shard_map/pack/pallas_call | solution.py:233
  1.9 10.3 %all-to-all-start = ((bf16[8,20,1280]{2,1,0:T(8,128)(2,1)}), bf16[8,20,1280]{2,1,0:T(8,128)(2,1)S(1)}, u32[]{:S(2)}, u32[]{:S(2)}) async-start(bf16[8,20,1280]{2,1,0:T(8,128)(2,1)} %pack.1), calls=%async_computation | async-start | bytes 983040 | tf_op jit(solution)/shard_map/all_to_all | solution.py:277
  12.2 0.0 copy-done.4
  12.2 0.1 reshape.177
  12.4 0.1 lt.50
  12.5 0.1 reshape.178
  12.6 0.2 convert_reduce_fusion
  12.8 0.1 select_reduce_fusion
  12.9 0.1 broadcast_add_fusion
  13.0 13.3 %all-to-all-done = bf16[8,20,1280]{2,1,0:T(8,128)(2,1)S(1)} async-done(((bf16[8,20,1280]{2,1,0:T(8,128)(2,1)}), bf16[8,20,1280]{2,1,0:T(8,128)(2,1)S(1)}, u32[]{:S(2)}, u32[]{:S(2)}) %all-to-all-start) | async-done | bytes 409632 | tf_op jit(solution)/shard_map/all_to_all | solution.py:277
  26.3 0.1 reshape.179
  26.4 1.2 broadcast_in_dim.48
  27.6 4.3 %all-to-all-start.1 = ((bf16[4,160,1024]{2,1,0:T(8,128)(2,1)}), bf16[4,160,1024]{2,1,0:T(8,128)(2,1)S(1)}, u32[]{:S(2)}, u32[]{:S(2)}) async-start(bf16[4,160,1024]{2,1,0:T(8,128)(2,1)} %broadcast_in_dim.48), calls=%async_computation.1 | async-start | bytes 2621440 | tf_op jit(solution)/shard_map/all_to_all | solution.py:277
  31.9 0.2 convert_reduce_fusion.1
  32.1 0.1 add.138.refs_4_
  32.2 25.8 %all_gather.3 = bf16[1280,256]{1,0:T(8,128)(2,1)S(1)} all-gather(bf16[160,256]{1,0:T(8,128)(2,1)S(1)} %slice.9), channel_id=1, replica_groups=mesh['zl'=2,'x'=4,'y'=8,'zh'=4,'core'=2] {'y'}, dimensions={0}, use_global_device_ids=true | all-gather | bytes 737280 | tf_op jit(solution)/shard_map/all_gather | solution.py:286
  58.0 1.9 %collective-permute-start = (bf16[32,40,256]{2,1,0:T(8,128)(2,1)S(1)}, bf16[32,40,256]{2,1,0:T(8,128)(2,1)S(1)}, u32[]{:S(2)}, u32[]{:S(2)}) collective-permute-start(bf16[32,40,256]{2,1,0:T(8,128)(2,1)S(1)} %bitcast.24), channel_id=1, source_target_pairs={{0,1},{1,0},{2,3},{3,2},{4,5},{5,4},{6,7},{7,6},{8,9},{9,8},{10,11... | collective-permute-start | bytes 1966088 | tf_op jit(solution)/shard_map/ppermute | solution.py:288
  59.9 0.2 convert_reduce_fusion.2
  60.1 0.1 select_reduce_fusion.1
  60.3 0.1 concatenate.3.refs_0_
  60.3 1.6 %collective-permute-done.refs_3_ = bf16[32,40,256]{2,1,0:T(8,128)(2,1)S(1)} collective-permute-done((bf16[32,40,256]{2,1,0:T(8,128)(2,1)S(1)}, bf16[32,40,256]{2,1,0:T(8,128)(2,1)S(1)}, u32[]{:S(2)}, u32[]{:S(2)}) %collective-permute-start) | collective-permute-done | bytes 655392 | tf_op jit(solution)/shard_map/ppermute | solution.py:288
  62.0 0.0 all-to-all-done.1
  62.0 18.1 %attend_rest.1 = (bf16[4,40,1152]{2,1,0:T(8,128)(2,1)S(1)}, bf16[4,40,1152]{2,1,0:T(8,128)(2,1)S(1)}, bf16[4,40,1152]{2,1,0:T(8,128)(2,1)S(1)}) custom-call(s32[136]{0:T(256)S(1)} %concatenate.3.refs_0_, bf16[16,40,1024]{2,1,0:T(8,128)(2,1)S(1)} %bitcast.22, bf16[32,40,256]{2,1,0:T(8,128)(2,1)S(1)} %bitcast.25, ...), custom_call_target="tpu_custom_call" | custom-call | tf_op jit(solution)/shard_map/attend_rest/pallas_call | solution.py:165
  80.1 7.0 %collective-permute-start.2 = (bf16[160,1152]{1,0:T(8,128)(2,1)S(1)}, bf16[160,1152]{1,0:T(8,128)(2,1)S(1)}, u32[]{:S(2)}, u32[]{:S(2)}) collective-permute-start(bf16[160,1152]{1,0:T(8,128)(2,1)S(1)} %bitcast.30), channel_id=1, source_target_pairs={{0,192},{64,0},{128,64},{192,128},{1,193},{65,1},{129,65},{193,129... | collective-permute-start | bytes 1105928 | tf_op jit(solution)/shard_map/ppermute | solution.py:294
  87.2 3.5 %collective-permute-start.1 = (bf16[160,1152]{1,0:T(8,128)(2,1)S(1)}, bf16[160,1152]{1,0:T(8,128)(2,1)S(1)}, u32[]{:S(2)}, u32[]{:S(2)}) collective-permute-start(bf16[160,1152]{1,0:T(8,128)(2,1)S(1)} %bitcast.29), channel_id=1, source_target_pairs={{0,128},{64,192},{128,0},{192,64},{1,129},{65,193},{129,1},{193,65... | collective-permute-start | bytes 1105928 | tf_op jit(solution)/shard_map/ppermute | solution.py:294
  90.7 3.3 %collective-permute-start.3 = (bf16[160,1152]{1,0:T(8,128)(2,1)S(1)}, bf16[160,1152]{1,0:T(8,128)(2,1)S(1)}, u32[]{:S(2)}, u32[]{:S(2)}) collective-permute-start(bf16[160,1152]{1,0:T(8,128)(2,1)S(1)} %bitcast.28), channel_id=1, source_target_pairs={{0,64},{64,128},{128,192},{192,0},{1,65},{65,129},{129,193},{193,1... | collective-permute-start | bytes 1105928 | tf_op jit(solution)/shard_map/ppermute | solution.py:294
  94.0 8.9 %attend_own.1 = bf16[4,40,1152]{2,1,0:T(8,128)(2,1)S(1)} custom-call(s32[136]{0:T(256)S(1)} %concatenate.3.refs_0_, bf16[16,40,1024]{2,1,0:T(8,128)(2,1)S(1)} %bitcast.23, bf16[32,40,256]{2,1,0:T(8,128)(2,1)S(1)} %bitcast.26, bf16[32,40,256]{2,1,0:T(8,128)(2,1)S(1)} %collective-permute-done.refs_3_, s32[1,2560]{1,0:T(1,128)S(1)} %add.138.refs_4_), custom_call_target="tpu_custom_call" | custom-call | tf_op jit(solution)/shard_map/attend_own/pallas_call | solution.py:165
  102.8 0.0 copy-start
  102.9 0.7 copy-done
  103.6 0.0 collective-permute-done.2.refs_1_
  103.6 0.0 copy-start.1
  103.6 0.0 collective-permute-done.1.refs_0_
  103.6 0.0 copy-start.2
  103.6 5.2 %collective-permute-done.3.refs_2_ = bf16[160,1152]{1,0:T(8,128)(2,1)S(1)} collective-permute-done((bf16[160,1152]{1,0:T(8,128)(2,1)S(1)}, bf16[160,1152]{1,0:T(8,128)(2,1)S(1)}, u32[]{:S(2)}, u32[]{:S(2)}) %collective-permute-start.3) | collective-permute-done | bytes 368672 | tf_op jit(solution)/shard_map/ppermute | solution.py:294
  108.8 0.0 copy-start.3
  108.8 0.7 copy-done.3
  109.5 0.0 copy-done.1
  109.5 0.0 copy-done.2
  109.6 3.0 %merge.1 = bf16[8,20,1024]{2,1,0:T(8,128)(2,1)} custom-call(bf16[160,1152]{1,0:T(8,128)(2,1)} %copy-done.2, bf16[160,1152]{1,0:T(8,128)(2,1)} %copy-done.1, bf16[160,1152]{1,0:T(8,128)(2,1)} %copy-done.3, bf16[160,1152]{1,0:T(8,128)(2,1)} %bitcast.27), custom_call_target="tpu_custom_call" | custom-call | tf_op jit(solution)/shard_map/merge/pallas_call | solution.py:217
  112.6 19.1 %all_to_all.15 = bf16[8,20,1024]{2,1,0:T(8,128)(2,1)S(1)} all-to-all(bf16[8,20,1024]{2,1,0:T(8,128)(2,1)} %merge.1), channel_id=1, replica_groups=mesh['zl'=2,'x'=4,'y'=8,'zh'=4,'core'=2] {'zl','zh'}, dimensions={0} | all-to-all | bytes 655360 | tf_op jit(solution)/shard_map/all_to_all | solution.py:277
  131.7 0.2 copy.18
  131.9 1.0 copy.21
  (12 shorter events, 0.2 us)
Async XLA Ops:
  0.0 12.2 %copy-start.4 = (s32[128]{0:T(128)S(1)}, s32[128]{0:T(128)}, u32[]{:S(2)}) copy-start(s32[128]{0:T(128)} %param.7) | copy-start | bytes 1540
  1.9 24.4 %all-to-all-start = ((bf16[8,20,1280]{2,1,0:T(8,128)(2,1)}), bf16[8,20,1280]{2,1,0:T(8,128)(2,1)S(1)}, u32[]{:S(2)}, u32[]{:S(2)}) async-start(bf16[8,20,1280]{2,1,0:T(8,128)(2,1)} %pack.1), calls=%async_computation | async-start | bytes 983040 | tf_op jit(solution)/shard_map/all_to_all | solution.py:277
  27.6 34.4 %all-to-all-start.1 = ((bf16[4,160,1024]{2,1,0:T(8,128)(2,1)}), bf16[4,160,1024]{2,1,0:T(8,128)(2,1)S(1)}, u32[]{:S(2)}, u32[]{:S(2)}) async-start(bf16[4,160,1024]{2,1,0:T(8,128)(2,1)} %broadcast_in_dim.48), calls=%async_computation.1 | async-start | bytes 2621440 | tf_op jit(solution)/shard_map/all_to_all | solution.py:277
  58.0 4.0 %collective-permute-start = (bf16[32,40,256]{2,1,0:T(8,128)(2,1)S(1)}, bf16[32,40,256]{2,1,0:T(8,128)(2,1)S(1)}, u32[]{:S(2)}, u32[]{:S(2)}) collective-permute-start(bf16[32,40,256]{2,1,0:T(8,128)(2,1)S(1)} %bitcast.24), channel_id=1, source_target_pairs={{0,1},{1,0},{2,3},{3,2},{4,5},{5,4},{6,7},{7,6},{8,9},{9,8},{10,11... | collective-permute-start | bytes 1966088 | tf_op jit(solution)/shard_map/ppermute | solution.py:288
  80.1 23.4 %collective-permute-start.2 = (bf16[160,1152]{1,0:T(8,128)(2,1)S(1)}, bf16[160,1152]{1,0:T(8,128)(2,1)S(1)}, u32[]{:S(2)}, u32[]{:S(2)}) collective-permute-start(bf16[160,1152]{1,0:T(8,128)(2,1)S(1)} %bitcast.30), channel_id=1, source_target_pairs={{0,192},{64,0},{128,64},{192,128},{1,193},{65,1},{129,65},{193,129... | collective-permute-start | bytes 1105928 | tf_op jit(solution)/shard_map/ppermute | solution.py:294
  87.2 16.4 %collective-permute-start.1 = (bf16[160,1152]{1,0:T(8,128)(2,1)S(1)}, bf16[160,1152]{1,0:T(8,128)(2,1)S(1)}, u32[]{:S(2)}, u32[]{:S(2)}) collective-permute-start(bf16[160,1152]{1,0:T(8,128)(2,1)S(1)} %bitcast.29), channel_id=1, source_target_pairs={{0,128},{64,192},{128,0},{192,64},{1,129},{65,193},{129,1},{193,65... | collective-permute-start | bytes 1105928 | tf_op jit(solution)/shard_map/ppermute | solution.py:294
  90.7 18.2 %collective-permute-start.3 = (bf16[160,1152]{1,0:T(8,128)(2,1)S(1)}, bf16[160,1152]{1,0:T(8,128)(2,1)S(1)}, u32[]{:S(2)}, u32[]{:S(2)}) collective-permute-start(bf16[160,1152]{1,0:T(8,128)(2,1)S(1)} %bitcast.28), channel_id=1, source_target_pairs={{0,64},{64,128},{128,192},{192,0},{1,65},{65,129},{129,193},{193,1... | collective-permute-start | bytes 1105928 | tf_op jit(solution)/shard_map/ppermute | solution.py:294
  102.8 0.7 copy-start
  103.6 6.0 %copy-start.1 = (bf16[160,1152]{1,0:T(8,128)(2,1)}, bf16[160,1152]{1,0:T(8,128)(2,1)S(1)}, u32[]{:S(2)}) copy-start(bf16[160,1152]{1,0:T(8,128)(2,1)S(1)} %collective-permute-done.2.refs_1_) | copy-start | bytes 1105924
  103.6 6.0 %copy-start.2 = (bf16[160,1152]{1,0:T(8,128)(2,1)}, bf16[160,1152]{1,0:T(8,128)(2,1)S(1)}, u32[]{:S(2)}) copy-start(bf16[160,1152]{1,0:T(8,128)(2,1)S(1)} %collective-permute-done.1.refs_0_) | copy-start | bytes 1105924
  108.8 0.7 copy-start.3

commit v6 on v5

--- a/solution.py
+++ b/solution.py
@@ -53,7 +53,6 @@
     row = lax.broadcasted_iota(jnp.int32, (PART, 128), 0)
     row_offset = (row // PIECE) * PART + row % PIECE + core * PIECE
     lane = lax.broadcasted_iota(jnp.int32, (PART, 128), 1)
-    hidden_row = jnp.full((ROWS, 128), -3e38, jnp.float32)
 
     def open_tile(tile):
         heads = [
@@ -63,46 +62,43 @@
         qa[...] = jnp.concatenate(heads, axis=0).astype(jnp.bfloat16)
         pos = row_offset + meta[72 + tile] * BLOCK_TOKENS
         qp[...] = jnp.concatenate([pos] * GROUP_HEADS, axis=0)
-        mx[...] = hidden_row
-
-    def both(score_to, mix_from, masked, j):
-        start = pl.multiple_of(j * CHUNK, CHUNK)
-        parts = [slice(part * 128, (part + 1) * 128) for part in range(CHUNK // 128)]
-        keys = ka[pl.ds(start, CHUNK), :]
-        key_pos = [
-            kp[0:1, pl.ds(pl.multiple_of(start + part * 128, 128), 128)]
-            for part in range(CHUNK // 128)
-        ]
-        values = va[pl.ds(start, CHUNK), :]
+
+    def both(score_to, mix_from, count):
+        width = count * CHUNK
         for at in range(0, ROWS, STRIP):
             rows = slice(at, at + STRIP)
             if mix_from is not None:
                 level = tb[rows, :]
                 weights = [
-                    jnp.exp2(mix_from[j, rows, part] * SCALE - level).astype(jnp.bfloat16)
-                    for part in parts
+                    jnp.exp2(mix_from[rows, start : start + 128] * SCALE - level).astype(
+                        jnp.bfloat16
+                    )
+                    for start in range(0, width, 128)
                 ]
             s = lax.dot_general(
-                qa[rows, :], keys, (((1,), (1,)), ((), ())), preferred_element_type=jnp.float32
+                qa[rows, :],
+                ka[0:width, :],
+                (((1,), (1,)), ((), ())),
+                preferred_element_type=jnp.float32,
             )
             if mix_from is not None:
-                acc[rows, :] += jnp.dot(
-                    jnp.concatenate(weights, axis=1), values, preferred_element_type=jnp.float32
+                acc[rows, :] = jnp.dot(
+                    jnp.concatenate(weights, axis=1),
+                    va[0:width, :],
+                    preferred_element_type=jnp.float32,
                 )
-            top = mx[rows, :]
             query_pos = qp[rows, :]
-            for part, pos in zip(parts, key_pos):
-                piece = s[:, part]
-                if masked:
-                    piece = jnp.where(pos <= query_pos, piece, HIDDEN)
-                score_to[j, rows, part] = piece
-                top = jnp.maximum(top, piece)
+            top = None
+            for start in range(0, width, 128):
+                seen = kp[0:1, start : start + 128] <= query_pos
+                piece = jnp.where(seen, s[:, start : start + 128], HIDDEN)
+                score_to[rows, start : start + 128] = piece
+                top = piece if top is None else jnp.maximum(top, piece)
             mx[rows, :] = top
 
     def start_mix():
         top = jnp.max(mx[...], axis=1, keepdims=True) * SCALE
         tb[...] = jnp.broadcast_to(top, (ROWS, 128))
-        acc[...] = jnp.zeros((ROWS, 256), jnp.float32)
 
     def close_tile(tile):
         shift = lax.rem(own_x + NX - tile // OWN_TILES, NX)
@@ -127,15 +123,11 @@
     first = meta[88 + first_place]
     open_tile(first)
 
-    def run(score_to, mix_from, clear, count):
-        def step(masked, j, carry):
-            both(score_to, mix_from, masked, j)
-            return carry
-
-        lax.fori_loop(0, clear, functools.partial(step, False), 0)
-        lax.fori_loop(clear, count, functools.partial(step, True), 0)
-
-    run(sc_even, None, meta[120 + first], meta[104 + first])
+    def run(score_to, mix_from, count):
+        for number in range(1, KEYS // CHUNK + 1):
+            pl.when(count == number)(functools.partial(both, score_to, mix_from, number))
+
+    run(sc_even, None, meta[104 + first])
     start_mix()
 
     def two_tiles(pair, carry):
@@ -145,7 +137,7 @@
             following = meta[88 + first_place + jnp.minimum(k + 1, tiles - 1)]
             open_tile(following)
             mix_from, score_to = (sc_odd, sc_even) if odd else (sc_even, sc_odd)
-            run(score_to, mix_from, meta[120 + following], meta[104 + tile])
+            run(score_to, mix_from, meta[104 + tile])
             close_tile(tile)
             start_mix()
         return carry
@@ -177,8 +169,8 @@
                 pltpu.VMEM((KEYS, 128), jnp.bfloat16),
                 pltpu.VMEM((KEYS, 256), jnp.bfloat16),
                 pltpu.VMEM((ROWS, 128), jnp.int32),
-                pltpu.VMEM((KEYS // CHUNK, ROWS, CHUNK), jnp.float32),
-                pltpu.VMEM((KEYS // CHUNK, ROWS, CHUNK), jnp.float32),
+                pltpu.VMEM((ROWS, KEYS), jnp.float32),
+                pltpu.VMEM((ROWS, KEYS), jnp.float32),
                 pltpu.VMEM((ROWS, 128), jnp.float32),
                 pltpu.VMEM((ROWS, 128), jnp.float32),
                 pltpu.VMEM((ROWS, 256), jnp.float32),
@@ -250,8 +242,6 @@
     )
     seen = jnp.sum((key_block[None, :] <= query_block[:, None]).astype(jnp.int32), axis=1)
     chunks = jnp.maximum((seen * BLOCK_TOKENS + CHUNK - 1) // CHUNK, 1)
-    strict = jnp.sum((key_block[None, :] < query_block[:, None]).astype(jnp.int32), axis=1)
-    clear = strict * BLOCK_TOKENS // CHUNK
     tiles = jnp.arange(TILES, dtype=jnp.int32)
     own_x = lax.axis_index("x")
     remote = (tiles // OWN_TILES != own_x).astype(jnp.int32)
@@ -265,7 +255,7 @@
     place = (inner // PIECE) * PART + inner % PIECE + key_core * PIECE
     key_pos = in_order[:, None] * BLOCK_TOKENS + place[None, :]
     head = jnp.concatenate([core.reshape(1), own_x.reshape(1), jnp.zeros((6,), jnp.int32)])
-    meta = jnp.concatenate([head, rank, in_order, query_block, tile_at, chunks, clear])
+    meta = jnp.concatenate([head, rank, in_order, query_block, tile_at, chunks])
     return meta, key_pos.reshape(1, KEYS)
 
 

time: 133 us -> 126 us (0.947)
  Pallas kernels: 31.9 us -> 23.4 us
  waiting for transfers between devices: 20.2 us -> 23.3 us
  starting transfers between devices: 30.3 us -> 28.6 us
    pallas_call x2, Pallas kernels: 27 us -> 18.5 us  [attend(): pl.pallas_call(kernel, out_shape=[jax.ShapeDtypeStruct((OWN_TILES, PART,...]
    ppermute x3, waiting for transfers between devices: 5.21 us -> 8.55 us  [on_device(): lax.ppermute(rest[shift - 1].reshape(shape), 'x', ring(-shift, NX))]
    ppermute x3, starting transfers between devices: 13.8 us -> 12.1 us  [on_device(): lax.ppermute(rest[shift - 1].reshape(shape), 'x', ring(-shift, NX))]
  transfers between devices with their start and end apart: 6 -> 6, of which waited for: 3 -> 4; matrix products, arithmetic and copies ran while one was open for 1% -> 1% of each run, Pallas kernels for 7% -> 5%
where the time goes in v6:
time: 126 us
  blocking collectives  44.8 us (36%)
  starting transfers between devices  28.6 us (23%)
  Pallas kernels  23.4 us (19%)
  waiting for transfers between devices  23.3 us (18%)
  local copies, waits for them, and re-layouts  4.55 us (4%)
    all_gather x1, blocking collectives, on_device(): own = lax.all_gather(kv, 'y', axis=0, tiled=True)  25.8 us
    all_to_all x1, blocking collectives, over(): return lax.all_to_all(x, axes, split_axis=0, concat_axis=0, tiled=True)  19 us
    pallas_call x2, Pallas kernels, attend(): pl.pallas_call(kernel, out_shape=[jax.ShapeDtypeStruct((OWN_TILES, PART,...  18.5 us
    all_to_all x2, starting transfers between devices, over(): return lax.all_to_all(x, axes, split_axis=0, concat_axis=0, tiled=True)  14.6 us
    all_to_all x2, waiting for transfers between devices, over(): return lax.all_to_all(x, axes, split_axis=0, concat_axis=0, tiled=True)  13.5 us
    ppermute x3, starting transfers between devices, on_device(): lax.ppermute(rest[shift - 1].reshape(shape), 'x', ring(-shift, NX))  12.1 us
    ppermute x3, waiting for transfers between devices, on_device(): lax.ppermute(rest[shift - 1].reshape(shape), 'x', ring(-shift, NX))  8.55 us
    pallas_call x1, Pallas kernels, merge(): pl.pallas_call(merge_kernel, out_shape=jax.ShapeDtypeStruct((NZ, PIECE, W...  3.05 us
  transfers between devices with their start and end apart: 6, of which 4 were waited for; matrix products, arithmetic and copies ran while one was open for 1% of the time, Pallas kernels for 5%

profile of v6, /device:TPU:56, one launch (start us, length us, event | category | flops | bytes accessed | tf_op | source)
XLA Modules:
  0.0 125.8 jit_solution(18085549235603702009)
XLA Ops:
  0.0 0.0 copy-start.4
  0.0 1.9 %pack.1 = bf16[8,20,1280]{2,1,0:T(8,128)(2,1)} custom-call(bf16[20,8192]{1,0:T(8,128)(2,1)} %q_ref.1, bf16[20,1024]{1,0:T(8,128)(2,1)} %k_ref.1, bf16[20,1024]{1,0:T(8,128)(2,1)} %v_ref.1), custom_call_target="tpu_custom_call" | custom-call | tf_op jit(solution)/shard_map/pack/pallas_call | solution.py:225
  1.9 10.3 %all-to-all-start = ((bf16[8,20,1280]{2,1,0:T(8,128)(2,1)}), bf16[8,20,1280]{2,1,0:T(8,128)(2,1)S(1)}, u32[]{:S(2)}, u32[]{:S(2)}) async-start(bf16[8,20,1280]{2,1,0:T(8,128)(2,1)} %pack.1), calls=%async_computation | async-start | bytes 983040 | tf_op jit(solution)/shard_map/all_to_all | solution.py:267
  12.2 0.0 copy-done.4
  12.2 0.1 reshape.177
  12.4 0.1 lt.41
  12.5 0.2 convert_reduce_fusion
  12.7 0.1 select_reduce_fusion
  12.8 13.5 %all-to-all-done = bf16[8,20,1280]{2,1,0:T(8,128)(2,1)S(1)} async-done(((bf16[8,20,1280]{2,1,0:T(8,128)(2,1)}), bf16[8,20,1280]{2,1,0:T(8,128)(2,1)S(1)}, u32[]{:S(2)}, u32[]{:S(2)}) %all-to-all-start) | async-done | bytes 409632 | tf_op jit(solution)/shard_map/all_to_all | solution.py:267
  26.3 0.1 reshape.179
  26.4 1.2 broadcast_in_dim.48
  27.7 4.3 %all-to-all-start.1 = ((bf16[4,160,1024]{2,1,0:T(8,128)(2,1)}), bf16[4,160,1024]{2,1,0:T(8,128)(2,1)S(1)}, u32[]{:S(2)}, u32[]{:S(2)}) async-start(bf16[4,160,1024]{2,1,0:T(8,128)(2,1)} %broadcast_in_dim.48), calls=%async_computation.1 | async-start | bytes 2621440 | tf_op jit(solution)/shard_map/all_to_all | solution.py:267
  31.9 0.1 broadcast_add_fusion
  32.0 25.8 %all_gather.3 = bf16[1280,256]{1,0:T(8,128)(2,1)S(1)} all-gather(bf16[160,256]{1,0:T(8,128)(2,1)S(1)} %slice.9), channel_id=1, replica_groups=mesh['zl'=2,'x'=4,'y'=8,'zh'=4,'core'=2] {'y'}, dimensions={0}, use_global_device_ids=true | all-gather | bytes 737280 | tf_op jit(solution)/shard_map/all_gather | solution.py:276
  57.9 1.9 %collective-permute-start = (bf16[32,40,256]{2,1,0:T(8,128)(2,1)S(1)}, bf16[32,40,256]{2,1,0:T(8,128)(2,1)S(1)}, u32[]{:S(2)}, u32[]{:S(2)}) collective-permute-start(bf16[32,40,256]{2,1,0:T(8,128)(2,1)S(1)} %bitcast.24), channel_id=1, source_target_pairs={{0,1},{1,0},{2,3},{3,2},{4,5},{5,4},{6,7},{7,6},{8,9},{9,8},{10,11... | collective-permute-start | bytes 1966088 | tf_op jit(solution)/shard_map/ppermute | solution.py:278
  59.8 0.1 reshape.178
  59.9 0.1 add.137.refs_4_
  60.0 0.2 convert_reduce_fusion.2
  60.2 0.2 convert_reduce_fusion.1
  60.4 0.1 select_reduce_fusion.1
  60.5 0.1 concatenate.3.refs_0_
  60.6 1.3 %collective-permute-done.refs_3_ = bf16[32,40,256]{2,1,0:T(8,128)(2,1)S(1)} collective-permute-done((bf16[32,40,256]{2,1,0:T(8,128)(2,1)S(1)}, bf16[32,40,256]{2,1,0:T(8,128)(2,1)S(1)}, u32[]{:S(2)}, u32[]{:S(2)}) %collective-permute-start) | collective-permute-done | bytes 655392 | tf_op jit(solution)/shard_map/ppermute | solution.py:278
  61.9 0.0 all-to-all-done.1
  61.9 12.5 %attend_rest.1 = (bf16[4,40,1152]{2,1,0:T(8,128)(2,1)S(1)}, bf16[4,40,1152]{2,1,0:T(8,128)(2,1)S(1)}, bf16[4,40,1152]{2,1,0:T(8,128)(2,1)S(1)}) custom-call(s32[120]{0:T(128)S(1)} %concatenate.3.refs_0_, bf16[16,40,1024]{2,1,0:T(8,128)(2,1)S(1)} %bitcast.22, bf16[32,40,256]{2,1,0:T(8,128)(2,1)S(1)} %bitcast.25, ...), custom_call_target="tpu_custom_call" | custom-call | tf_op jit(solution)/shard_map/attend_rest/pallas_call | solution.py:157
  74.3 5.8 %collective-permute-start.2 = (bf16[160,1152]{1,0:T(8,128)(2,1)S(1)}, bf16[160,1152]{1,0:T(8,128)(2,1)S(1)}, u32[]{:S(2)}, u32[]{:S(2)}) collective-permute-start(bf16[160,1152]{1,0:T(8,128)(2,1)S(1)} %bitcast.30), channel_id=1, source_target_pairs={{0,192},{64,0},{128,64},{192,128},{1,193},{65,1},{129,65},{193,129... | collective-permute-start | bytes 1105928 | tf_op jit(solution)/shard_map/ppermute | solution.py:284
  80.2 3.0 %collective-permute-start.1 = (bf16[160,1152]{1,0:T(8,128)(2,1)S(1)}, bf16[160,1152]{1,0:T(8,128)(2,1)S(1)}, u32[]{:S(2)}, u32[]{:S(2)}) collective-permute-start(bf16[160,1152]{1,0:T(8,128)(2,1)S(1)} %bitcast.29), channel_id=1, source_target_pairs={{0,128},{64,192},{128,0},{192,64},{1,129},{65,193},{129,1},{193,65... | collective-permute-start | bytes 1105928 | tf_op jit(solution)/shard_map/ppermute | solution.py:284
  83.2 3.3 %collective-permute-start.3 = (bf16[160,1152]{1,0:T(8,128)(2,1)S(1)}, bf16[160,1152]{1,0:T(8,128)(2,1)S(1)}, u32[]{:S(2)}, u32[]{:S(2)}) collective-permute-start(bf16[160,1152]{1,0:T(8,128)(2,1)S(1)} %bitcast.28), channel_id=1, source_target_pairs={{0,64},{64,128},{128,192},{192,0},{1,65},{65,129},{129,193},{193,1... | collective-permute-start | bytes 1105928 | tf_op jit(solution)/shard_map/ppermute | solution.py:284
  86.5 6.0 %attend_own.1 = bf16[4,40,1152]{2,1,0:T(8,128)(2,1)S(1)} custom-call(s32[120]{0:T(128)S(1)} %concatenate.3.refs_0_, bf16[16,40,1024]{2,1,0:T(8,128)(2,1)S(1)} %bitcast.23, bf16[32,40,256]{2,1,0:T(8,128)(2,1)S(1)} %bitcast.26, bf16[32,40,256]{2,1,0:T(8,128)(2,1)S(1)} %collective-permute-done.refs_3_, s32[1,2560]{1,0:T(1,128)S(1)} %add.137.refs_4_), custom_call_target="tpu_custom_call" | custom-call | tf_op jit(solution)/shard_map/attend_own/pallas_call | solution.py:157
  92.5 0.0 copy-start
  92.5 0.8 copy-done
  93.3 2.9 %collective-permute-done.2.refs_1_ = bf16[160,1152]{1,0:T(8,128)(2,1)S(1)} collective-permute-done((bf16[160,1152]{1,0:T(8,128)(2,1)S(1)}, bf16[160,1152]{1,0:T(8,128)(2,1)S(1)}, u32[]{:S(2)}, u32[]{:S(2)}) %collective-permute-start.2) | collective-permute-done | bytes 368672 | tf_op jit(solution)/shard_map/ppermute | solution.py:284
  96.2 0.0 copy-start.1
  96.2 0.0 collective-permute-done.1.refs_0_
  96.2 0.0 copy-start.2
  96.2 5.6 %collective-permute-done.3.refs_2_ = bf16[160,1152]{1,0:T(8,128)(2,1)S(1)} collective-permute-done((bf16[160,1152]{1,0:T(8,128)(2,1)S(1)}, bf16[160,1152]{1,0:T(8,128)(2,1)S(1)}, u32[]{:S(2)}, u32[]{:S(2)}) %collective-permute-start.3) | collective-permute-done | bytes 368672 | tf_op jit(solution)/shard_map/ppermute | solution.py:284
  101.9 0.0 copy-start.3
  101.9 0.7 copy-done.3
  102.6 0.0 copy-done.1
  102.6 0.0 copy-done.2
  102.6 3.0 %merge.1 = bf16[8,20,1024]{2,1,0:T(8,128)(2,1)} custom-call(bf16[160,1152]{1,0:T(8,128)(2,1)} %copy-done.2, bf16[160,1152]{1,0:T(8,128)(2,1)} %copy-done.1, bf16[160,1152]{1,0:T(8,128)(2,1)} %copy-done.3, bf16[160,1152]{1,0:T(8,128)(2,1)} %bitcast.27), custom_call_target="tpu_custom_call" | custom-call | tf_op jit(solution)/shard_map/merge/pallas_call | solution.py:209
  105.6 19.0 %all_to_all.15 = bf16[8,20,1024]{2,1,0:T(8,128)(2,1)S(1)} all-to-all(bf16[8,20,1024]{2,1,0:T(8,128)(2,1)} %merge.1), channel_id=1, replica_groups=mesh['zl'=2,'x'=4,'y'=8,'zh'=4,'core'=2] {'zl','zh'}, dimensions={0} | all-to-all | bytes 655360 | tf_op jit(solution)/shard_map/all_to_all | solution.py:267
  124.6 0.2 copy.18
  124.8 1.0 copy.21
  (11 shorter events, 0.1 us)
Async XLA Ops:
  0.0 12.2 %copy-start.4 = (s32[128]{0:T(128)S(1)}, s32[128]{0:T(128)}, u32[]{:S(2)}) copy-start(s32[128]{0:T(128)} %param.7) | copy-start | bytes 1540
  1.9 24.4 %all-to-all-start = ((bf16[8,20,1280]{2,1,0:T(8,128)(2,1)}), bf16[8,20,1280]{2,1,0:T(8,128)(2,1)S(1)}, u32[]{:S(2)}, u32[]{:S(2)}) async-start(bf16[8,20,1280]{2,1,0:T(8,128)(2,1)} %pack.1), calls=%async_computation | async-start | bytes 983040 | tf_op jit(solution)/shard_map/all_to_all | solution.py:267
  27.7 34.2 %all-to-all-start.1 = ((bf16[4,160,1024]{2,1,0:T(8,128)(2,1)}), bf16[4,160,1024]{2,1,0:T(8,128)(2,1)S(1)}, u32[]{:S(2)}, u32[]{:S(2)}) async-start(bf16[4,160,1024]{2,1,0:T(8,128)(2,1)} %broadcast_in_dim.48), calls=%async_computation.1 | async-start | bytes 2621440 | tf_op jit(solution)/shard_map/all_to_all | solution.py:267
  57.9 4.0 %collective-permute-start = (bf16[32,40,256]{2,1,0:T(8,128)(2,1)S(1)}, bf16[32,40,256]{2,1,0:T(8,128)(2,1)S(1)}, u32[]{:S(2)}, u32[]{:S(2)}) collective-permute-start(bf16[32,40,256]{2,1,0:T(8,128)(2,1)S(1)} %bitcast.24), channel_id=1, source_target_pairs={{0,1},{1,0},{2,3},{3,2},{4,5},{5,4},{6,7},{7,6},{8,9},{9,8},{10,11... | collective-permute-start | bytes 1966088 | tf_op jit(solution)/shard_map/ppermute | solution.py:278
  74.3 21.9 %collective-permute-start.2 = (bf16[160,1152]{1,0:T(8,128)(2,1)S(1)}, bf16[160,1152]{1,0:T(8,128)(2,1)S(1)}, u32[]{:S(2)}, u32[]{:S(2)}) collective-permute-start(bf16[160,1152]{1,0:T(8,128)(2,1)S(1)} %bitcast.30), channel_id=1, source_target_pairs={{0,192},{64,0},{128,64},{192,128},{1,193},{65,1},{129,65},{193,129... | collective-permute-start | bytes 1105928 | tf_op jit(solution)/shard_map/ppermute | solution.py:284
  80.2 16.1 %collective-permute-start.1 = (bf16[160,1152]{1,0:T(8,128)(2,1)S(1)}, bf16[160,1152]{1,0:T(8,128)(2,1)S(1)}, u32[]{:S(2)}, u32[]{:S(2)}) collective-permute-start(bf16[160,1152]{1,0:T(8,128)(2,1)S(1)} %bitcast.29), channel_id=1, source_target_pairs={{0,128},{64,192},{128,0},{192,64},{1,129},{65,193},{129,1},{193,65... | collective-permute-start | bytes 1105928 | tf_op jit(solution)/shard_map/ppermute | solution.py:284
  83.2 18.7 %collective-permute-start.3 = (bf16[160,1152]{1,0:T(8,128)(2,1)S(1)}, bf16[160,1152]{1,0:T(8,128)(2,1)S(1)}, u32[]{:S(2)}, u32[]{:S(2)}) collective-permute-start(bf16[160,1152]{1,0:T(8,128)(2,1)S(1)} %bitcast.28), channel_id=1, source_target_pairs={{0,64},{64,128},{128,192},{192,0},{1,65},{65,129},{129,193},{193,1... | collective-permute-start | bytes 1105928 | tf_op jit(solution)/shard_map/ppermute | solution.py:284
  92.5 0.8 copy-start
  96.2 6.4 %copy-start.1 = (bf16[160,1152]{1,0:T(8,128)(2,1)}, bf16[160,1152]{1,0:T(8,128)(2,1)S(1)}, u32[]{:S(2)}) copy-start(bf16[160,1152]{1,0:T(8,128)(2,1)S(1)} %collective-permute-done.2.refs_1_) | copy-start | bytes 1105924
  96.2 6.4 %copy-start.2 = (bf16[160,1152]{1,0:T(8,128)(2,1)}, bf16[160,1152]{1,0:T(8,128)(2,1)S(1)}, u32[]{:S(2)}) copy-start(bf16[160,1152]{1,0:T(8,128)(2,1)S(1)} %collective-permute-done.1.refs_0_) | copy-start | bytes 1105924
  101.9 0.7 copy-start.3

commit v7 on v6

--- a/solution.py
+++ b/solution.py
@@ -102,7 +102,9 @@
 
     def close_tile(tile):
         shift = lax.rem(own_x + NX - tile // OWN_TILES, NX)
-        place = jnp.maximum(shift - 1, 0) * OWN_TILES + lax.rem(tile, OWN_TILES)
+        place = lax.rem(tile, OWN_TILES)
+        if tiles > OWN_TILES:
+            place += (shift // 2) * OWN_TILES
         total = acc[:, 128:256]
         result = acc[:, 0:128] / total
         spread = tb[...] + jnp.log2(total)
@@ -127,7 +129,7 @@
         for number in range(1, KEYS // CHUNK + 1):
             pl.when(count == number)(functools.partial(both, score_to, mix_from, number))
 
-    run(sc_even, None, meta[104 + first])
+    both(sc_even, None, KEYS // CHUNK)
     start_mix()
 
     def two_tiles(pair, carry):
@@ -147,10 +149,7 @@
         target[...] = out_ref[number * OWN_TILES : (number + 1) * OWN_TILES]
 
 
-def attend(mine, meta, q, own, other, key_pos):
-    tiles = OWN_TILES if mine else TILES - OWN_TILES
-    first_place = TILES - OWN_TILES if mine else 0
-
+def attend(first_place, tiles, meta, q, own, other, key_pos):
     def kernel(*refs):
         attend_kernel(tiles, first_place, *refs)
 
@@ -177,7 +176,6 @@
             ],
         ),
         compiler_params=pltpu.CompilerParams(vmem_limit_bytes=48 * 1024 * 1024),
-        name="attend_own" if mine else "attend_rest",
     )(meta, q, own, other, key_pos)
 
 
@@ -209,6 +207,8 @@
     return pl.pallas_call(
         merge_kernel,
         out_shape=jax.ShapeDtypeStruct((NZ, PIECE, WIDTH), jnp.bfloat16),
+        in_specs=[pl.BlockSpec(memory_space=pltpu.VMEM)] * NX,
+        out_specs=pl.BlockSpec(memory_space=pltpu.VMEM),
         name="merge",
     )(*parts)
 
@@ -244,8 +244,9 @@
     chunks = jnp.maximum((seen * BLOCK_TOKENS + CHUNK - 1) // CHUNK, 1)
     tiles = jnp.arange(TILES, dtype=jnp.int32)
     own_x = lax.axis_index("x")
-    remote = (tiles // OWN_TILES != own_x).astype(jnp.int32)
-    weight = (remote * 64 + chunks) * TILES + tiles
+    shift = (own_x + NX - tiles // OWN_TILES) % NX
+    turn = jnp.where(shift == 2, 2, jnp.where(shift == 0, 0, 1))
+    weight = (turn * 64 + chunks) * TILES + tiles
     place = jnp.sum((weight[None, :] > weight[:, None]).astype(jnp.int32), axis=1)
     tile_at = jnp.sum(jnp.where(place[None, :] == tiles[:, None], tiles[None, :], 0), axis=1)
     spot = jnp.arange(BLOCK_TOKENS, dtype=jnp.int32)
@@ -279,11 +280,16 @@
     meta, key_pos = schedule(block_order)
     q = q.reshape(TILES, PART, WIDTH)
     shape = (TOKENS, WIDTH + 128)
-    rest = attend(False, meta, q, own, other, key_pos)
-    parts = [
-        lax.ppermute(rest[shift - 1].reshape(shape), "x", ring(-shift, NX)) for shift in (2, 1, 3)
-    ]
-    mine = attend(True, meta, q, own, other, key_pos)
+    inputs = (meta, q, own, other, key_pos)
+
+    def send(part, shift):
+        return lax.ppermute(part.reshape(shape), "x", ring(-shift, NX))
+
+    far = attend(0, OWN_TILES, *inputs)
+    parts = [send(far[0], 2)]
+    near = attend(OWN_TILES, 2 * OWN_TILES, *inputs)
+    parts += [send(near[0], 1), send(near[1], 3)]
+    mine = attend(3 * OWN_TILES, OWN_TILES, *inputs)
     parts.append(mine[0].reshape(shape))
     attended = over(merge(parts), z_axes)
     return attended.transpose(1, 0, 2).reshape(PIECE, NZ * WIDTH)

time: 126 us -> 121 us (0.960)
  the two profiles are of different devices: /device:TPU:56 before, /device:TPU:6 now
where the time goes in v7:
time: 121 us; the launch traced here: 120 us
  blocking collectives  44.9 us (37%)
  starting transfers between devices  26.9 us (22%)
  Pallas kernels  22.8 us (19%)
  waiting for transfers between devices  19.9 us (16%)
  local copies, waits for them, and re-layouts  4.55 us (4%)
    all_gather x1, blocking collectives, on_device(): own = lax.all_gather(kv, 'y', axis=0, tiled=True)  27.5 us
    pallas_call x3, Pallas kernels, attend(): pl.pallas_call(kernel, out_shape=[jax.ShapeDtypeStruct((OWN_TILES, PART,...  17.8 us
    all_to_all x1, blocking collectives, over(): return lax.all_to_all(x, axes, split_axis=0, concat_axis=0, tiled=True)  17.4 us
    all_to_all x2, starting transfers between devices, over(): return lax.all_to_all(x, axes, split_axis=0, concat_axis=0, tiled=True)  15.1 us
    all_to_all x2, waiting for transfers between devices, over(): return lax.all_to_all(x, axes, split_axis=0, concat_axis=0, tiled=True)  13.5 us
    ppermute x3, starting transfers between devices, send(): return lax.ppermute(part.reshape(shape), 'x', ring(-shift, NX))  9.91 us
    ppermute x3, waiting for transfers between devices, send(): return lax.ppermute(part.reshape(shape), 'x', ring(-shift, NX))  5.18 us
    pallas_call x1, Pallas kernels, merge(): pl.pallas_call(merge_kernel, out_shape=jax.ShapeDtypeStruct((NZ, PIECE, W...  3.05 us
  transfers between devices with their start and end apart: 6, of which 4 were waited for; matrix products, arithmetic and copies ran while one was open for 1% of the time, Pallas kernels for 11%

profile of v7, /device:TPU:6, one launch (start us, length us, event | category | flops | bytes accessed | tf_op | source)
XLA Modules:
  0.0 120.1 jit_solution(6561894996653439325)
XLA Ops:
  0.0 0.0 copy-start.4
  0.0 1.9 %pack.1 = bf16[8,20,1280]{2,1,0:T(8,128)(2,1)} custom-call(bf16[20,8192]{1,0:T(8,128)(2,1)} %q_ref.1, bf16[20,1024]{1,0:T(8,128)(2,1)} %k_ref.1, bf16[20,1024]{1,0:T(8,128)(2,1)} %v_ref.1), custom_call_target="tpu_custom_call" | custom-call | tf_op jit(solution)/shard_map/pack/pallas_call | solution.py:225
  1.9 10.3 %all-to-all-start = ((bf16[8,20,1280]{2,1,0:T(8,128)(2,1)}), bf16[8,20,1280]{2,1,0:T(8,128)(2,1)S(1)}, u32[]{:S(2)}, u32[]{:S(2)}) async-start(bf16[8,20,1280]{2,1,0:T(8,128)(2,1)} %pack.1), calls=%async_computation | async-start | bytes 983040 | tf_op jit(solution)/shard_map/all_to_all | solution.py:268
  12.2 0.0 copy-done.4
  12.2 0.1 reshape.207
  12.4 0.1 lt.47
  12.5 0.2 convert_reduce_fusion
  12.7 0.1 select_reduce_fusion
  12.8 13.5 %all-to-all-done = bf16[8,20,1280]{2,1,0:T(8,128)(2,1)S(1)} async-done(((bf16[8,20,1280]{2,1,0:T(8,128)(2,1)}), bf16[8,20,1280]{2,1,0:T(8,128)(2,1)S(1)}, u32[]{:S(2)}, u32[]{:S(2)}) %all-to-all-start) | async-done | bytes 409632 | tf_op jit(solution)/shard_map/all_to_all | solution.py:268
  26.3 0.1 reshape.209
  26.4 1.2 %broadcast_in_dim.54 = bf16[4,160,1024]{2,1,0:T(8,128)(2,1)} broadcast(bf16[160,1024]{1,0:T(8,128)(2,1)S(1)} %slice.8), dimensions={1,2} | broadcast | bytes 1638400 | tf_op jit(solution)/shard_map/broadcast_in_dim | solution.py:276
  27.7 4.8 %all-to-all-start.1 = ((bf16[4,160,1024]{2,1,0:T(8,128)(2,1)}), bf16[4,160,1024]{2,1,0:T(8,128)(2,1)S(1)}, u32[]{:S(2)}, u32[]{:S(2)}) async-start(bf16[4,160,1024]{2,1,0:T(8,128)(2,1)} %broadcast_in_dim.54), calls=%async_computation.1 | async-start | bytes 2621440 | tf_op jit(solution)/shard_map/all_to_all | solution.py:268
  32.4 0.1 broadcast_add_fusion
  32.5 27.5 %all_gather.3 = bf16[1280,256]{1,0:T(8,128)(2,1)S(1)} all-gather(bf16[160,256]{1,0:T(8,128)(2,1)S(1)} %slice.9), channel_id=1, replica_groups=mesh['zl'=2,'x'=4,'y'=8,'zh'=4,'core'=2] {'y'}, dimensions={0}, use_global_device_ids=true | all-gather | bytes 737280 | tf_op jit(solution)/shard_map/all_gather | solution.py:277
  60.0 1.9 %collective-permute-start = (bf16[32,40,256]{2,1,0:T(8,128)(2,1)S(1)}, bf16[32,40,256]{2,1,0:T(8,128)(2,1)S(1)}, u32[]{:S(2)}, u32[]{:S(2)}) collective-permute-start(bf16[32,40,256]{2,1,0:T(8,128)(2,1)S(1)} %bitcast.25), channel_id=1, source_target_pairs={{0,1},{1,0},{2,3},{3,2},{4,5},{5,4},{6,7},{7,6},{8,9},{9,8},{10,11... | collective-permute-start | bytes 1966088 | tf_op jit(solution)/shard_map/ppermute | solution.py:279
  61.9 0.1 reshape.208
  62.0 0.1 add.153.refs_4_
  62.1 0.2 convert_reduce_fusion.2
  62.3 0.2 convert_reduce_fusion.1
  62.5 0.1 select_reduce_fusion.1
  62.6 0.1 concatenate.3.refs_0_
  62.7 1.3 %collective-permute-done.refs_3_ = bf16[32,40,256]{2,1,0:T(8,128)(2,1)S(1)} collective-permute-done((bf16[32,40,256]{2,1,0:T(8,128)(2,1)S(1)}, bf16[32,40,256]{2,1,0:T(8,128)(2,1)S(1)}, u32[]{:S(2)}, u32[]{:S(2)}) %collective-permute-start) | collective-permute-done | bytes 655392 | tf_op jit(solution)/shard_map/ppermute | solution.py:279
  64.0 0.0 all-to-all-done.1
  64.0 4.9 %shard_map.46 = bf16[4,40,1152]{2,1,0:T(8,128)(2,1)S(1)} custom-call(s32[120]{0:T(128)S(1)} %concatenate.3.refs_0_, bf16[16,40,1024]{2,1,0:T(8,128)(2,1)S(1)} %bitcast.22, bf16[32,40,256]{2,1,0:T(8,128)(2,1)S(1)} %bitcast.26, bf16[32,40,256]{2,1,0:T(8,128)(2,1)S(1)} %collective-permute-done.refs_3_, s32[1,2560]{1,0:T(1,128)S(1)} %add.153.refs_4_), custom_call_target="tpu_custom_call" | custom-call | tf_op jit(solution)/shard_map/pallas_call | solution.py:156
  68.8 3.8 %collective-permute-start.1 = (bf16[160,1152]{1,0:T(8,128)(2,1)S(1)}, bf16[160,1152]{1,0:T(8,128)(2,1)S(1)}, u32[]{:S(2)}, u32[]{:S(2)}) collective-permute-start(bf16[160,1152]{1,0:T(8,128)(2,1)S(1)} %bitcast.30), channel_id=1, source_target_pairs={{0,128},{64,192},{128,0},{192,64},{1,129},{65,193},{129,1},{193,65... | collective-permute-start | bytes 1105928 | tf_op jit(solution)/shard_map/ppermute | solution.py:286
  72.7 8.1 %shard_map.47 = (bf16[4,40,1152]{2,1,0:T(8,128)(2,1)S(1)}, bf16[4,40,1152]{2,1,0:T(8,128)(2,1)S(1)}) custom-call(s32[120]{0:T(128)S(1)} %concatenate.3.refs_0_, bf16[16,40,1024]{2,1,0:T(8,128)(2,1)S(1)} %bitcast.23, bf16[32,40,256]{2,1,0:T(8,128)(2,1)S(1)} %bitcast.27, bf16[32,40,256]{2,1,0:T(8,128)(2,1)S(1)} %collective-permute-done.refs_3_, ...), custom_call_target="tpu_custom_call" | custom-call | tf_op jit(solution)/shard_map/pallas_call | solution.py:156
  80.8 3.7 %collective-permute-start.3 = (bf16[160,1152]{1,0:T(8,128)(2,1)S(1)}, bf16[160,1152]{1,0:T(8,128)(2,1)S(1)}, u32[]{:S(2)}, u32[]{:S(2)}) collective-permute-start(bf16[160,1152]{1,0:T(8,128)(2,1)S(1)} %bitcast.32), channel_id=1, source_target_pairs={{0,64},{64,128},{128,192},{192,0},{1,65},{65,129},{129,193},{193,1... | collective-permute-start | bytes 1105928 | tf_op jit(solution)/shard_map/ppermute | solution.py:286
  84.5 2.3 %collective-permute-start.2 = (bf16[160,1152]{1,0:T(8,128)(2,1)S(1)}, bf16[160,1152]{1,0:T(8,128)(2,1)S(1)}, u32[]{:S(2)}, u32[]{:S(2)}) collective-permute-start(bf16[160,1152]{1,0:T(8,128)(2,1)S(1)} %bitcast.31), channel_id=1, source_target_pairs={{0,192},{64,0},{128,64},{192,128},{1,193},{65,1},{129,65},{193,129... | collective-permute-start | bytes 1105928 | tf_op jit(solution)/shard_map/ppermute | solution.py:286
  86.9 4.9 %shard_map.48 = bf16[4,40,1152]{2,1,0:T(8,128)(2,1)S(1)} custom-call(s32[120]{0:T(128)S(1)} %concatenate.3.refs_0_, bf16[16,40,1024]{2,1,0:T(8,128)(2,1)S(1)} %bitcast.24, bf16[32,40,256]{2,1,0:T(8,128)(2,1)S(1)} %bitcast.28, bf16[32,40,256]{2,1,0:T(8,128)(2,1)S(1)} %collective-permute-done.refs_3_, s32[1,2560]{1,0:T(1,128)S(1)} %add.153.refs_4_), custom_call_target="tpu_custom_call" | custom-call | tf_op jit(solution)/shard_map/pallas_call | solution.py:156
  91.8 0.0 copy-start
  91.8 0.8 copy-done
  92.5 0.0 collective-permute-done.1.refs_0_
  92.5 0.0 copy-start.1
  92.5 0.5 collective-permute-done.3.refs_2_
  93.0 0.0 copy-start.2
  93.0 4.7 %collective-permute-done.2.refs_1_ = bf16[160,1152]{1,0:T(8,128)(2,1)S(1)} collective-permute-done((bf16[160,1152]{1,0:T(8,128)(2,1)S(1)}, bf16[160,1152]{1,0:T(8,128)(2,1)S(1)}, u32[]{:S(2)}, u32[]{:S(2)}) %collective-permute-start.2) | collective-permute-done | bytes 368672 | tf_op jit(solution)/shard_map/ppermute | solution.py:286
  97.7 0.0 copy-start.3
  97.7 0.7 copy-done.3
  98.4 0.0 copy-done.1
  98.4 0.0 copy-done.2
  98.5 3.0 %merge.1 = bf16[8,20,1024]{2,1,0:T(8,128)(2,1)} custom-call(bf16[160,1152]{1,0:T(8,128)(2,1)} %copy-done.1, bf16[160,1152]{1,0:T(8,128)(2,1)} %copy-done.3, bf16[160,1152]{1,0:T(8,128)(2,1)} %copy-done.2, bf16[160,1152]{1,0:T(8,128)(2,1)} %bitcast.29), custom_call_target="tpu_custom_call" | custom-call | tf_op jit(solution)/shard_map/merge/pallas_call | solution.py:207
  101.5 17.4 %all_to_all.15 = bf16[8,20,1024]{2,1,0:T(8,128)(2,1)S(1)} all-to-all(bf16[8,20,1024]{2,1,0:T(8,128)(2,1)} %merge.1), channel_id=1, replica_groups=mesh['zl'=2,'x'=4,'y'=8,'zh'=4,'core'=2] {'zl','zh'}, dimensions={0} | all-to-all | bytes 655360 | tf_op jit(solution)/shard_map/all_to_all | solution.py:268
  118.9 0.2 copy.18
  119.1 1.0 copy.21
  (11 shorter events, 0.1 us)
Async XLA Ops:
  0.0 12.2 %copy-start.4 = (s32[128]{0:T(128)S(1)}, s32[128]{0:T(128)}, u32[]{:S(2)}) copy-start(s32[128]{0:T(128)} %param.7) | copy-start | bytes 1540
  1.9 24.4 %all-to-all-start = ((bf16[8,20,1280]{2,1,0:T(8,128)(2,1)}), bf16[8,20,1280]{2,1,0:T(8,128)(2,1)S(1)}, u32[]{:S(2)}, u32[]{:S(2)}) async-start(bf16[8,20,1280]{2,1,0:T(8,128)(2,1)} %pack.1), calls=%async_computation | async-start | bytes 983040 | tf_op jit(solution)/shard_map/all_to_all | solution.py:268
  27.7 36.3 %all-to-all-start.1 = ((bf16[4,160,1024]{2,1,0:T(8,128)(2,1)}), bf16[4,160,1024]{2,1,0:T(8,128)(2,1)S(1)}, u32[]{:S(2)}, u32[]{:S(2)}) async-start(bf16[4,160,1024]{2,1,0:T(8,128)(2,1)} %broadcast_in_dim.54), calls=%async_computation.1 | async-start | bytes 2621440 | tf_op jit(solution)/shard_map/all_to_all | solution.py:268
  60.0 4.0 %collective-permute-start = (bf16[32,40,256]{2,1,0:T(8,128)(2,1)S(1)}, bf16[32,40,256]{2,1,0:T(8,128)(2,1)S(1)}, u32[]{:S(2)}, u32[]{:S(2)}) collective-permute-start(bf16[32,40,256]{2,1,0:T(8,128)(2,1)S(1)} %bitcast.25), channel_id=1, source_target_pairs={{0,1},{1,0},{2,3},{3,2},{4,5},{5,4},{6,7},{7,6},{8,9},{9,8},{10,11... | collective-permute-start | bytes 1966088 | tf_op jit(solution)/shard_map/ppermute | solution.py:279
  68.8 23.7 %collective-permute-start.1 = (bf16[160,1152]{1,0:T(8,128)(2,1)S(1)}, bf16[160,1152]{1,0:T(8,128)(2,1)S(1)}, u32[]{:S(2)}, u32[]{:S(2)}) collective-permute-start(bf16[160,1152]{1,0:T(8,128)(2,1)S(1)} %bitcast.30), channel_id=1, source_target_pairs={{0,128},{64,192},{128,0},{192,64},{1,129},{65,193},{129,1},{193,65... | collective-permute-start | bytes 1105928 | tf_op jit(solution)/shard_map/ppermute | solution.py:286
  80.8 12.2 %collective-permute-start.3 = (bf16[160,1152]{1,0:T(8,128)(2,1)S(1)}, bf16[160,1152]{1,0:T(8,128)(2,1)S(1)}, u32[]{:S(2)}, u32[]{:S(2)}) collective-permute-start(bf16[160,1152]{1,0:T(8,128)(2,1)S(1)} %bitcast.32), channel_id=1, source_target_pairs={{0,64},{64,128},{128,192},{192,0},{1,65},{65,129},{129,193},{193,1... | collective-permute-start | bytes 1105928 | tf_op jit(solution)/shard_map/ppermute | solution.py:286
  84.5 13.2 %collective-permute-start.2 = (bf16[160,1152]{1,0:T(8,128)(2,1)S(1)}, bf16[160,1152]{1,0:T(8,128)(2,1)S(1)}, u32[]{:S(2)}, u32[]{:S(2)}) collective-permute-start(bf16[160,1152]{1,0:T(8,128)(2,1)S(1)} %bitcast.31), channel_id=1, source_target_pairs={{0,192},{64,0},{128,64},{192,128},{1,193},{65,1},{129,65},{193,129... | collective-permute-start | bytes 1105928 | tf_op jit(solution)/shard_map/ppermute | solution.py:286
  91.8 0.8 copy-start
  92.5 5.9 %copy-start.1 = (bf16[160,1152]{1,0:T(8,128)(2,1)}, bf16[160,1152]{1,0:T(8,128)(2,1)S(1)}, u32[]{:S(2)}) copy-start(bf16[160,1152]{1,0:T(8,128)(2,1)S(1)} %collective-permute-done.1.refs_0_) | copy-start | bytes 1105924
  93.0 5.4 %copy-start.2 = (bf16[160,1152]{1,0:T(8,128)(2,1)}, bf16[160,1152]{1,0:T(8,128)(2,1)S(1)}, u32[]{:S(2)}) copy-start(bf16[160,1152]{1,0:T(8,128)(2,1)S(1)} %collective-permute-done.3.refs_2_) | copy-start | bytes 1105924
  97.7 0.7 copy-start.3

commit v8 on v7

--- a/solution.py
+++ b/solution.py
@@ -61,7 +61,7 @@
         ]
         qa[...] = jnp.concatenate(heads, axis=0).astype(jnp.bfloat16)
         pos = row_offset + meta[72 + tile] * BLOCK_TOKENS
-        qp[...] = jnp.concatenate([pos] * GROUP_HEADS, axis=0)
+        qp[...] = pos
 
     def both(score_to, mix_from, count):
         width = count * CHUNK
@@ -87,7 +87,7 @@
                     va[0:width, :],
                     preferred_element_type=jnp.float32,
                 )
-            query_pos = qp[rows, :]
+            query_pos = jnp.concatenate([qp[...]] * (STRIP // PART), axis=0)
             top = None
             for start in range(0, width, 128):
                 seen = kp[0:1, start : start + 128] <= query_pos
@@ -107,19 +107,20 @@
             place += (shift // 2) * OWN_TILES
         total = acc[:, 128:256]
         result = acc[:, 0:128] / total
-        spread = tb[...] + jnp.log2(total)
-        stats = jnp.zeros((PART, 128), jnp.float32)
+        top = tb[...]
+        level_top = jnp.zeros((PART, 128), jnp.float32)
+        level_total = jnp.ones((PART, 128), jnp.float32)
         for head in range(GROUP_HEADS):
             rows = slice(head * PART, (head + 1) * PART)
             out_ref[place, :, head * 128 : (head + 1) * 128] = result[rows].astype(jnp.bfloat16)
-            level = spread[rows]
-            high = level.astype(jnp.bfloat16).astype(jnp.float32)
-            rest = level - high
-            middle = rest.astype(jnp.bfloat16).astype(jnp.float32)
-            low = rest - middle
-            stats = jnp.where(lane == head, high, stats)
-            stats = jnp.where(lane == 8 + head, middle, stats)
-            stats = jnp.where(lane == 16 + head, low, stats)
+            level_top = jnp.where(lane == head, top[rows], level_top)
+            level_total = jnp.where(lane == head, total[rows], level_total)
+        level = level_top + jnp.log2(level_total)
+        high = level.astype(jnp.bfloat16).astype(jnp.float32)
+        rest = level - high
+        middle = rest.astype(jnp.bfloat16).astype(jnp.float32)
+        low = rest - middle
+        stats = (high + pltpu.roll(middle, 8, 1)) + pltpu.roll(low, 16, 1)
         out_ref[place, :, WIDTH : WIDTH + 128] = stats.astype(jnp.bfloat16)
 
     first = meta[88 + first_place]
@@ -167,7 +168,7 @@
                 pltpu.VMEM((ROWS, 128), jnp.bfloat16),
                 pltpu.VMEM((KEYS, 128), jnp.bfloat16),
                 pltpu.VMEM((KEYS, 256), jnp.bfloat16),
-                pltpu.VMEM((ROWS, 128), jnp.int32),
+                pltpu.VMEM((PART, 128), jnp.int32),
                 pltpu.VMEM((ROWS, KEYS), jnp.float32),
                 pltpu.VMEM((ROWS, KEYS), jnp.float32),
                 pltpu.VMEM((ROWS, 128), jnp.float32),
@@ -192,15 +193,21 @@
     total = shares[0]
     for share in shares[1:]:
         total = total + share
-    shares = [share / total for share in shares]
-    for head in range(GROUP_HEADS):
-        columns = slice(head * 128, (head + 1) * 128)
-        mixed = sum(
-            part[:, columns].astype(jnp.float32) * share[:, head : head + 1]
-            for part, share in zip(parts, shares)
+    row = lax.broadcasted_iota(jnp.int32, (256, WIDTH), 0)
+    column = lax.broadcasted_iota(jnp.int32, (256, WIDTH), 1)
+    lift = jnp.where(row % 128 == column // 128, 1.0, 0.0).astype(jnp.bfloat16)
+    mixed = None
+    for part, share in zip(parts, shares):
+        share = share / total
+        high = share.astype(jnp.bfloat16)
+        low = (share - high.astype(jnp.float32)).astype(jnp.bfloat16)
+        wide = jnp.dot(
+            jnp.concatenate([high, low], axis=1), lift, preferred_element_type=jnp.float32
         )
-        for z in range(NZ):
-            out_ref[z, :, columns] = mixed[z * PIECE : (z + 1) * PIECE].astype(jnp.bfloat16)
+        term = part[:, 0:WIDTH].astype(jnp.float32) * wide
+        mixed = term if mixed is None else mixed + term
+    for z in range(NZ):
+        out_ref[z] = mixed[z * PIECE : (z + 1) * PIECE].astype(jnp.bfloat16)
 
 
 def merge(parts):

time: 121 us -> 121 us (level)
  no operation moved by 1% of the time
where the time goes in v8:
time: 121 us; the launch traced here: 120 us
  blocking collectives  44.9 us (37%)
  starting transfers between devices  26.9 us (22%)
  Pallas kernels  23.4 us (19%)
  waiting for transfers between devices  19.7 us (16%)
  local copies, waits for them, and re-layouts  4.55 us (4%)
    all_gather x1, blocking collectives, on_device(): own = lax.all_gather(kv, 'y', axis=0, tiled=True)  27.5 us
    pallas_call x3, Pallas kernels, attend(): pl.pallas_call(kernel, out_shape=[jax.ShapeDtypeStruct((OWN_TILES, PART,...  18.8 us
    all_to_all x1, blocking collectives, over(): return lax.all_to_all(x, axes, split_axis=0, concat_axis=0, tiled=True)  17.4 us
    all_to_all x2, starting transfers between devices, over(): return lax.all_to_all(x, axes, split_axis=0, concat_axis=0, tiled=True)  15.1 us
    all_to_all x2, waiting for transfers between devices, over(): return lax.all_to_all(x, axes, split_axis=0, concat_axis=0, tiled=True)  13.5 us
    ppermute x3, starting transfers between devices, send(): return lax.ppermute(part.reshape(shape), 'x', ring(-shift, NX))  9.9 us
    ppermute x3, waiting for transfers between devices, send(): return lax.ppermute(part.reshape(shape), 'x', ring(-shift, NX))  4.95 us
    pallas_call x1, Pallas kernels, merge(): pl.pallas_call(merge_kernel, out_shape=jax.ShapeDtypeStruct((NZ, PIECE, W...  2.73 us
  transfers between devices with their start and end apart: 6, of which 4 were waited for; matrix products, arithmetic and copies ran while one was open for 1% of the time, Pallas kernels for 11%

profile of v8, /device:TPU:6, one launch (start us, length us, event | category | flops | bytes accessed | tf_op | source)
XLA Modules:
  0.0 120.5 jit_solution(1879401791756357422)
XLA Ops:
  0.0 0.0 copy-start.4
  0.0 1.9 %pack.1 = bf16[8,20,1280]{2,1,0:T(8,128)(2,1)} custom-call(bf16[20,8192]{1,0:T(8,128)(2,1)} %q_ref.1, bf16[20,1024]{1,0:T(8,128)(2,1)} %k_ref.1, bf16[20,1024]{1,0:T(8,128)(2,1)} %v_ref.1), custom_call_target="tpu_custom_call" | custom-call | tf_op jit(solution)/shard_map/pack/pallas_call | solution.py:232
  1.9 10.3 %all-to-all-start = ((bf16[8,20,1280]{2,1,0:T(8,128)(2,1)}), bf16[8,20,1280]{2,1,0:T(8,128)(2,1)S(1)}, u32[]{:S(2)}, u32[]{:S(2)}) async-start(bf16[8,20,1280]{2,1,0:T(8,128)(2,1)} %pack.1), calls=%async_computation | async-start | bytes 983040 | tf_op jit(solution)/shard_map/all_to_all | solution.py:275
  12.2 0.0 copy-done.4
  12.2 0.1 reshape.207
  12.4 0.1 lt.47
  12.5 0.2 convert_reduce_fusion
  12.7 0.1 select_reduce_fusion
  12.8 13.5 %all-to-all-done = bf16[8,20,1280]{2,1,0:T(8,128)(2,1)S(1)} async-done(((bf16[8,20,1280]{2,1,0:T(8,128)(2,1)}), bf16[8,20,1280]{2,1,0:T(8,128)(2,1)S(1)}, u32[]{:S(2)}, u32[]{:S(2)}) %all-to-all-start) | async-done | bytes 409632 | tf_op jit(solution)/shard_map/all_to_all | solution.py:275
  26.3 0.1 reshape.209
  26.4 1.2 %broadcast_in_dim.54 = bf16[4,160,1024]{2,1,0:T(8,128)(2,1)} broadcast(bf16[160,1024]{1,0:T(8,128)(2,1)S(1)} %slice.8), dimensions={1,2} | broadcast | bytes 1638400 | tf_op jit(solution)/shard_map/broadcast_in_dim | solution.py:283
  27.7 4.8 %all-to-all-start.1 = ((bf16[4,160,1024]{2,1,0:T(8,128)(2,1)}), bf16[4,160,1024]{2,1,0:T(8,128)(2,1)S(1)}, u32[]{:S(2)}, u32[]{:S(2)}) async-start(bf16[4,160,1024]{2,1,0:T(8,128)(2,1)} %broadcast_in_dim.54), calls=%async_computation.1 | async-start | bytes 2621440 | tf_op jit(solution)/shard_map/all_to_all | solution.py:275
  32.4 0.1 broadcast_add_fusion
  32.5 27.5 %all_gather.3 = bf16[1280,256]{1,0:T(8,128)(2,1)S(1)} all-gather(bf16[160,256]{1,0:T(8,128)(2,1)S(1)} %slice.9), channel_id=1, replica_groups=mesh['zl'=2,'x'=4,'y'=8,'zh'=4,'core'=2] {'y'}, dimensions={0}, use_global_device_ids=true | all-gather | bytes 737280 | tf_op jit(solution)/shard_map/all_gather | solution.py:284
  60.0 1.9 %collective-permute-start = (bf16[32,40,256]{2,1,0:T(8,128)(2,1)S(1)}, bf16[32,40,256]{2,1,0:T(8,128)(2,1)S(1)}, u32[]{:S(2)}, u32[]{:S(2)}) collective-permute-start(bf16[32,40,256]{2,1,0:T(8,128)(2,1)S(1)} %bitcast.25), channel_id=1, source_target_pairs={{0,1},{1,0},{2,3},{3,2},{4,5},{5,4},{6,7},{7,6},{8,9},{9,8},{10,11... | collective-permute-start | bytes 1966088 | tf_op jit(solution)/shard_map/ppermute | solution.py:286
  61.9 0.1 reshape.208
  62.0 0.1 add.153.refs_4_
  62.1 0.2 convert_reduce_fusion.2
  62.3 0.2 convert_reduce_fusion.1
  62.5 0.1 select_reduce_fusion.1
  62.6 0.1 concatenate.3.refs_0_
  62.7 1.3 %collective-permute-done.refs_3_ = bf16[32,40,256]{2,1,0:T(8,128)(2,1)S(1)} collective-permute-done((bf16[32,40,256]{2,1,0:T(8,128)(2,1)S(1)}, bf16[32,40,256]{2,1,0:T(8,128)(2,1)S(1)}, u32[]{:S(2)}, u32[]{:S(2)}) %collective-permute-start) | collective-permute-done | bytes 655392 | tf_op jit(solution)/shard_map/ppermute | solution.py:286
  64.0 0.0 all-to-all-done.1
  64.0 5.1 %shard_map.46 = bf16[4,40,1152]{2,1,0:T(8,128)(2,1)S(1)} custom-call(s32[120]{0:T(128)S(1)} %concatenate.3.refs_0_, bf16[16,40,1024]{2,1,0:T(8,128)(2,1)S(1)} %bitcast.22, bf16[32,40,256]{2,1,0:T(8,128)(2,1)S(1)} %bitcast.26, bf16[32,40,256]{2,1,0:T(8,128)(2,1)S(1)} %collective-permute-done.refs_3_, s32[1,2560]{1,0:T(1,128)S(1)} %add.153.refs_4_), custom_call_target="tpu_custom_call" | custom-call | tf_op jit(solution)/shard_map/pallas_call | solution.py:157
  69.1 3.8 %collective-permute-start.1 = (bf16[160,1152]{1,0:T(8,128)(2,1)S(1)}, bf16[160,1152]{1,0:T(8,128)(2,1)S(1)}, u32[]{:S(2)}, u32[]{:S(2)}) collective-permute-start(bf16[160,1152]{1,0:T(8,128)(2,1)S(1)} %bitcast.30), channel_id=1, source_target_pairs={{0,128},{64,192},{128,0},{192,64},{1,129},{65,193},{129,1},{193,65... | collective-permute-start | bytes 1105928 | tf_op jit(solution)/shard_map/ppermute | solution.py:293
  72.9 8.6 %shard_map.47 = (bf16[4,40,1152]{2,1,0:T(8,128)(2,1)S(1)}, bf16[4,40,1152]{2,1,0:T(8,128)(2,1)S(1)}) custom-call(s32[120]{0:T(128)S(1)} %concatenate.3.refs_0_, bf16[16,40,1024]{2,1,0:T(8,128)(2,1)S(1)} %bitcast.23, bf16[32,40,256]{2,1,0:T(8,128)(2,1)S(1)} %bitcast.27, bf16[32,40,256]{2,1,0:T(8,128)(2,1)S(1)} %collective-permute-done.refs_3_, ...), custom_call_target="tpu_custom_call" | custom-call | tf_op jit(solution)/shard_map/pallas_call | solution.py:157
  81.5 3.7 %collective-permute-start.3 = (bf16[160,1152]{1,0:T(8,128)(2,1)S(1)}, bf16[160,1152]{1,0:T(8,128)(2,1)S(1)}, u32[]{:S(2)}, u32[]{:S(2)}) collective-permute-start(bf16[160,1152]{1,0:T(8,128)(2,1)S(1)} %bitcast.32), channel_id=1, source_target_pairs={{0,64},{64,128},{128,192},{192,0},{1,65},{65,129},{129,193},{193,1... | collective-permute-start | bytes 1105928 | tf_op jit(solution)/shard_map/ppermute | solution.py:293
  85.2 2.3 %collective-permute-start.2 = (bf16[160,1152]{1,0:T(8,128)(2,1)S(1)}, bf16[160,1152]{1,0:T(8,128)(2,1)S(1)}, u32[]{:S(2)}, u32[]{:S(2)}) collective-permute-start(bf16[160,1152]{1,0:T(8,128)(2,1)S(1)} %bitcast.31), channel_id=1, source_target_pairs={{0,192},{64,0},{128,64},{192,128},{1,193},{65,1},{129,65},{193,129... | collective-permute-start | bytes 1105928 | tf_op jit(solution)/shard_map/ppermute | solution.py:293
  87.6 5.1 %shard_map.48 = bf16[4,40,1152]{2,1,0:T(8,128)(2,1)S(1)} custom-call(s32[120]{0:T(128)S(1)} %concatenate.3.refs_0_, bf16[16,40,1024]{2,1,0:T(8,128)(2,1)S(1)} %bitcast.24, bf16[32,40,256]{2,1,0:T(8,128)(2,1)S(1)} %bitcast.28, bf16[32,40,256]{2,1,0:T(8,128)(2,1)S(1)} %collective-permute-done.refs_3_, s32[1,2560]{1,0:T(1,128)S(1)} %add.153.refs_4_), custom_call_target="tpu_custom_call" | custom-call | tf_op jit(solution)/shard_map/pallas_call | solution.py:157
  92.7 0.0 copy-start
  92.7 0.8 copy-done
  93.4 0.0 collective-permute-done.1.refs_0_
  93.4 0.0 copy-start.1
  93.4 0.3 collective-permute-done.3.refs_2_
  93.7 0.0 copy-start.2
  93.7 4.7 %collective-permute-done.2.refs_1_ = bf16[160,1152]{1,0:T(8,128)(2,1)S(1)} collective-permute-done((bf16[160,1152]{1,0:T(8,128)(2,1)S(1)}, bf16[160,1152]{1,0:T(8,128)(2,1)S(1)}, u32[]{:S(2)}, u32[]{:S(2)}) %collective-permute-start.2) | collective-permute-done | bytes 368672 | tf_op jit(solution)/shard_map/ppermute | solution.py:293
  98.4 0.0 copy-start.3
  98.4 0.7 copy-done.3
  99.1 0.0 copy-done.1
  99.1 0.0 copy-done.2
  99.1 2.7 %merge.1 = bf16[8,20,1024]{2,1,0:T(8,128)(2,1)} custom-call(bf16[160,1152]{1,0:T(8,128)(2,1)} %copy-done.1, bf16[160,1152]{1,0:T(8,128)(2,1)} %copy-done.3, bf16[160,1152]{1,0:T(8,128)(2,1)} %copy-done.2, bf16[160,1152]{1,0:T(8,128)(2,1)} %bitcast.29), custom_call_target="tpu_custom_call" | custom-call | tf_op jit(solution)/shard_map/merge/pallas_call | solution.py:214
  101.9 17.4 %all_to_all.15 = bf16[8,20,1024]{2,1,0:T(8,128)(2,1)S(1)} all-to-all(bf16[8,20,1024]{2,1,0:T(8,128)(2,1)} %merge.1), channel_id=1, replica_groups=mesh['zl'=2,'x'=4,'y'=8,'zh'=4,'core'=2] {'zl','zh'}, dimensions={0} | all-to-all | bytes 655360 | tf_op jit(solution)/shard_map/all_to_all | solution.py:275
  119.3 0.2 copy.18
  119.5 1.0 copy.21
  (11 shorter events, 0.1 us)
Async XLA Ops:
  0.0 12.2 %copy-start.4 = (s32[128]{0:T(128)S(1)}, s32[128]{0:T(128)}, u32[]{:S(2)}) copy-start(s32[128]{0:T(128)} %param.7) | copy-start | bytes 1540
  1.9 24.4 %all-to-all-start = ((bf16[8,20,1280]{2,1,0:T(8,128)(2,1)}), bf16[8,20,1280]{2,1,0:T(8,128)(2,1)S(1)}, u32[]{:S(2)}, u32[]{:S(2)}) async-start(bf16[8,20,1280]{2,1,0:T(8,128)(2,1)} %pack.1), calls=%async_computation | async-start | bytes 983040 | tf_op jit(solution)/shard_map/all_to_all | solution.py:275
  27.7 36.3 %all-to-all-start.1 = ((bf16[4,160,1024]{2,1,0:T(8,128)(2,1)}), bf16[4,160,1024]{2,1,0:T(8,128)(2,1)S(1)}, u32[]{:S(2)}, u32[]{:S(2)}) async-start(bf16[4,160,1024]{2,1,0:T(8,128)(2,1)} %broadcast_in_dim.54), calls=%async_computation.1 | async-start | bytes 2621440 | tf_op jit(solution)/shard_map/all_to_all | solution.py:275
  60.0 4.0 %collective-permute-start = (bf16[32,40,256]{2,1,0:T(8,128)(2,1)S(1)}, bf16[32,40,256]{2,1,0:T(8,128)(2,1)S(1)}, u32[]{:S(2)}, u32[]{:S(2)}) collective-permute-start(bf16[32,40,256]{2,1,0:T(8,128)(2,1)S(1)} %bitcast.25), channel_id=1, source_target_pairs={{0,1},{1,0},{2,3},{3,2},{4,5},{5,4},{6,7},{7,6},{8,9},{9,8},{10,11... | collective-permute-start | bytes 1966088 | tf_op jit(solution)/shard_map/ppermute | solution.py:286
  69.1 24.4 %collective-permute-start.1 = (bf16[160,1152]{1,0:T(8,128)(2,1)S(1)}, bf16[160,1152]{1,0:T(8,128)(2,1)S(1)}, u32[]{:S(2)}, u32[]{:S(2)}) collective-permute-start(bf16[160,1152]{1,0:T(8,128)(2,1)S(1)} %bitcast.30), channel_id=1, source_target_pairs={{0,128},{64,192},{128,0},{192,64},{1,129},{65,193},{129,1},{193,65... | collective-permute-start | bytes 1105928 | tf_op jit(solution)/shard_map/ppermute | solution.py:293
  81.5 12.2 %collective-permute-start.3 = (bf16[160,1152]{1,0:T(8,128)(2,1)S(1)}, bf16[160,1152]{1,0:T(8,128)(2,1)S(1)}, u32[]{:S(2)}, u32[]{:S(2)}) collective-permute-start(bf16[160,1152]{1,0:T(8,128)(2,1)S(1)} %bitcast.32), channel_id=1, source_target_pairs={{0,64},{64,128},{128,192},{192,0},{1,65},{65,129},{129,193},{193,1... | collective-permute-start | bytes 1105928 | tf_op jit(solution)/shard_map/ppermute | solution.py:293
  85.2 13.2 %collective-permute-start.2 = (bf16[160,1152]{1,0:T(8,128)(2,1)S(1)}, bf16[160,1152]{1,0:T(8,128)(2,1)S(1)}, u32[]{:S(2)}, u32[]{:S(2)}) collective-permute-start(bf16[160,1152]{1,0:T(8,128)(2,1)S(1)} %bitcast.31), channel_id=1, source_target_pairs={{0,192},{64,0},{128,64},{192,128},{1,193},{65,1},{129,65},{193,129... | collective-permute-start | bytes 1105928 | tf_op jit(solution)/shard_map/ppermute | solution.py:293
  92.7 0.8 copy-start
  93.4 5.7 %copy-start.1 = (bf16[160,1152]{1,0:T(8,128)(2,1)}, bf16[160,1152]{1,0:T(8,128)(2,1)S(1)}, u32[]{:S(2)}) copy-start(bf16[160,1152]{1,0:T(8,128)(2,1)S(1)} %collective-permute-done.1.refs_0_) | copy-start | bytes 1105924
  93.7 5.4 %copy-start.2 = (bf16[160,1152]{1,0:T(8,128)(2,1)}, bf16[160,1152]{1,0:T(8,128)(2,1)S(1)}, u32[]{:S(2)}) copy-start(bf16[160,1152]{1,0:T(8,128)(2,1)S(1)} %collective-permute-done.3.refs_2_) | copy-start | bytes 1105924
  98.4 0.7 copy-start.3

commit v9 on v8

--- a/solution.py
+++ b/solution.py
@@ -34,7 +34,12 @@
     tiles, first_place, meta, q_ref, own_ref, other_ref, kp, *refs
 ):
     out_refs = refs[: tiles // OWN_TILES]
-    out_ref, qa, ka, va, qp, sc_even, sc_odd, mx, tb, acc = refs[tiles // OWN_TILES :]
+    refs = refs[tiles // OWN_TILES :]
+    if first_place == 0:
+        ka, va, *refs = refs
+    else:
+        ka, va = own_ref, other_ref
+    out_ref, qa, qp, sc_even, sc_odd, mx, tb, acc = refs
     core = meta[0]
     own_x = meta[1]
 
@@ -48,8 +53,9 @@
         va[pl.ds(start, BLOCK_TOKENS), 0:128] = both[:, 128:256]
         return carry
 
-    lax.fori_loop(0, NB, load_block, 0, unroll=4)
-    va[:, 128:256] = jnp.ones((KEYS, 128), jnp.bfloat16)
+    if first_place == 0:
+        lax.fori_loop(0, NB, load_block, 0, unroll=4)
+        va[:, 128:256] = jnp.ones((KEYS, 128), jnp.bfloat16)
     row = lax.broadcasted_iota(jnp.int32, (PART, 128), 0)
     row_offset = (row // PIECE) * PART + row % PIECE + core * PIECE
     lane = lax.broadcasted_iota(jnp.int32, (PART, 128), 1)
@@ -151,23 +157,25 @@
 
 
 def attend(first_place, tiles, meta, q, own, other, key_pos):
+    part = jax.ShapeDtypeStruct((OWN_TILES, PART, WIDTH + 128), jnp.bfloat16)
+    shapes = [part] * (tiles // OWN_TILES)
+    if first_place == 0:
+        shapes += [jax.ShapeDtypeStruct((KEYS, width), jnp.bfloat16) for width in (128, 256)]
+
     def kernel(*refs):
         attend_kernel(tiles, first_place, *refs)
 
     return pl.pallas_call(
         kernel,
-        out_shape=[jax.ShapeDtypeStruct((OWN_TILES, PART, WIDTH + 128), jnp.bfloat16)]
-        * (tiles // OWN_TILES),
+        out_shape=shapes,
         grid_spec=pltpu.PrefetchScalarGridSpec(
             num_scalar_prefetch=1,
             grid=(),
             in_specs=[pl.BlockSpec(memory_space=pltpu.VMEM)] * 4,
-            out_specs=[pl.BlockSpec(memory_space=pltpu.VMEM)] * (tiles // OWN_TILES),
+            out_specs=[pl.BlockSpec(memory_space=pltpu.VMEM)] * len(shapes),
             scratch_shapes=[
                 pltpu.VMEM((tiles, PART, WIDTH + 128), jnp.bfloat16),
                 pltpu.VMEM((ROWS, 128), jnp.bfloat16),
-                pltpu.VMEM((KEYS, 128), jnp.bfloat16),
-                pltpu.VMEM((KEYS, 256), jnp.bfloat16),
                 pltpu.VMEM((PART, 128), jnp.int32),
                 pltpu.VMEM((ROWS, KEYS), jnp.float32),
                 pltpu.VMEM((ROWS, KEYS), jnp.float32),
@@ -287,12 +295,12 @@
     meta, key_pos = schedule(block_order)
     q = q.reshape(TILES, PART, WIDTH)
     shape = (TOKENS, WIDTH + 128)
-    inputs = (meta, q, own, other, key_pos)
 
     def send(part, shift):
         return lax.ppermute(part.reshape(shape), "x", ring(-shift, NX))
 
-    far = attend(0, OWN_TILES, *inputs)
+    far = attend(0, OWN_TILES, meta, q, own, other, key_pos)
+    inputs = (meta, q, far[1], far[2], key_pos)
     parts = [send(far[0], 2)]
     near = attend(OWN_TILES, 2 * OWN_TILES, *inputs)
     parts += [send(near[0], 1), send(near[1], 3)]

time: 121 us -> 126 us (1.041)
  waiting for transfers between devices: 19.7 us -> 23.1 us
    ppermute x3, waiting for transfers between devices: 4.95 us -> 8.38 us  [send(): return lax.ppermute(part.reshape(shape), 'x', ring(-shift, NX))]
    pallas_call x3, Pallas kernels: 18.8 us -> 20 us  [attend(): pl.pallas_call(kernel, out_shape=shapes, grid_spec=pltpu.PrefetchScalarGr...]
  transfers between devices with their start and end apart: 6 -> 6, of which waited for: 4 -> 4; matrix products, arithmetic and copies ran while one was open for 1% -> 1% of each run, Pallas kernels for 11% -> 4%
where the time goes in v9:
time: 126 us; the launch traced here: 125 us
  blocking collectives  45.5 us (36%)
  starting transfers between devices  26.4 us (21%)
  Pallas kernels  24.6 us (20%)
  waiting for transfers between devices  23.1 us (18%)
  local copies, waits for them, and re-layouts  4.53 us (4%)
    all_gather x1, blocking collectives, on_device(): own = lax.all_gather(kv, 'y', axis=0, tiled=True)  27.5 us
    pallas_call x3, Pallas kernels, attend(): pl.pallas_call(kernel, out_shape=shapes, grid_spec=pltpu.PrefetchScalarGr...  20 us
    all_to_all x1, blocking collectives, over(): return lax.all_to_all(x, axes, split_axis=0, concat_axis=0, tiled=True)  18 us
    all_to_all x2, starting transfers between devices, over(): return lax.all_to_all(x, axes, split_axis=0, concat_axis=0, tiled=True)  15.1 us
    all_to_all x2, waiting for transfers between devices, over(): return lax.all_to_all(x, axes, split_axis=0, concat_axis=0, tiled=True)  13.5 us
    ppermute x3, starting transfers between devices, send(): return lax.ppermute(part.reshape(shape), 'x', ring(-shift, NX))  9.36 us
    ppermute x3, waiting for transfers between devices, send(): return lax.ppermute(part.reshape(shape), 'x', ring(-shift, NX))  8.38 us
    pallas_call x1, Pallas kernels, merge(): pl.pallas_call(merge_kernel, out_shape=jax.ShapeDtypeStruct((NZ, PIECE, W...  2.75 us
  transfers between devices with their start and end apart: 6, of which 4 were waited for; matrix products, arithmetic and copies ran while one was open for 1% of the time, Pallas kernels for 4%

profile of v9, /device:TPU:6, one launch (start us, length us, event | category | flops | bytes accessed | tf_op | source)
XLA Modules:
  0.0 125.2 jit_solution(16048046343737579091)
XLA Ops:
  0.0 0.0 copy-start.4
  0.0 1.9 %pack.1 = bf16[8,20,1280]{2,1,0:T(8,128)(2,1)} custom-call(bf16[20,8192]{1,0:T(8,128)(2,1)} %q_ref.1, bf16[20,1024]{1,0:T(8,128)(2,1)} %k_ref.1, bf16[20,1024]{1,0:T(8,128)(2,1)} %v_ref.1), custom_call_target="tpu_custom_call" | custom-call | tf_op jit(solution)/shard_map/pack/pallas_call | solution.py:240
  1.9 10.3 %all-to-all-start = ((bf16[8,20,1280]{2,1,0:T(8,128)(2,1)}), bf16[8,20,1280]{2,1,0:T(8,128)(2,1)S(1)}, u32[]{:S(2)}, u32[]{:S(2)}) async-start(bf16[8,20,1280]{2,1,0:T(8,128)(2,1)} %pack.1), calls=%async_computation | async-start | bytes 983040 | tf_op jit(solution)/shard_map/all_to_all | solution.py:283
  12.2 0.0 copy-done.4
  12.2 0.1 reshape.207
  12.4 0.1 lt.47
  12.5 0.2 convert_reduce_fusion
  12.7 0.1 select_reduce_fusion
  12.8 13.5 %all-to-all-done = bf16[8,20,1280]{2,1,0:T(8,128)(2,1)S(1)} async-done(((bf16[8,20,1280]{2,1,0:T(8,128)(2,1)}), bf16[8,20,1280]{2,1,0:T(8,128)(2,1)S(1)}, u32[]{:S(2)}, u32[]{:S(2)}) %all-to-all-start) | async-done | bytes 409632 | tf_op jit(solution)/shard_map/all_to_all | solution.py:283
  26.3 0.1 reshape.209
  26.4 1.2 broadcast_in_dim.54
  27.6 4.8 %all-to-all-start.1 = ((bf16[4,160,1024]{2,1,0:T(8,128)(2,1)}), bf16[4,160,1024]{2,1,0:T(8,128)(2,1)S(1)}, u32[]{:S(2)}, u32[]{:S(2)}) async-start(bf16[4,160,1024]{2,1,0:T(8,128)(2,1)} %broadcast_in_dim.54), calls=%async_computation.1 | async-start | bytes 2621440 | tf_op jit(solution)/shard_map/all_to_all | solution.py:283
  32.4 0.1 broadcast_add_fusion
  32.5 27.5 %all_gather.3 = bf16[1280,256]{1,0:T(8,128)(2,1)S(1)} all-gather(bf16[160,256]{1,0:T(8,128)(2,1)S(1)} %slice.9), channel_id=1, replica_groups=mesh['zl'=2,'x'=4,'y'=8,'zh'=4,'core'=2] {'y'}, dimensions={0}, use_global_device_ids=true | all-gather | bytes 737280 | tf_op jit(solution)/shard_map/all_gather | solution.py:292
  60.0 1.9 %collective-permute-start = (bf16[32,40,256]{2,1,0:T(8,128)(2,1)S(1)}, bf16[32,40,256]{2,1,0:T(8,128)(2,1)S(1)}, u32[]{:S(2)}, u32[]{:S(2)}) collective-permute-start(bf16[32,40,256]{2,1,0:T(8,128)(2,1)S(1)} %bitcast.25), channel_id=1, source_target_pairs={{0,1},{1,0},{2,3},{3,2},{4,5},{5,4},{6,7},{7,6},{8,9},{9,8},{10,11... | collective-permute-start | bytes 1966088 | tf_op jit(solution)/shard_map/ppermute | solution.py:294
  61.9 0.1 reshape.208
  62.0 0.1 add.153.refs_4_
  62.1 0.2 convert_reduce_fusion.2
  62.3 0.2 convert_reduce_fusion.1
  62.5 0.1 select_reduce_fusion.1
  62.6 0.1 concatenate.3.refs_0_
  62.7 1.3 %collective-permute-done.refs_3_ = bf16[32,40,256]{2,1,0:T(8,128)(2,1)S(1)} collective-permute-done((bf16[32,40,256]{2,1,0:T(8,128)(2,1)S(1)}, bf16[32,40,256]{2,1,0:T(8,128)(2,1)S(1)}, u32[]{:S(2)}, u32[]{:S(2)}) %collective-permute-start) | collective-permute-done | bytes 655392 | tf_op jit(solution)/shard_map/ppermute | solution.py:294
  63.9 0.0 all-to-all-done.1
  63.9 5.5 %shard_map.46 = (bf16[4,40,1152]{2,1,0:T(8,128)(2,1)S(1)}, bf16[2560,128]{1,0:T(8,128)(2,1)S(1)}, bf16[2560,256]{1,0:T(8,128)(2,1)S(1)}) custom-call(s32[120]{0:T(128)S(1)} %concatenate.3.refs_0_, bf16[16,40,1024]{2,1,0:T(8,128)(2,1)S(1)} %bitcast.22, bf16[32,40,256]{2,1,0:T(8,128)(2,1)S(1)} %bitcast.26, ...), custom_call_target="tpu_custom_call" | custom-call | tf_op jit(solution)/shard_map/pallas_call | solution.py:168
  69.4 9.2 %shard_map.47 = (bf16[4,40,1152]{2,1,0:T(8,128)(2,1)S(1)}, bf16[4,40,1152]{2,1,0:T(8,128)(2,1)S(1)}) custom-call(s32[120]{0:T(128)S(1)} %concatenate.3.refs_0_, bf16[16,40,1024]{2,1,0:T(8,128)(2,1)S(1)} %bitcast.23, bf16[2560,128]{1,0:T(8,128)(2,1)S(1)} %get-tuple-element.11.refs_2_, bf16[2560,256]{1,0:T(8,128)(2,1)S(1)} %get-tuple-element.12.refs_3_, ...), custom_call_target="tpu_custom_call" | custom-call | tf_op jit(solution)/shard_map/pallas_call | solution.py:168
  78.6 1.9 %collective-permute-start.3 = (bf16[160,1152]{1,0:T(8,128)(2,1)S(1)}, bf16[160,1152]{1,0:T(8,128)(2,1)S(1)}, u32[]{:S(2)}, u32[]{:S(2)}) collective-permute-start(bf16[160,1152]{1,0:T(8,128)(2,1)S(1)} %bitcast.30), channel_id=1, source_target_pairs={{0,64},{64,128},{128,192},{192,0},{1,65},{65,129},{129,193},{193,1... | collective-permute-start | bytes 1105928 | tf_op jit(solution)/shard_map/ppermute | solution.py:300
  80.5 3.9 %collective-permute-start.2 = (bf16[160,1152]{1,0:T(8,128)(2,1)S(1)}, bf16[160,1152]{1,0:T(8,128)(2,1)S(1)}, u32[]{:S(2)}, u32[]{:S(2)}) collective-permute-start(bf16[160,1152]{1,0:T(8,128)(2,1)S(1)} %bitcast.29), channel_id=1, source_target_pairs={{0,192},{64,0},{128,64},{192,128},{1,193},{65,1},{129,65},{193,129... | collective-permute-start | bytes 1105928 | tf_op jit(solution)/shard_map/ppermute | solution.py:300
  84.5 3.5 %collective-permute-start.1 = (bf16[160,1152]{1,0:T(8,128)(2,1)S(1)}, bf16[160,1152]{1,0:T(8,128)(2,1)S(1)}, u32[]{:S(2)}, u32[]{:S(2)}) collective-permute-start(bf16[160,1152]{1,0:T(8,128)(2,1)S(1)} %bitcast.28), channel_id=1, source_target_pairs={{0,128},{64,192},{128,0},{192,64},{1,129},{65,193},{129,1},{193,65... | collective-permute-start | bytes 1105928 | tf_op jit(solution)/shard_map/ppermute | solution.py:300
  88.0 5.4 %shard_map.48 = bf16[4,40,1152]{2,1,0:T(8,128)(2,1)S(1)} custom-call(s32[120]{0:T(128)S(1)} %concatenate.3.refs_0_, bf16[16,40,1024]{2,1,0:T(8,128)(2,1)S(1)} %bitcast.24, bf16[2560,128]{1,0:T(8,128)(2,1)S(1)} %get-tuple-element.11.refs_2_, bf16[2560,256]{1,0:T(8,128)(2,1)S(1)} %get-tuple-element.12.refs_3_, s32[1,2560]{1,0:T(1,128)S(1)} %add.153.refs_4_), custom_call_target="tpu_custom_call" | custom-call | tf_op jit(solution)/shard_map/pallas_call | solution.py:168
  93.4 0.0 copy-start
  93.4 0.8 copy-done
  94.2 0.0 collective-permute-done.3.refs_2_
  94.2 0.0 copy-start.1
  94.2 0.6 collective-permute-done.2.refs_1_
  94.7 0.0 copy-start.2
  94.7 7.8 %collective-permute-done.1.refs_0_ = bf16[160,1152]{1,0:T(8,128)(2,1)S(1)} collective-permute-done((bf16[160,1152]{1,0:T(8,128)(2,1)S(1)}, bf16[160,1152]{1,0:T(8,128)(2,1)S(1)}, u32[]{:S(2)}, u32[]{:S(2)}) %collective-permute-start.1) | collective-permute-done | bytes 368672 | tf_op jit(solution)/shard_map/ppermute | solution.py:300
  102.5 0.0 copy-start.3
  102.5 0.7 copy-done.3
  103.3 0.0 copy-done.1
  103.3 0.0 copy-done.2
  103.3 2.7 %merge.1 = bf16[8,20,1024]{2,1,0:T(8,128)(2,1)} custom-call(bf16[160,1152]{1,0:T(8,128)(2,1)} %copy-done.3, bf16[160,1152]{1,0:T(8,128)(2,1)} %copy-done.2, bf16[160,1152]{1,0:T(8,128)(2,1)} %copy-done.1, bf16[160,1152]{1,0:T(8,128)(2,1)} %bitcast.27), custom_call_target="tpu_custom_call" | custom-call | tf_op jit(solution)/shard_map/merge/pallas_call | solution.py:222
  106.0 18.0 %all_to_all.15 = bf16[8,20,1024]{2,1,0:T(8,128)(2,1)S(1)} all-to-all(bf16[8,20,1024]{2,1,0:T(8,128)(2,1)} %merge.1), channel_id=1, replica_groups=mesh['zl'=2,'x'=4,'y'=8,'zh'=4,'core'=2] {'zl','zh'}, dimensions={0} | all-to-all | bytes 655360 | tf_op jit(solution)/shard_map/all_to_all | solution.py:283
  124.0 0.2 copy.18
  124.2 1.0 copy.21
  (11 shorter events, 0.1 us)
Async XLA Ops:
  0.0 12.2 %copy-start.4 = (s32[128]{0:T(128)S(1)}, s32[128]{0:T(128)}, u32[]{:S(2)}) copy-start(s32[128]{0:T(128)} %param.7) | copy-start | bytes 1540
  1.9 24.4 %all-to-all-start = ((bf16[8,20,1280]{2,1,0:T(8,128)(2,1)}), bf16[8,20,1280]{2,1,0:T(8,128)(2,1)S(1)}, u32[]{:S(2)}, u32[]{:S(2)}) async-start(bf16[8,20,1280]{2,1,0:T(8,128)(2,1)} %pack.1), calls=%async_computation | async-start | bytes 983040 | tf_op jit(solution)/shard_map/all_to_all | solution.py:283
  27.6 36.3 %all-to-all-start.1 = ((bf16[4,160,1024]{2,1,0:T(8,128)(2,1)}), bf16[4,160,1024]{2,1,0:T(8,128)(2,1)S(1)}, u32[]{:S(2)}, u32[]{:S(2)}) async-start(bf16[4,160,1024]{2,1,0:T(8,128)(2,1)} %broadcast_in_dim.54), calls=%async_computation.1 | async-start | bytes 2621440 | tf_op jit(solution)/shard_map/all_to_all | solution.py:283
  60.0 4.0 %collective-permute-start = (bf16[32,40,256]{2,1,0:T(8,128)(2,1)S(1)}, bf16[32,40,256]{2,1,0:T(8,128)(2,1)S(1)}, u32[]{:S(2)}, u32[]{:S(2)}) collective-permute-start(bf16[32,40,256]{2,1,0:T(8,128)(2,1)S(1)} %bitcast.25), channel_id=1, source_target_pairs={{0,1},{1,0},{2,3},{3,2},{4,5},{5,4},{6,7},{7,6},{8,9},{9,8},{10,11... | collective-permute-start | bytes 1966088 | tf_op jit(solution)/shard_map/ppermute | solution.py:294
  78.6 15.6 %collective-permute-start.3 = (bf16[160,1152]{1,0:T(8,128)(2,1)S(1)}, bf16[160,1152]{1,0:T(8,128)(2,1)S(1)}, u32[]{:S(2)}, u32[]{:S(2)}) collective-permute-start(bf16[160,1152]{1,0:T(8,128)(2,1)S(1)} %bitcast.30), channel_id=1, source_target_pairs={{0,64},{64,128},{128,192},{192,0},{1,65},{65,129},{129,193},{193,1... | collective-permute-start | bytes 1105928 | tf_op jit(solution)/shard_map/ppermute | solution.py:300
  80.5 14.2 %collective-permute-start.2 = (bf16[160,1152]{1,0:T(8,128)(2,1)S(1)}, bf16[160,1152]{1,0:T(8,128)(2,1)S(1)}, u32[]{:S(2)}, u32[]{:S(2)}) collective-permute-start(bf16[160,1152]{1,0:T(8,128)(2,1)S(1)} %bitcast.29), channel_id=1, source_target_pairs={{0,192},{64,0},{128,64},{192,128},{1,193},{65,1},{129,65},{193,129... | collective-permute-start | bytes 1105928 | tf_op jit(solution)/shard_map/ppermute | solution.py:300
  84.5 18.1 %collective-permute-start.1 = (bf16[160,1152]{1,0:T(8,128)(2,1)S(1)}, bf16[160,1152]{1,0:T(8,128)(2,1)S(1)}, u32[]{:S(2)}, u32[]{:S(2)}) collective-permute-start(bf16[160,1152]{1,0:T(8,128)(2,1)S(1)} %bitcast.28), channel_id=1, source_target_pairs={{0,128},{64,192},{128,0},{192,64},{1,129},{65,193},{129,1},{193,65... | collective-permute-start | bytes 1105928 | tf_op jit(solution)/shard_map/ppermute | solution.py:300
  93.4 0.8 copy-start
  94.2 9.1 %copy-start.1 = (bf16[160,1152]{1,0:T(8,128)(2,1)}, bf16[160,1152]{1,0:T(8,128)(2,1)S(1)}, u32[]{:S(2)}) copy-start(bf16[160,1152]{1,0:T(8,128)(2,1)S(1)} %collective-permute-done.3.refs_2_) | copy-start | bytes 1105924
  94.7 8.6 %copy-start.2 = (bf16[160,1152]{1,0:T(8,128)(2,1)}, bf16[160,1152]{1,0:T(8,128)(2,1)S(1)}, u32[]{:S(2)}) copy-start(bf16[160,1152]{1,0:T(8,128)(2,1)S(1)} %collective-permute-done.2.refs_1_) | copy-start | bytes 1105924
  102.5 0.7 copy-start.3
